TPU v7x, 32 devices: a whole 2x2x4 slice. The times are simulated.
32 devices in a mesh: scen: 2 (over y), site: 4 (over z), sub: 2 (over x), var: 2 (over core).
Axes of the slice: x: 2, y: 2, z: 4, core: 2. Of those that a mesh axis runs over, the one named last changes fastest.
Arguments:
- green_tensor: bfloat16 [8, 2, 16, 2, 2, 3, 32, 6, 128], P(('scen', 'site'), 'sub', None, 'var'), parts along dimension 0, may hold values from -0.078125 to 0.078125
- rupture_spectra: bfloat16 [2, 2, 512, 6, 1024], P(None, None, ('scen', 'var'), None, ('sub', 'site')), parts along dimension 2, may hold values from -6 to 6
- pair_site: int32 [8, 2, 16], P(('scen', 'site'), 'sub'), parts along dimension 0, may hold values from 0 to 3, as said below
- pair_block: int32 [8, 2, 16], P(('scen', 'site'), 'sub'), parts along dimension 0, may hold values from 0 to 3, as said below
- pair_count: int32 [8, 2, 16], P(('scen', 'site'), 'sub'), parts along dimension 0, may hold values from 0 to 128, as said below
- band_offset: int32 [2], P('scen'), parts along dimension 0, may hold values from 0 to 127
Outputs:
- site_spectra: float32 [2, 2, 3, 256, 1024], P(None, None, None, 'var', ('scen', 'site', 'sub')), parts along dimension 4
There are 2 independent parts, one for each index of `scen`. A program takes and returns all parts, laid end to end along the dimension named above; each array names one. Nothing has to cross between parts.
Inputs may be any that keep to these rules, and one draw needn't show every extreme that they name: On each device the live slots come first and are followed by unused slots; live slots name distinct pairs; unused slots have pair_count 0. No device has more than 12 live slots, and some device of every draw has exactly 12. `pair_site`: site block within the device's 4 site blocks. `pair_block`: subfault block within the device's group of 4 blocks.
All inputs are finite; a program needn't handle non-finite values.
Results may differ from a plain program's by a relative error of at most 0.0003.
Values may be sent and summed in bfloat16 or wider, within the bound.
No kernel may reach another device: no remote copies, remote signals or barrier semaphores. Data moves between devices by JAX's collectives and lax.ppermute only.
A program may use at most 64 MiB of HBM per device.

v0:
```python
import jax
import jax.numpy as jnp
from jax import lax
from jax.sharding import PartitionSpec as P

FREQS = 2
SITE_BLOCKS = 4


CORNER = 48.0


def pair_terms(
    totals,
    tiles,
    spectra,
    spec_start,
    total_start,
    site_table,
    block_table,
    count_table,
    slot_count,
):
    width = tiles.shape[1]
    block_sites = tiles.shape[4]
    variants = spectra.shape[2]
    columns = jnp.arange(128, dtype=jnp.int32)

    def add_pair(slot, totals):
        tensor_tile = lax.dynamic_index_in_dim(tiles, slot, 0, keepdims=False)
        spectrum = lax.dynamic_slice(
            spectra, (spec_start, 0, 0, 0, block_table[slot] * 128), (width, 2, variants, 6, 128)
        )
        keep_mask = (columns < count_table[slot]).astype(spectrum.dtype)
        spectrum = spectrum * keep_mask
        products = jnp.einsum(
            "fpcsmk,fqvmk->fpqcvs", tensor_tile, spectrum, preferred_element_type=jnp.float32
        )
        real_part = products[:, 0, 0] - products[:, 1, 1]
        imag_part = products[:, 0, 1] + products[:, 1, 0]
        contrib = jnp.stack([real_part, imag_part], axis=1)
        corner = (total_start, 0, 0, 0, site_table[slot] * block_sites)
        current = lax.dynamic_slice(totals, corner, contrib.shape)
        return lax.dynamic_update_slice(totals, current + contrib, corner)

    return lax.fori_loop(0, slot_count, add_pair, totals)


def shards(green_tensor, rupture_spectra, pair_site, pair_block, pair_count, band_offset):
    site_table = pair_site[0, 0]
    block_table = pair_block[0, 0]
    count_table = pair_count[0, 0]
    block_sites = green_tensor.shape[6]
    site_width = SITE_BLOCKS * block_sites
    spectra = lax.all_gather(rupture_spectra, "site", axis=4, tiled=True)
    slot_count = green_tensor.shape[2]
    local_vars = spectra.shape[2]
    empty = jnp.zeros((FREQS, 2, 3, local_vars, site_width), jnp.float32)
    piece_start = jnp.int32(0)
    totals = pair_terms(
        empty,
        lax.all_gather(green_tensor, "var", axis=3, tiled=True)[0, 0],
        spectra,
        piece_start,
        piece_start,
        site_table,
        block_table,
        count_table,
        slot_count,
    )
    partial_value = lax.psum_scatter(totals, "sub", scatter_dimension=4, tiled=True)
    freq_index = (band_offset[0] + jnp.arange(FREQS, dtype=jnp.int32)).astype(jnp.float32)
    brune = 1.0 / (1.0 + (freq_index / CORNER) ** 2)
    return partial_value * brune[:, None, None, None, None]


def solution(mesh):
    return jax.shard_map(
        shards,
        mesh=mesh,
        in_specs=(
            P(("scen", "site"), "sub", None, "var", None, None, None, None, None),
            P(None, None, ("scen", "var"), None, ("sub", "site")),
            P(("scen", "site"), "sub", None),
            P(("scen", "site"), "sub", None),
            P(("scen", "site"), "sub", None),
            P("scen"),
        ),
        out_specs=P(None, None, None, "var", ("scen", "site", "sub")),
        check_vma=False,
    )
```

profile of v0, /device:TPU:0, one launch (start us, length us, event | category | flops | bytes accessed | tf_op | source)
XLA Modules:
  0.0 213.4 jit_solution(682382720835881932)
XLA Ops:
  6.5 0.7 all-gather.3.cloned.1.call-update
  7.3 0.7 all-gather.5.cloned.1.call-update
  8.1 67.0 %all-gather.3.cloned.1.call-done = bf16[2,2,128,6,512]{4,2,3,1,0:T(8,128)(2,1)} async-done(((bf16[2,2,128,6,128]{4,2,3,1,0:T(8,128)(2,1)}), bf16[2,2,128,6,512]{4,2,3,1,0:T(8,128)(2,1)}) %all-gather.3.cloned.1.call-update) | async-done | bytes 3145744 | tf_op jit(solution)/shard_map/all_gather | solution.py:55
  75.1 21.5 %all-gather.5.cloned.1.call-done = bf16[1,1,16,2,2,3,32,6,128]{8,6,7,5,4,3,2,1,0:T(8,128)(2,1)} async-done(((bf16[1,1,16,1,2,3,32,6,128]{8,6,7,5,4,3,2,1,0:T(8,128)(2,1)}), bf16[1,1,16,2,2,3,32,6,128]{8,6,7,5,4,3,2,1,0:T(8,128)(2,1)}) %all-gather.5.cloned.1.call-update) | async-done | bytes 9437200 | tf_op jit(solution)/shard_map/all_gather | solution.py:62
  96.7 88.6 %while.14 = (s32[]{:T(128)}, f32[2,2,3,128,128]{3,4,2,1,0:T(8,128)S(1)}, s32[16]{0:T(128)S(1)}, s32[16]{0:T(128)S(1)}, bf16[2,2,128,6,512]{4,2,3,1,0:T(8,128)(2,...) while((s32[]{:T(128)}, ...), condition=%wide.region_1.2_spmd.clone, body=%wide.region_0.1_spmd.clone.sunk | while | flops 152715536 | bytes 3343629 | solution.py:46
  98.5 0.6 compare_convert_fusion.2
  99.2 1.7 convolution_bitcast_fusion.2
  101.0 0.6 dynamic_slice.67
  103.5 0.6 dynamic_slice.69
  104.1 0.6 compare_convert_fusion.2
  104.7 1.7 convolution_bitcast_fusion.2
  106.5 0.6 dynamic_slice.67
  109.6 0.6 compare_convert_fusion.2
  110.2 1.7 convolution_bitcast_fusion.2
  112.0 0.6 dynamic_slice.67
  114.6 0.6 dynamic_slice.69
  115.2 0.6 compare_convert_fusion.2
  115.8 1.7 convolution_bitcast_fusion.2
  117.6 0.6 dynamic_slice.67
  120.1 0.6 dynamic_slice.69
  120.7 0.6 compare_convert_fusion.2
  121.3 1.7 convolution_bitcast_fusion.2
  123.1 0.6 dynamic_slice.67
  126.2 0.6 compare_convert_fusion.2
  126.9 1.7 convolution_bitcast_fusion.2
  128.7 0.6 dynamic_slice.67
  131.2 0.6 dynamic_slice.69
  131.8 0.6 compare_convert_fusion.2
  132.4 1.7 convolution_bitcast_fusion.2
  134.2 0.6 dynamic_slice.67
  136.7 0.6 dynamic_slice.69
  137.3 0.6 compare_convert_fusion.2
  137.9 1.7 convolution_bitcast_fusion.2
  139.7 0.6 dynamic_slice.67
  142.3 0.6 dynamic_slice.69
  142.9 0.6 compare_convert_fusion.2
  143.5 1.7 convolution_bitcast_fusion.2
  145.3 0.6 dynamic_slice.67
  148.4 0.6 compare_convert_fusion.2
  149.0 1.7 convolution_bitcast_fusion.2
  150.8 0.6 dynamic_slice.67
  153.3 0.6 dynamic_slice.69
  153.9 0.6 compare_convert_fusion.2
  154.6 1.7 convolution_bitcast_fusion.2
  156.4 0.6 dynamic_slice.67
  158.9 0.6 dynamic_slice.69
  159.5 0.6 compare_convert_fusion.2
  160.1 1.7 convolution_bitcast_fusion.2
  161.9 0.6 dynamic_slice.67
  164.4 0.6 dynamic_slice.69
  165.0 0.6 compare_convert_fusion.2
  165.6 1.7 convolution_bitcast_fusion.2
  167.4 0.6 dynamic_slice.67
  169.9 0.6 dynamic_slice.69
  170.5 0.6 compare_convert_fusion.2
  171.2 1.7 convolution_bitcast_fusion.2
  173.0 0.6 dynamic_slice.67
  176.1 0.6 compare_convert_fusion.2
  176.7 1.7 convolution_bitcast_fusion.2
  181.6 0.6 compare_convert_fusion.2
  182.2 1.7 convolution_bitcast_fusion.2
  185.4 0.9 copy-done
  186.9 18.1 %reduce-scatter.2.cloned.1.call-done = f32[2,2,3,128,64]{3,4,2,1,0:T(8,128)} async-done(((f32[2,2,3,128,128]{3,4,2,1,0:T(8,128)}), f32[2,2,3,128,64]{3,4,2,1,0:T(8,128)}) %reduce-scatter.2.cloned.1.call-update) | async-done | bytes 393232 | tf_op jit(solution)/shard_map/reduce_scatter | solution.py:71
  205.0 1.8 broadcast_multiply_fusion
  (101 shorter events, 15.8 us)
Async XLA Ops:
  6.5 90.2 %copy-start.1 = (s32[1,1,16]{2,1,0:T(1,128)S(1)}, s32[1,1,16]{2,1,0:T(1,128)}, u32[]{:S(2)}) copy-start(s32[1,1,16]{2,1,0:T(1,128)} %param.10) | copy-start | bytes 196
  6.5 90.2 %copy-start.2 = (s32[1,1,16]{2,1,0:T(1,128)S(1)}, s32[1,1,16]{2,1,0:T(1,128)}, u32[]{:S(2)}) copy-start(s32[1,1,16]{2,1,0:T(1,128)} %param.11) | copy-start | bytes 196
  6.5 90.2 %copy-start.3 = (s32[1,1,16]{2,1,0:T(1,128)S(1)}, s32[1,1,16]{2,1,0:T(1,128)}, u32[]{:S(2)}) copy-start(s32[1,1,16]{2,1,0:T(1,128)} %param.12) | copy-start | bytes 196
  6.5 68.5 %all-gather.3.cloned.1.call-start = ((), (), s32[]{:S(2)}) async-start(), calls=%async_computation.1 | async-start | bytes 3932160 | tf_op jit(solution)/shard_map/all_gather | solution.py:55
  7.3 89.4 %all-gather.5.cloned.1.call-start = ((), (), s32[]{:S(2)}) async-start(), calls=%async_computation.2 | async-start | bytes 14155776 | tf_op jit(solution)/shard_map/all_gather | solution.py:62
  8.0 197.0 %reduce-scatter.2.cloned.1.call-start = ((), (), s32[]{:S(2)}) async-start(), calls=%async_computation.3 | async-start | bytes 1179648 | tf_op jit(solution)/shard_map/reduce_scatter | solution.py:71
  185.3 0.9 copy-start
Sparse Core Ops, SparseCore 0:
  8.9 66.1 all-gather.2
  76.6 19.9 all-gather.4
  186.4 18.5 reduce-scatter.1
where the time goes:
time: 214 us; the launch traced here: 213 us
  waiting for transfers between devices  108 us (50%)
  local copies, waits for them, and re-layouts  29.8 us (14%)
  matrix products  27.9 us (13%)
  loops' own time  20.9 us (10%)
  between operations  13.8 us (6%)
  other arithmetic  12.8 us (6%)
    all_gather x1, waiting for transfers between devices, shards(): spectra = lax.all_gather(rupture_spectra, 'site', axis=4, tiled=True)  67 us
    dot_general x16, matrix products, add_pair(): jnp.einsum('fpcsmk,fqvmk->fpqcvs', tensor_tile, spectrum, preferred_eleme...  27.9 us
    all_gather x1, waiting for transfers between devices, shards(): lax.all_gather(green_tensor, 'var', axis=3, tiled=True)[0, 0]  21.5 us
    another operation x1, loops' own time, pair_terms(): return lax.fori_loop(0, slot_count, add_pair, totals)  20.9 us
    reduce_scatter x1, waiting for transfers between devices, shards(): lax.psum_scatter(totals, 'sub', scatter_dimension=4, tiled=True)  18.1 us
    convert_element_type x16, other arithmetic, add_pair(): keep_mask = (columns < count_table[slot]).astype(spectrum.dtype)  9.88 us
    dynamic_slice x16, local copies, waits for them, and re-layouts, add_pair(): corner = (total_start, 0, 0, 0, site_table[slot] * block_sites)  9.52 us
    dynamic_slice x16, local copies, waits for them, and re-layouts, add_pair(): keep_mask = (columns < count_table[slot]).astype(spectrum.dtype)  9.52 us
  transfers between devices with their start and end apart: 3, of which 3 were waited for; matrix products, arithmetic and copies ran while one was open for 0% of the time, Pallas kernels for 0%

commit v1 on v0

v1 whole, which is shorter than its diff:
```python
import functools

import jax
import jax.numpy as jnp
from jax import lax
from jax.experimental import pallas as pl
from jax.experimental.pallas import tpu as pltpu
from jax.sharding import PartitionSpec as P

FREQS = 2
SITE_BLOCKS = 4
SUB_BLOCKS = 4
CORNER = 48.0


def place_of(block, z):
    flip = z >= 2
    block = jnp.where(flip, 3 - block, block)
    z = jnp.where(flip, 3 - z, z)
    return jnp.where(block < 2, block ^ z, block)


def pair_kernel(lo, hi, last, line, freq, *refs):
    refs = list(refs)
    ids, site_t, block_t, count_t = refs[:4]
    refs = refs[4:]
    g_own, g_other = refs[:2]
    refs = refs[2:]
    n = hi - lo
    sources = []
    for place in range(lo, hi):
        if line and place >= 2:
            sources.append(refs[:2])
            refs = refs[2:]
        else:
            sources.append(refs[:1])
            refs = refs[1:]
    acc_in = None
    if lo > 0:
        acc_in = refs.pop(0)
    if last:
        keep, send = refs[:2]
        refs = refs[2:]
    else:
        acc_out = refs.pop(0)
    gbuf, mbuf, counts, gsem, msem = refs
    z, j, v = ids[0], ids[1], ids[2]
    slots = g_own.shape[0]
    middle = jnp.logical_and(z > 0, z < 3)

    for q in range(n):
        srcs = sources[q]
        if len(srcs) == 1:
            pltpu.make_async_copy(srcs[0], mbuf.at[q], msem.at[q]).start()
        else:

            @pl.when(middle)
            def _():
                pltpu.make_async_copy(srcs[0], mbuf.at[q], msem.at[q]).start()

            @pl.when(jnp.logical_not(middle))
            def _():
                pltpu.make_async_copy(srcs[1], mbuf.at[q], msem.at[q]).start()

    for q in range(n):
        for s in range(SITE_BLOCKS):
            counts[q, s] = 0

    def slot_at(p):
        block = block_t[0, 0, p]
        place = place_of(block, z) if line else block
        live = jnp.logical_and(
            count_t[0, 0, p] > 0, jnp.logical_and(place >= lo, place < hi)
        )
        half = SITE_BLOCKS // 2
        s = site_t[0, 0, p]
        row = (s // half ^ j) * half + s % half
        return live, place - lo, row

    def load(p, _):
        live, q, row = slot_at(p)

        @pl.when(live)
        def _():
            counts[q, row] = count_t[0, 0, p]

            @pl.when(v == freq)
            def _():
                pltpu.make_async_copy(
                    g_own.at[p], gbuf.at[q, :, :, :, row], gsem
                ).start()

            @pl.when(v != freq)
            def _():
                pltpu.make_async_copy(
                    g_other.at[p], gbuf.at[q, :, :, :, row], gsem
                ).start()

        return 0

    lax.fori_loop(0, slots, load, 0)

    def drain(p, _):
        live, q, row = slot_at(p)

        @pl.when(live)
        def _():
            pltpu.make_async_copy(g_own.at[p], gbuf.at[q, :, :, :, row], gsem).wait()

        return 0

    lax.fori_loop(0, slots, drain, 0)
    for q in range(n):
        pltpu.make_async_copy(sources[q][0], mbuf.at[q], msem.at[q]).wait()

    moments = gbuf.shape[3]
    block_sites = gbuf.shape[5]
    variants = mbuf.shape[3]
    sites = SITE_BLOCKS * block_sites
    for c in range(3):
        total = None
        for q in range(n):
            lane = lax.broadcasted_iota(jnp.int32, (block_sites, 128), 1)
            pieces = []
            for m in range(moments):
                rows = []
                for r in range(2):
                    for s in range(SITE_BLOCKS):
                        rows.append(
                            jnp.where(
                                lane < counts[q, s],
                                gbuf[q, r, c, m, s],
                                jnp.zeros((), gbuf.dtype),
                            )
                        )
                pieces.append(jnp.concatenate(rows, axis=0))
            lhs = jnp.concatenate(pieces, axis=1)
            rhs = jnp.concatenate(
                [mbuf[q, :, m].reshape(2 * variants, 128) for m in range(moments)],
                axis=1,
            )
            prod = lax.dot_general(
                lhs, rhs, (((1,), (1,)), ((), ())), preferred_element_type=jnp.float32
            )
            total = prod if total is None else total + prod
        real = total[:sites, :variants] - total[sites:, variants:]
        imag = total[:sites, variants:] + total[sites:, :variants]
        for r, value in enumerate((real, imag)):
            if acc_in is not None:
                value = value + acc_in[r, c]
            if last:
                keep[r, c] = value[: sites // 2]
                send[r, c] = value[sites // 2 :]
            else:
                acc_out[r, c] = value


def pair_sums(lo, hi, last, line, freq, ids, tables, tensors, sources, acc=None):
    slots, _, comps, moments, block_sites, columns = tensors[0].shape
    variants = sources[0].shape[2]
    sites = SITE_BLOCKS * block_sites
    n = hi - lo
    smem = pl.BlockSpec(memory_space=pltpu.SMEM)
    hbm = pl.BlockSpec(memory_space=pl.ANY)
    vmem = pl.BlockSpec(memory_space=pltpu.VMEM)
    operands = [ids, *tables, *tensors, *sources]
    in_specs = [smem] * 4 + [hbm] * (2 + len(sources))
    if acc is not None:
        operands.append(acc)
        in_specs.append(vmem)
    if last:
        shape = jax.ShapeDtypeStruct((2, comps, sites // 2, variants), jnp.float32)
        out_shape = (shape, shape)
        out_specs = (vmem, vmem)
    else:
        out_shape = jax.ShapeDtypeStruct((2, comps, sites, variants), jnp.float32)
        out_specs = vmem
    flops = n * 2 * (2 * comps * sites) * (2 * variants) * moments * columns
    return pl.pallas_call(
        functools.partial(pair_kernel, lo, hi, last, line, freq),
        out_shape=out_shape,
        in_specs=in_specs,
        out_specs=out_specs,
        scratch_shapes=[
            pltpu.VMEM(
                (n, 2, comps, moments, SITE_BLOCKS, block_sites, columns),
                tensors[0].dtype,
            ),
            pltpu.VMEM((n, 2, moments, variants, columns), sources[0].dtype),
            pltpu.SMEM((n, SITE_BLOCKS), jnp.int32),
            pltpu.SemaphoreType.DMA,
            pltpu.SemaphoreType.DMA((n,)),
        ],
        compiler_params=pltpu.CompilerParams(vmem_limit_bytes=24 << 20),
        cost_estimate=pl.CostEstimate(
            flops=flops, bytes_accessed=n * 1_600_000, transcendentals=0
        ),
    )(*operands)


def line_steps(own):
    send = functools.partial(lax.ppermute, axis_name="site")
    pairs = send(own, perm=[(0, 1), (1, 0), (2, 3), (3, 2)])
    inner = send(own, perm=[(1, 2), (2, 1)])
    outer = send(inner, perm=[(1, 0), (2, 3)])
    inner_far = send(pairs, perm=[(1, 2), (2, 1)])
    outer_far = send(inner_far, perm=[(1, 0), (2, 3)])
    return pairs, inner, outer, inner_far, outer_far


def shards(n_site, n_sub, tensor, spectra, pair_site, pair_block, pair_count, offset):
    spectra = spectra.transpose(0, 1, 3, 2, 4)
    tensor = tensor[0, 0, :, 0].transpose(0, 1, 2, 4, 3, 5)
    tables = (pair_site, pair_block, pair_count)
    line = n_site == SUB_BLOCKS
    swap = n_sub == 2
    half = lax.axis_index("sub") if swap else 0
    ids = jnp.stack([lax.axis_index("site"), half, lax.axis_index("var")])
    ids = ids.astype(jnp.int32)
    kept, sent = [], []
    if line:
        steps = [line_steps(spectra[f]) for f in range(FREQS)]
    else:
        whole = lax.all_gather(spectra, "site", axis=4, tiled=True)
    other = lax.ppermute(tensor, "var", [(0, 1), (1, 0)])
    sums = functools.partial(
        pair_sums, line=line, ids=ids, tables=tables, tensors=(tensor, other)
    )
    for f in range(FREQS):
        if line:
            pairs, inner, outer, inner_far, outer_far = steps[f]
            acc = sums(0, 3, False, freq=f, sources=(spectra[f], pairs, inner, outer))
            keep, send = sums(
                3, 4, True, freq=f, sources=(inner_far, outer_far), acc=acc
            )
        else:
            parts = [whole[f, ..., 128 * b : 128 * (b + 1)] for b in range(SUB_BLOCKS)]
            keep, send = sums(0, 4, True, freq=f, sources=parts)
        kept.append(keep)
        sent.append(send)
    if swap:
        got = [lax.ppermute(send, "sub", [(0, 1), (1, 0)]) for send in sent]
        sums = [keep + more for keep, more in zip(kept, got)]
    else:
        sums = [
            lax.psum_scatter(
                jnp.concatenate(both, axis=2), "sub", scatter_dimension=2, tiled=True
            )
            for both in zip(kept, sent)
        ]
    freq_index = (offset[0] + jnp.arange(FREQS, dtype=jnp.int32)).astype(jnp.float32)
    brune = 1.0 / (1.0 + (freq_index / CORNER) ** 2)
    result = jnp.stack([sums[f] * brune[f] for f in range(FREQS)])
    return result.transpose(0, 1, 2, 4, 3)


def solution(mesh):
    return jax.shard_map(
        functools.partial(shards, mesh.shape["site"], mesh.shape["sub"]),
        mesh=mesh,
        in_specs=(
            P(("scen", "site"), "sub", None, "var", None, None, None, None, None),
            P(None, None, ("scen", "var"), None, ("sub", "site")),
            P(("scen", "site"), "sub", None),
            P(("scen", "site"), "sub", None),
            P(("scen", "site"), "sub", None),
            P("scen"),
        ),
        out_specs=P(None, None, None, "var", ("scen", "site", "sub")),
        check_vma=False,
    )
```

time: 214 us -> 73 us (0.34)
  waiting for transfers between devices: 108 us -> 37.9 us
  matrix products: 27.9 us -> 0 us
  local copies, waits for them, and re-layouts: 29.8 us -> 6.02 us
  loops' own time: 20.9 us -> 0 us
  starting transfers between devices: 0.08 us -> 14 us
  between operations: 13.8 us -> 0.81 us
  Pallas kernels: 0 us -> 11.7 us
  other arithmetic: 12.8 us -> 2.11 us
    all_gather x2 -> x0, waiting for transfers between devices: 88.6 us -> none  [the longest x1 67 us: shards(): spectra = lax.all_gather(rupture_spectra, 'site', axis=4, tiled=True)]
    ppermute x0 -> x13, waiting for transfers between devices: none -> 37.9 us  [the longest x2 16.1 us: line_steps(): pairs = send(own, perm=[(0, 1), (1, 0), (2, 3), (3, 2)])]
    dynamic_slice x64 -> x0, local copies, waits for them, and re-layouts: 28.9 us -> none  [the longest x16 9.52 us: add_pair(): corner = (total_start, 0, 0, 0, site_table[slot] * block_sites)]
    dot_general x16 -> x0, matrix products: 27.9 us -> none  [add_pair(): jnp.einsum('fpcsmk,fqvmk->fpqcvs', tensor_tile, spectrum, preferred_eleme...]
    another operation x1 -> x0, loops' own time: 20.9 us -> none  [pair_terms(): return lax.fori_loop(0, slot_count, add_pair, totals)]
    reduce_scatter x1 -> x0, waiting for transfers between devices: 18.1 us -> none  [shards(): lax.psum_scatter(totals, 'sub', scatter_dimension=4, tiled=True)]
    ppermute x0 -> x13, starting transfers between devices: none -> 14 us  [the longest x2 2.94 us: shards(): got = [lax.ppermute(send, 'sub', [(0, 1), (1, 0)]) for send in sent]]
    pallas_call x0 -> x4, Pallas kernels: none -> 11.7 us  [pair_sums(): pl.pallas_call(functools.partial(pair_kernel, lo, hi, last, line, freq),...]
  transfers between devices with their start and end apart: 3 -> 13, of which waited for: 3 -> 7; matrix products, arithmetic and copies ran while one was open for 0% -> 3% of each run, Pallas kernels for 0% -> 16%
where the time goes in v1:
time: 73 us; the launch traced here: 72.6 us
  waiting for transfers between devices  37.9 us (52%)
  starting transfers between devices  14 us (19%)
  Pallas kernels  11.7 us (16%)
  local copies, waits for them, and re-layouts  6.02 us (8%)
  other arithmetic  2.11 us (3%)
  between operations  0.81 us (1%)
    ppermute x2, waiting for transfers between devices, line_steps(): pairs = send(own, perm=[(0, 1), (1, 0), (2, 3), (3, 2)])  16.1 us
    ppermute x2, waiting for transfers between devices, line_steps(): outer = send(inner, perm=[(1, 0), (2, 3)])  14.1 us
    pallas_call x4, Pallas kernels, pair_sums(): pl.pallas_call(functools.partial(pair_kernel, lo, hi, last, line, freq),...  11.7 us
    unnamed x8, local copies, waits for them, and re-layouts  4.3 us
    ppermute x2, waiting for transfers between devices, line_steps(): outer_far = send(inner_far, perm=[(1, 0), (2, 3)])  4.13 us
    ppermute x2, waiting for transfers between devices, shards(): got = [lax.ppermute(send, 'sub', [(0, 1), (1, 0)]) for send in sent]  3.67 us
    ppermute x2, starting transfers between devices, shards(): got = [lax.ppermute(send, 'sub', [(0, 1), (1, 0)]) for send in sent]  2.94 us
    ppermute x2, starting transfers between devices, line_steps(): pairs = send(own, perm=[(0, 1), (1, 0), (2, 3), (3, 2)])  2.72 us
  transfers between devices with their start and end apart: 13, of which 7 were waited for; matrix products, arithmetic and copies ran while one was open for 3% of the time, Pallas kernels for 16%

profile of v1, /device:TPU:0, one launch (start us, length us, event | category | flops | bytes accessed | tf_op | source)
XLA Modules:
  0.0 72.6 jit_solution(12548354348133764269)
XLA Ops:
  0.0 0.5 collective-permute-start
  0.5 1.2 %slice_bitcast_fusion.1 = (bf16[2,6,128,128]{3,2,1,0:T(8,128)(2,1)S(1)}, bf16[2,6,128,128]{3,2,1,0:T(8,128)(2,1)S(1)}) fusion(bf16[2,2,6,128,128]{4,3,2,1,0:T(8,128)(2,1)} %bitcast.26), kind=kLoop, calls=%fused_computation.1 | loop fusion | bytes 1572864 | tf_op jit(solution)/shard_map/squeeze | solution.py:222
  1.6 2.6 %collective-permute-start.1 = (bf16[2,6,128,128]{3,2,1,0:T(8,128)(2,1)S(1)}, bf16[2,6,128,128]{3,2,1,0:T(8,128)(2,1)S(1)}, u32[]{:S(2)}, u32[]{:S(2)}) collective-permute-start(bf16[2,6,128,128]{3,2,1,0:T(8,128)(2,1)S(1)} %get-tuple-element.13.refs_6_), channel_id=1, source_target_pairs={{0,4},{4,0},{8,12},{12,8},{1,5},{5,1},{9,13},{13,9},{2,6},{6,2},{1... | collective-permute-start | bytes 1179656 | tf_op jit(solution)/shard_map/ppermute | solution.py:203
  4.3 0.1 collective-permute-start.7
  4.3 0.7 collective-permute-start.4
  5.0 9.2 %collective-permute-done.1.refs_7_ = bf16[2,6,128,128]{3,2,1,0:T(8,128)(2,1)S(1)} collective-permute-done((bf16[2,6,128,128]{3,2,1,0:T(8,128)(2,1)S(1)}, bf16[2,6,128,128]{3,2,1,0:T(8,128)(2,1)S(1)}, u32[]{:S(2)}, u32[]{:S(2)}) %collective-permute-start.1) | collective-permute-done | bytes 393248 | tf_op jit(solution)/shard_map/ppermute | solution.py:203
  14.2 0.7 collective-permute-start.2
  14.9 0.7 collective-permute-start.10
  15.6 6.9 %collective-permute-done.7.refs_7_ = bf16[2,6,128,128]{3,2,1,0:T(8,128)(2,1)S(1)} collective-permute-done((bf16[2,6,128,128]{3,2,1,0:T(8,128)(2,1)S(1)}, bf16[2,6,128,128]{3,2,1,0:T(8,128)(2,1)S(1)}, u32[]{:S(2)}, u32[]{:S(2)}) %collective-permute-start.7) | collective-permute-done | bytes 393248 | tf_op jit(solution)/shard_map/ppermute | solution.py:203
  22.5 0.7 collective-permute-start.8
  23.2 0.0 collective-permute-done.4.refs_8_
  23.2 1.3 %collective-permute-start.5 = (bf16[2,6,128,128]{3,2,1,0:T(8,128)(2,1)S(1)}, bf16[2,6,128,128]{3,2,1,0:T(8,128)(2,1)}, u32[]{:S(2)}, u32[]{:S(2)}) collective-permute-start(bf16[2,6,128,128]{3,2,1,0:T(8,128)(2,1)S(1)} %collective-permute-done.4.refs_8_), channel_id=1, source_target_pairs={{4,0},{8,12},{5,1},{9,13},{6,2},{10,14},{7,3},{11,15},{20,16},{24,... | collective-permute-start | bytes 1179656 | tf_op jit(solution)/shard_map/ppermute | solution.py:205
  24.5 0.0 collective-permute-done.2.refs_6_
  24.5 1.3 %collective-permute-start.3 = (bf16[2,6,128,128]{3,2,1,0:T(8,128)(2,1)S(1)}, bf16[2,6,128,128]{3,2,1,0:T(8,128)(2,1)}, u32[]{:S(2)}, u32[]{:S(2)}) collective-permute-start(bf16[2,6,128,128]{3,2,1,0:T(8,128)(2,1)S(1)} %collective-permute-done.2.refs_6_), channel_id=1, source_target_pairs={{4,0},{8,12},{5,1},{9,13},{6,2},{10,14},{7,3},{11,15},{20,16},{24,... | collective-permute-start | bytes 1179656 | tf_op jit(solution)/shard_map/ppermute | solution.py:207
  26.4 0.0 collective-permute-done.10.refs_8_
  26.4 1.3 %collective-permute-start.11 = (bf16[2,6,128,128]{3,2,1,0:T(8,128)(2,1)S(1)}, bf16[2,6,128,128]{3,2,1,0:T(8,128)(2,1)S(1)}, u32[]{:S(2)}, u32[]{:S(2)}) collective-permute-start(bf16[2,6,128,128]{3,2,1,0:T(8,128)(2,1)S(1)} %collective-permute-done.10.refs_8_), channel_id=1, source_target_pairs={{4,0},{8,12},{5,1},{9,13},{6,2},{10,14},{7,3},{11,15},{20,16},{24,... | collective-permute-start | bytes 1179656 | tf_op jit(solution)/shard_map/ppermute | solution.py:205
  27.8 0.0 collective-permute-done.8.refs_6_
  27.8 1.3 %collective-permute-start.9 = (bf16[2,6,128,128]{3,2,1,0:T(8,128)(2,1)S(1)}, bf16[2,6,128,128]{3,2,1,0:T(8,128)(2,1)S(1)}, u32[]{:S(2)}, u32[]{:S(2)}) collective-permute-start(bf16[2,6,128,128]{3,2,1,0:T(8,128)(2,1)S(1)} %collective-permute-done.8.refs_6_), channel_id=1, source_target_pairs={{4,0},{8,12},{5,1},{9,13},{6,2},{10,14},{7,3},{11,15},{20,16},{24,... | collective-permute-start | bytes 1179656 | tf_op jit(solution)/shard_map/ppermute | solution.py:207
  29.1 0.1 pad_add_fusion.refs_0_
  29.1 9.9 %collective-permute-done.5.refs_9_ = bf16[2,6,128,128]{3,2,1,0:T(8,128)(2,1)} collective-permute-done((bf16[2,6,128,128]{3,2,1,0:T(8,128)(2,1)S(1)}, bf16[2,6,128,128]{3,2,1,0:T(8,128)(2,1)}, u32[]{:S(2)}, u32[]{:S(2)}) %collective-permute-start.5) | collective-permute-done | bytes 393248 | tf_op jit(solution)/shard_map/ppermute | solution.py:205
  39.1 0.0 collective-permute-done.refs_5_
  39.1 0.0 copy-start
  39.1 2.3 %copy-done = bf16[1,1,16,1,2,3,32,6,128]{8,6,7,5,4,3,2,1,0:T(8,128)(2,1)S(1)} copy-done((bf16[1,1,16,1,2,3,32,6,128]{8,6,7,5,4,3,2,1,0:T(8,128)(2,1)S(1)}, bf16[1,1,16,1,2,3,32,6,128]{8,6,7,5,4,3,2,1,0:T(8,128)(2,1)}, u32[]{:S(2)}) %copy-start) | copy-done | bytes 4718616
  41.4 0.0 copy-start.1
  41.4 0.7 copy-done.1
  42.1 0.0 copy-start.2
  42.1 0.7 copy-done.2
  42.7 0.0 copy-start.3
  42.7 0.7 copy-done.3
  43.4 3.1 %shard_map.64.refs_8_ = f32[2,3,128,128]{3,2,1,0:T(8,128)S(1)} custom-call(s32[3]{0:T(128)S(1)} %pad_add_fusion.refs_0_, s32[1,1,16]{2,1,0:T(1,128)S(1)} %copy-done.1, s32[1,1,16]{2,1,0:T(1,128)S(1)} %copy-done.2, s32[1,1,16]{2,1,0:T(1,128)S(1)} %copy-done.3, bf16[16,2,3,6,32,128]{5,4,3,2,1,0:T(8,128)(2,1)S(1)} %bitcast.22, ...), custom_call_target="tpu_custom_call" | custom-call | flops 905969664 | bytes 4800000 | tf_op jit(solution)/shard_map/pallas_call | solution.py:179
  46.5 1.0 %collective-permute-done.3.refs_7_ = bf16[2,6,128,128]{3,2,1,0:T(8,128)(2,1)} collective-permute-done((bf16[2,6,128,128]{3,2,1,0:T(8,128)(2,1)S(1)}, bf16[2,6,128,128]{3,2,1,0:T(8,128)(2,1)}, u32[]{:S(2)}, u32[]{:S(2)}) %collective-permute-start.3) | collective-permute-done | bytes 393248 | tf_op jit(solution)/shard_map/ppermute | solution.py:207
  47.5 2.1 %shard_map.65 = (f32[2,3,64,128]{3,2,1,0:T(8,128)S(1)}, f32[2,3,64,128]{3,2,1,0:T(8,128)S(1)}) custom-call(s32[3]{0:T(128)S(1)} %pad_add_fusion.refs_0_, s32[1,1,16]{2,1,0:T(1,128)S(1)} %copy-done.1, s32[1,1,16]{2,1,0:T(1,128)S(1)} %copy-done.2, s32[1,1,16]{2,1,0:T(1,128)S(1)} %copy-done.3, bf16[16,2,3,6,32,128]{5,4,3,2,1,0:T(8,128)(2,1)S(1)} %bitcast.23, ...), custom_call_target="tpu_custom_call" | custom-call | flops 301989888 | bytes 1600000 | tf_op jit(solution)/shard_map/pallas_call | solution.py:179
  49.6 1.6 %collective-permute-start.6 = (f32[2,3,64,128]{3,2,1,0:T(8,128)S(1)}, f32[2,3,64,128]{3,2,1,0:T(8,128)S(1)}, u32[]{:S(2)}, u32[]{:S(2)}) collective-permute-start(f32[2,3,64,128]{3,2,1,0:T(8,128)S(1)} %get-tuple-element.10), channel_id=1, source_target_pairs={{0,2},{2,0},{1,3},{3,1},{4,6},{6,4},{5,7},{7,5},{8,10},{10,8},{9,1... | collective-permute-start | bytes 589832 | tf_op jit(solution)/shard_map/ppermute | solution.py:242
  51.2 0.6 fusion
  51.7 4.1 %collective-permute-done.11.refs_9_ = bf16[2,6,128,128]{3,2,1,0:T(8,128)(2,1)S(1)} collective-permute-done((bf16[2,6,128,128]{3,2,1,0:T(8,128)(2,1)S(1)}, bf16[2,6,128,128]{3,2,1,0:T(8,128)(2,1)S(1)}, u32[]{:S(2)}, u32[]{:S(2)}) %collective-permute-start.11) | collective-permute-done | bytes 393248 | tf_op jit(solution)/shard_map/ppermute | solution.py:205
  55.8 4.0 %shard_map.66.refs_8_ = f32[2,3,128,128]{3,2,1,0:T(8,128)S(1)} custom-call(s32[3]{0:T(128)S(1)} %pad_add_fusion.refs_0_, s32[1,1,16]{2,1,0:T(1,128)S(1)} %copy-done.1, s32[1,1,16]{2,1,0:T(1,128)S(1)} %copy-done.2, s32[1,1,16]{2,1,0:T(1,128)S(1)} %copy-done.3, bf16[16,2,3,6,32,128]{5,4,3,2,1,0:T(8,128)(2,1)S(1)} %bitcast.24, ...), custom_call_target="tpu_custom_call" | custom-call | flops 905969664 | bytes 4800000 | tf_op jit(solution)/shard_map/pallas_call | solution.py:179
  59.9 3.1 %collective-permute-done.9.refs_7_ = bf16[2,6,128,128]{3,2,1,0:T(8,128)(2,1)S(1)} collective-permute-done((bf16[2,6,128,128]{3,2,1,0:T(8,128)(2,1)S(1)}, bf16[2,6,128,128]{3,2,1,0:T(8,128)(2,1)S(1)}, u32[]{:S(2)}, u32[]{:S(2)}) %collective-permute-start.9) | collective-permute-done | bytes 393248 | tf_op jit(solution)/shard_map/ppermute | solution.py:207
  63.0 2.5 %shard_map.67 = (f32[2,3,64,128]{3,2,1,0:T(8,128)S(1)}, f32[2,3,64,128]{3,2,1,0:T(8,128)S(1)}) custom-call(s32[3]{0:T(128)S(1)} %pad_add_fusion.refs_0_, s32[1,1,16]{2,1,0:T(1,128)S(1)} %copy-done.1, s32[1,1,16]{2,1,0:T(1,128)S(1)} %copy-done.2, s32[1,1,16]{2,1,0:T(1,128)S(1)} %copy-done.3, bf16[16,2,3,6,32,128]{5,4,3,2,1,0:T(8,128)(2,1)S(1)} %bitcast.25, ...), custom_call_target="tpu_custom_call" | custom-call | flops 301989888 | bytes 1600000 | tf_op jit(solution)/shard_map/pallas_call | solution.py:179
  65.5 1.4 %collective-permute-start.12 = (f32[2,3,64,128]{3,2,1,0:T(8,128)S(1)}, f32[2,3,64,128]{3,2,1,0:T(8,128)S(1)}, u32[]{:S(2)}, u32[]{:S(2)}) collective-permute-start(f32[2,3,64,128]{3,2,1,0:T(8,128)S(1)} %get-tuple-element.12), channel_id=1, source_target_pairs={{0,2},{2,0},{1,3},{3,1},{4,6},{6,4},{5,7},{7,5},{8,10},{10,8},{9,1... | collective-permute-start | bytes 589832 | tf_op jit(solution)/shard_map/ppermute | solution.py:242
  66.8 0.0 collective-permute-done.6
  66.8 0.7 multiply_bitcast_fusion.1
  67.5 3.7 %collective-permute-done.12 = f32[2,3,64,128]{3,2,1,0:T(8,128)S(1)} collective-permute-done((f32[2,3,64,128]{3,2,1,0:T(8,128)S(1)}, f32[2,3,64,128]{3,2,1,0:T(8,128)S(1)}, u32[]{:S(2)}, u32[]{:S(2)}) %collective-permute-start.12) | collective-permute-done | bytes 196640 | tf_op jit(solution)/shard_map/ppermute | solution.py:242
  71.2 0.6 multiply_bitcast_fusion
  71.8 0.8 %maximum_bitcast_fusion = f32[2,2,3,128,64]{3,4,2,1,0:T(8,128)} fusion(f32[1,2,3,64,128]{4,3,2,1,0:T(8,128)S(1)} %multiply_bitcast_fusion, f32[1,2,3,64,128]{4,3,2,1,0:T(8,128)S(1)} %multiply_bitcast_fusion.1), kind=kLoop, calls=%fused_computation.2 | loop fusion | flops 98304 | bytes 786432 | tf_op jit(solution)/shard_map/transpose | solution.py:254
  (1 shorter events, 0.0 us)
Async XLA Ops:
  0.0 39.1 %collective-permute-start = (bf16[16,2,3,6,32,128]{5,4,3,2,1,0:T(8,128)(2,1)}, bf16[16,2,3,6,32,128]{5,4,3,2,1,0:T(8,128)(2,1)}, u32[]{:S(2)}, u32[]{:S(2)}) collective-permute-start(bf16[16,2,3,6,32,128]{5,4,3,2,1,0:T(8,128)(2,1)} %bitcast.21), channel_id=1, source_target_pairs={{0,1},{1,0},{2,3},{3,2},{4,5},{5,4},{6,7},{7,6},{8,9},{9,8},{10,11... | collective-permute-start | bytes 14155784 | tf_op jit(solution)/shard_map/ppermute | solution.py:225
  1.6 12.6 %collective-permute-start.1 = (bf16[2,6,128,128]{3,2,1,0:T(8,128)(2,1)S(1)}, bf16[2,6,128,128]{3,2,1,0:T(8,128)(2,1)S(1)}, u32[]{:S(2)}, u32[]{:S(2)}) collective-permute-start(bf16[2,6,128,128]{3,2,1,0:T(8,128)(2,1)S(1)} %get-tuple-element.13.refs_6_), channel_id=1, source_target_pairs={{0,4},{4,0},{8,12},{12,8},{1,5},{5,1},{9,13},{13,9},{2,6},{6,2},{1... | collective-permute-start | bytes 1179656 | tf_op jit(solution)/shard_map/ppermute | solution.py:203
  4.3 18.2 %collective-permute-start.7 = (bf16[2,6,128,128]{3,2,1,0:T(8,128)(2,1)S(1)}, bf16[2,6,128,128]{3,2,1,0:T(8,128)(2,1)S(1)}, u32[]{:S(2)}, u32[]{:S(2)}) collective-permute-start(bf16[2,6,128,128]{3,2,1,0:T(8,128)(2,1)S(1)} %get-tuple-element.14.refs_6_), channel_id=1, source_target_pairs={{0,4},{4,0},{8,12},{12,8},{1,5},{5,1},{9,13},{13,9},{2,6},{6,2},{1... | collective-permute-start | bytes 1179656 | tf_op jit(solution)/shard_map/ppermute | solution.py:203
  4.3 18.8 %collective-permute-start.4 = (bf16[2,6,128,128]{3,2,1,0:T(8,128)(2,1)S(1)}, bf16[2,6,128,128]{3,2,1,0:T(8,128)(2,1)S(1)}, u32[]{:S(2)}, u32[]{:S(2)}) collective-permute-start(bf16[2,6,128,128]{3,2,1,0:T(8,128)(2,1)S(1)} %get-tuple-element.13.refs_6_), channel_id=1, source_target_pairs={{4,8},{8,4},{5,9},{9,5},{6,10},{10,6},{7,11},{11,7},{20,24},{24,20... | collective-permute-start | bytes 1179656 | tf_op jit(solution)/shard_map/ppermute | solution.py:204
  14.2 10.2 %collective-permute-start.2 = (bf16[2,6,128,128]{3,2,1,0:T(8,128)(2,1)S(1)}, bf16[2,6,128,128]{3,2,1,0:T(8,128)(2,1)S(1)}, u32[]{:S(2)}, u32[]{:S(2)}) collective-permute-start(bf16[2,6,128,128]{3,2,1,0:T(8,128)(2,1)S(1)} %collective-permute-done.1.refs_7_), channel_id=1, source_target_pairs={{4,8},{8,4},{5,9},{9,5},{6,10},{10,6},{7,11},{11,7},{20,24},{24,20... | collective-permute-start | bytes 1179656 | tf_op jit(solution)/shard_map/ppermute | solution.py:206
  14.9 11.5 %collective-permute-start.10 = (bf16[2,6,128,128]{3,2,1,0:T(8,128)(2,1)S(1)}, bf16[2,6,128,128]{3,2,1,0:T(8,128)(2,1)S(1)}, u32[]{:S(2)}, u32[]{:S(2)}) collective-permute-start(bf16[2,6,128,128]{3,2,1,0:T(8,128)(2,1)S(1)} %get-tuple-element.14.refs_6_), channel_id=1, source_target_pairs={{4,8},{8,4},{5,9},{9,5},{6,10},{10,6},{7,11},{11,7},{20,24},{24,20... | collective-permute-start | bytes 1179656 | tf_op jit(solution)/shard_map/ppermute | solution.py:204
  22.5 5.3 %collective-permute-start.8 = (bf16[2,6,128,128]{3,2,1,0:T(8,128)(2,1)S(1)}, bf16[2,6,128,128]{3,2,1,0:T(8,128)(2,1)S(1)}, u32[]{:S(2)}, u32[]{:S(2)}) collective-permute-start(bf16[2,6,128,128]{3,2,1,0:T(8,128)(2,1)S(1)} %collective-permute-done.7.refs_7_), channel_id=1, source_target_pairs={{4,8},{8,4},{5,9},{9,5},{6,10},{10,6},{7,11},{11,7},{20,24},{24,20... | collective-permute-start | bytes 1179656 | tf_op jit(solution)/shard_map/ppermute | solution.py:206
  23.2 15.9 %collective-permute-start.5 = (bf16[2,6,128,128]{3,2,1,0:T(8,128)(2,1)S(1)}, bf16[2,6,128,128]{3,2,1,0:T(8,128)(2,1)}, u32[]{:S(2)}, u32[]{:S(2)}) collective-permute-start(bf16[2,6,128,128]{3,2,1,0:T(8,128)(2,1)S(1)} %collective-permute-done.4.refs_8_), channel_id=1, source_target_pairs={{4,0},{8,12},{5,1},{9,13},{6,2},{10,14},{7,3},{11,15},{20,16},{24,... | collective-permute-start | bytes 1179656 | tf_op jit(solution)/shard_map/ppermute | solution.py:205
  24.5 23.0 %collective-permute-start.3 = (bf16[2,6,128,128]{3,2,1,0:T(8,128)(2,1)S(1)}, bf16[2,6,128,128]{3,2,1,0:T(8,128)(2,1)}, u32[]{:S(2)}, u32[]{:S(2)}) collective-permute-start(bf16[2,6,128,128]{3,2,1,0:T(8,128)(2,1)S(1)} %collective-permute-done.2.refs_6_), channel_id=1, source_target_pairs={{4,0},{8,12},{5,1},{9,13},{6,2},{10,14},{7,3},{11,15},{20,16},{24,... | collective-permute-start | bytes 1179656 | tf_op jit(solution)/shard_map/ppermute | solution.py:207
  26.4 29.4 %collective-permute-start.11 = (bf16[2,6,128,128]{3,2,1,0:T(8,128)(2,1)S(1)}, bf16[2,6,128,128]{3,2,1,0:T(8,128)(2,1)S(1)}, u32[]{:S(2)}, u32[]{:S(2)}) collective-permute-start(bf16[2,6,128,128]{3,2,1,0:T(8,128)(2,1)S(1)} %collective-permute-done.10.refs_8_), channel_id=1, source_target_pairs={{4,0},{8,12},{5,1},{9,13},{6,2},{10,14},{7,3},{11,15},{20,16},{24,... | collective-permute-start | bytes 1179656 | tf_op jit(solution)/shard_map/ppermute | solution.py:205
  27.8 35.2 %collective-permute-start.9 = (bf16[2,6,128,128]{3,2,1,0:T(8,128)(2,1)S(1)}, bf16[2,6,128,128]{3,2,1,0:T(8,128)(2,1)S(1)}, u32[]{:S(2)}, u32[]{:S(2)}) collective-permute-start(bf16[2,6,128,128]{3,2,1,0:T(8,128)(2,1)S(1)} %collective-permute-done.8.refs_6_), channel_id=1, source_target_pairs={{4,0},{8,12},{5,1},{9,13},{6,2},{10,14},{7,3},{11,15},{20,16},{24,... | collective-permute-start | bytes 1179656 | tf_op jit(solution)/shard_map/ppermute | solution.py:207
  39.1 2.3 %copy-start = (bf16[1,1,16,1,2,3,32,6,128]{8,6,7,5,4,3,2,1,0:T(8,128)(2,1)S(1)}, bf16[1,1,16,1,2,3,32,6,128]{8,6,7,5,4,3,2,1,0:T(8,128)(2,1)}, u32[]{:S(2)}) copy-start(bf16[1,1,16,1,2,3,32,6,128]{8,6,7,5,4,3,2,1,0:T(8,128)(2,1)} %param.6) | copy-start | bytes 14155780
  41.4 0.7 copy-start.1
  42.1 0.7 copy-start.2
  42.7 0.7 copy-start.3
  49.6 17.2 %collective-permute-start.6 = (f32[2,3,64,128]{3,2,1,0:T(8,128)S(1)}, f32[2,3,64,128]{3,2,1,0:T(8,128)S(1)}, u32[]{:S(2)}, u32[]{:S(2)}) collective-permute-start(f32[2,3,64,128]{3,2,1,0:T(8,128)S(1)} %get-tuple-element.10), channel_id=1, source_target_pairs={{0,2},{2,0},{1,3},{3,1},{4,6},{6,4},{5,7},{7,5},{8,10},{10,8},{9,1... | collective-permute-start | bytes 589832 | tf_op jit(solution)/shard_map/ppermute | solution.py:242
  65.5 5.7 %collective-permute-start.12 = (f32[2,3,64,128]{3,2,1,0:T(8,128)S(1)}, f32[2,3,64,128]{3,2,1,0:T(8,128)S(1)}, u32[]{:S(2)}, u32[]{:S(2)}) collective-permute-start(f32[2,3,64,128]{3,2,1,0:T(8,128)S(1)} %get-tuple-element.12), channel_id=1, source_target_pairs={{0,2},{2,0},{1,3},{3,1},{4,6},{6,4},{5,7},{7,5},{8,10},{10,8},{9,1... | collective-permute-start | bytes 589832 | tf_op jit(solution)/shard_map/ppermute | solution.py:242

commit v2 on v0

v2 whole, which is shorter than its diff:
```python
import functools

import jax
import jax.numpy as jnp
from jax import lax
from jax.experimental import pallas as pl
from jax.experimental.pallas import tpu as pltpu
from jax.sharding import PartitionSpec as P

FREQS = 2
SITE_BLOCKS = 4
SUB_BLOCKS = 4
CORNER = 48.0
VMEM_LIMIT = 40 << 20
PREPARE_LIMIT = 50 << 20

SMEM_SPEC = pl.BlockSpec(memory_space=pltpu.SMEM)
VMEM_SPEC = pl.BlockSpec(memory_space=pltpu.VMEM)
HBM_SPEC = pl.BlockSpec(memory_space=pl.ANY)


def place_of(block, z):
    flip = z >= 2
    block = jnp.where(flip, 3 - block, block)
    z = jnp.where(flip, 3 - z, z)
    return jnp.where(block < 2, block ^ z, block)


def prepare_kernel(line, table, own, other, dense, tiles, slot_of, counts, sem):
    z, j, v = table[3, 0], table[3, 1], table[3, 2]
    slots = own.shape[0]
    half = SITE_BLOCKS // 2
    _, _, comps, moments, block_sites, columns = own.shape

    def clear(i, _):
        slot_of[i] = 0
        counts[i] = 0
        return 0

    lax.fori_loop(0, SUB_BLOCKS * SITE_BLOCKS, clear, 0)

    def load(p, _):
        @pl.when(table[2, p] > 0)
        def _():
            pltpu.make_async_copy(own.at[p], tiles.at[0, p], sem).start()
            pltpu.make_async_copy(other.at[p], tiles.at[1, p], sem).start()
            block = table[1, p]
            place = place_of(block, z) if line else block
            s = table[0, p]
            at = place * SITE_BLOCKS + (s // half ^ j) * half + s % half
            slot_of[at] = p
            counts[at] = table[2, p]

        return 0

    lax.fori_loop(0, slots, load, 0)

    def drain(p, _):
        @pl.when(table[2, p] > 0)
        def _():
            pltpu.make_async_copy(own.at[p], tiles.at[0, p], sem).wait()
            pltpu.make_async_copy(other.at[p], tiles.at[1, p], sem).wait()

        return 0

    lax.fori_loop(0, slots, drain, 0)
    lane = lax.broadcasted_iota(jnp.int32, (block_sites, columns), 1)

    def lay(i, _):
        place = i // SITE_BLOCKS
        row = i % SITE_BLOCKS
        slot = slot_of[i]
        live = lane < counts[i]
        for role in range(2):
            f = v if role == 0 else 1 - v
            for r in range(2):
                start = pl.multiple_of((r * SITE_BLOCKS + row) * block_sites, block_sites)
                for c in range(comps):
                    for m in range(moments):
                        value = jnp.where(
                            live, tiles[role, slot, r, c, m], jnp.zeros((), dense.dtype)
                        )
                        dense[
                            f,
                            place,
                            c,
                            pl.ds(start, block_sites),
                            columns * m : columns * (m + 1),
                        ] = value
        return 0

    lax.fori_loop(0, SUB_BLOCKS * SITE_BLOCKS, lay, 0)


def prepare(line, table, own, other):
    slots, _, comps, moments, block_sites, columns = own.shape
    return pl.pallas_call(
        functools.partial(prepare_kernel, line),
        out_shape=pltpu.VMEM(
            (
                FREQS,
                SUB_BLOCKS,
                comps,
                2 * SITE_BLOCKS * block_sites,
                moments * columns,
            ),
            own.dtype,
        ),
        in_specs=[SMEM_SPEC] + [HBM_SPEC] * 2,
        out_specs=VMEM_SPEC,
        scratch_shapes=[
            pltpu.VMEM((2,) + own.shape, own.dtype),
            pltpu.SMEM((SUB_BLOCKS * SITE_BLOCKS,), jnp.int32),
            pltpu.SMEM((SUB_BLOCKS * SITE_BLOCKS,), jnp.int32),
            pltpu.SemaphoreType.DMA,
        ],
        compiler_params=pltpu.CompilerParams(vmem_limit_bytes=PREPARE_LIMIT),
        cost_estimate=pl.CostEstimate(
            flops=0, bytes_accessed=12_000_000, transcendentals=0
        ),
    )(table, own, other)


def products(dense, f, place, c, spectrum):
    moments, variants, columns = spectrum.shape[1:]
    rhs = jnp.concatenate(
        [spectrum[:, m].reshape(2 * variants, columns) for m in range(moments)], axis=1
    )
    total = lax.dot_general(
        dense[f, place, c],
        rhs,
        (((1,), (1,)), ((), ())),
        preferred_element_type=jnp.float32,
    )
    rows = total.shape[0] // 2
    real = total[:rows, :variants] - total[rows:, variants:]
    imag = total[:rows, variants:] + total[rows:, :variants]
    return real, imag


def early_kernel(dense, own, pairs, acc, spec, sem):
    copies = [
        pltpu.make_async_copy(source, spec.at[n], sem.at[n])
        for n, source in enumerate((own, pairs))
    ]
    for copy in copies:
        copy.start()
    for place in range(2):
        copies[place].wait()
        for f in range(FREQS):
            for c in range(dense.shape[2]):
                for r, value in enumerate(products(dense, f, place, c, spec[place, f])):
                    if place == 0:
                        acc[f, r, c] = value
                    else:
                        acc[f, r, c] += value


def early(dense, own, pairs):
    _, _, comps, rows, depth = dense.shape
    variants = own.shape[3]
    return pl.pallas_call(
        early_kernel,
        out_shape=pltpu.VMEM((FREQS, 2, comps, rows // 2, variants), jnp.float32),
        in_specs=[VMEM_SPEC, HBM_SPEC, HBM_SPEC],
        out_specs=VMEM_SPEC,
        scratch_shapes=[
            pltpu.VMEM((2,) + own.shape, own.dtype),
            pltpu.SemaphoreType.DMA((2,)),
        ],
        compiler_params=pltpu.CompilerParams(vmem_limit_bytes=VMEM_LIMIT),
        cost_estimate=pl.CostEstimate(
            flops=8 * comps * rows * 2 * variants * depth,
            bytes_accessed=4_000_000,
            transcendentals=0,
        ),
    )(dense, own, pairs)


def place_sums(dense, f, place, c, spectrum, sums):
    pair = products(dense, f, place, c, spectrum)
    return pair if sums is None else [a + b for a, b in zip(sums, pair)]


def split_halves(sums, c, keep, send):
    half = keep.shape[2]
    for r, value in enumerate(sums):
        keep[r, c] = value[:half]
        send[r, c] = value[half:]


def late_kernel(f, table, dense, acc, *refs):
    places = 2 - f
    sources = refs[: 2 * places]
    *outs, spec, sem = refs[2 * places :]
    is_mid = jnp.logical_and(table[3, 0] > 0, table[3, 0] < 3)

    @pl.when(is_mid)
    def _():
        for n, source in enumerate(sources[:places]):
            pltpu.make_async_copy(source, spec.at[n], sem.at[n]).start()

    @pl.when(jnp.logical_not(is_mid))
    def _():
        for n, source in enumerate(sources[places:]):
            pltpu.make_async_copy(source, spec.at[n], sem.at[n]).start()

    for n in range(places):
        pltpu.make_async_copy(sources[n], spec.at[n], sem.at[n]).wait()
    for c in range(dense.shape[2]):
        sums = [acc[f, r, c] for r in range(2)]
        for n in range(places):
            sums = place_sums(dense, f, 2 + n, c, spec[n], sums)
        if f == 0:
            split_halves(sums, c, *outs)
        else:
            for r, value in enumerate(sums):
                outs[0][r, c] = value


def late(f, table, dense, acc, sources):
    _, _, comps, rows, depth = dense.shape
    shape = sources[0].shape
    places = len(sources) // 2
    half = pltpu.VMEM((2, comps, rows // 4, shape[2]), jnp.float32)
    full = pltpu.VMEM((2, comps, rows // 2, shape[2]), jnp.float32)
    return pl.pallas_call(
        functools.partial(late_kernel, f),
        out_shape=(half, half) if f == 0 else full,
        in_specs=[SMEM_SPEC, VMEM_SPEC, VMEM_SPEC] + [HBM_SPEC] * len(sources),
        out_specs=(VMEM_SPEC, VMEM_SPEC) if f == 0 else VMEM_SPEC,
        scratch_shapes=[
            pltpu.VMEM((places,) + shape, dense.dtype),
            pltpu.SemaphoreType.DMA((places,)),
        ],
        compiler_params=pltpu.CompilerParams(vmem_limit_bytes=VMEM_LIMIT),
        cost_estimate=pl.CostEstimate(
            flops=2 * places * comps * rows * 2 * shape[2] * depth,
            bytes_accessed=800_000 * places,
            transcendentals=0,
        ),
    )(table, dense, acc, *sources)


def last_kernel(table, dense, acc, middle, far, keep, send):
    is_mid = jnp.logical_and(table[3, 0] > 0, table[3, 0] < 3)

    def run(source):
        for c in range(dense.shape[2]):
            sums = [acc[r, c] for r in range(2)]
            split_halves(place_sums(dense, 1, 3, c, source[...], sums), c, keep, send)

    @pl.when(is_mid)
    def _():
        run(middle)

    @pl.when(jnp.logical_not(is_mid))
    def _():
        run(far)


def last(table, dense, acc, middle, far):
    _, _, comps, rows, depth = dense.shape
    half = (2, comps, rows // 4, middle.shape[2])
    return pl.pallas_call(
        last_kernel,
        out_shape=(pltpu.VMEM(half, jnp.float32),) * 2,
        in_specs=[SMEM_SPEC] + [VMEM_SPEC] * 4,
        out_specs=(VMEM_SPEC,) * 2,
        compiler_params=pltpu.CompilerParams(vmem_limit_bytes=VMEM_LIMIT),
        cost_estimate=pl.CostEstimate(
            flops=2 * comps * rows * 2 * middle.shape[2] * depth,
            bytes_accessed=1_000_000,
            transcendentals=0,
        ),
    )(table, dense, acc, middle, far)


def whole_kernel(f, dense, parts, keep, send, spec, sem):
    copy = pltpu.make_async_copy(parts, spec, sem)
    copy.start()
    copy.wait()
    for c in range(dense.shape[2]):
        sums = None
        for place in range(SUB_BLOCKS):
            sums = place_sums(dense, f, place, c, spec[place], sums)
        split_halves(sums, c, keep, send)


def whole(f, dense, parts):
    _, _, comps, rows, depth = dense.shape
    half = jax.ShapeDtypeStruct((2, comps, rows // 4, parts.shape[3]), jnp.float32)
    return pl.pallas_call(
        functools.partial(whole_kernel, f),
        out_shape=(half, half),
        in_specs=[VMEM_SPEC, HBM_SPEC],
        out_specs=(VMEM_SPEC,) * 2,
        scratch_shapes=[
            pltpu.VMEM(parts.shape, parts.dtype),
            pltpu.SemaphoreType.DMA,
        ],
        compiler_params=pltpu.CompilerParams(vmem_limit_bytes=VMEM_LIMIT),
    )(dense, parts)


def finish_kernel(brune, *refs):
    result, value, sem = refs[-3:]
    copies = []
    for f in range(FREQS):
        keep, got = refs[2 * f : 2 * f + 2]
        for r in range(2):
            value[f, r] = (keep[r] + got[r]) * brune[f]
            copy = pltpu.make_async_copy(value.at[f, r], result.at[f, r], sem.at[f, r])
            copy.start()
            copies.append(copy)
    for copy in copies:
        copy.wait()


def finish(brune, pieces):
    shape = (FREQS,) + pieces[0].shape
    return pl.pallas_call(
        finish_kernel,
        out_shape=jax.ShapeDtypeStruct(shape, pieces[0].dtype),
        in_specs=[SMEM_SPEC] + [VMEM_SPEC] * len(pieces),
        out_specs=HBM_SPEC,
        scratch_shapes=[
            pltpu.VMEM(shape, pieces[0].dtype),
            pltpu.SemaphoreType.DMA((FREQS, 2)),
        ],
        compiler_params=pltpu.CompilerParams(vmem_limit_bytes=VMEM_LIMIT),
        cost_estimate=pl.CostEstimate(
            flops=400_000, bytes_accessed=600_000, transcendentals=0
        ),
    )(brune, *pieces)


def after(value, *others):
    return lax.optimization_barrier((value, *others))[0]


PAIRS = [(0, 1), (1, 0), (2, 3), (3, 2)]
INNER = [(1, 2), (2, 1)]
OUTER = [(1, 0), (2, 3)]


def line_steps(own, dense):
    move = functools.partial(lax.ppermute, axis_name="site")
    pairs = move(own, perm=PAIRS)
    inner = [move(own[f], perm=INNER) for f in range(FREQS)]
    outer = [move(inner[f], perm=OUTER) for f in range(FREQS)]
    ready = after(pairs, dense)
    middle = [move(after(ready[f], *inner), perm=INNER) for f in range(FREQS)]
    acc = early(dense, own, pairs)
    far = [move(after(middle[f], outer[f], acc), perm=OUTER) for f in range(FREQS)]
    first, second = zip(inner, middle, outer, far)
    return acc, first, second


def exchange(send):
    return lax.ppermute(send, "sub", [(0, 1), (1, 0)])


def shards(n_site, n_sub, tensor, spectra, pair_site, pair_block, pair_count, offset):
    spectra = spectra.transpose(0, 1, 3, 2, 4)
    tensor = tensor[0, 0, :, 0].transpose(0, 1, 2, 4, 3, 5)
    swap = n_sub == 2
    line = swap and n_site == SUB_BLOCKS
    half = lax.axis_index("sub") if swap else 0
    ids = jnp.stack([lax.axis_index("site"), half, lax.axis_index("var")])
    ids = jnp.pad(ids.astype(jnp.int32), (0, tensor.shape[0] - 3))
    table = jnp.stack([pair_site[0, 0], pair_block[0, 0], pair_count[0, 0], ids])
    freq_index = (offset[0] + jnp.arange(FREQS, dtype=jnp.int32)).astype(jnp.float32)
    brune = 1.0 / (1.0 + (freq_index / CORNER) ** 2)
    other = lax.ppermute(tensor, "var", [(0, 1), (1, 0)])
    dense = prepare(line, table, tensor, other)
    if line:
        acc, first, second = line_steps(spectra, dense)
        inner1, middle1, outer1, far1 = second
        keep, send = late(0, table, dense, acc, first)
        pieces = [keep, exchange(send)]
        more = late(1, table, dense, acc, (inner1, outer1))
        far1 = after(far1, pieces[1], more)
        keep, send = last(table, dense, more, middle1, far1)
        pieces += [keep, exchange(send)]
    else:
        gathered = lax.all_gather(spectra, "site", axis=4, tiled=True)
        pieces = []
        for f in range(FREQS):
            blocks = gathered[f].reshape(gathered.shape[1:4] + (SUB_BLOCKS, -1))
            keep, send = whole(f, dense, blocks.transpose(3, 0, 1, 2, 4))
            if swap:
                pieces += [keep, exchange(send)]
            else:
                both = jnp.concatenate([keep, send], axis=2)
                keep = lax.psum_scatter(both, "sub", scatter_dimension=2, tiled=True)
                pieces += [keep, jnp.zeros_like(keep)]
    result = finish(brune, pieces)
    return result.transpose(0, 1, 2, 4, 3)


def solution(mesh):
    return jax.shard_map(
        functools.partial(shards, mesh.shape["site"], mesh.shape["sub"]),
        mesh=mesh,
        in_specs=(
            P(("scen", "site"), "sub", None, "var", None, None, None, None, None),
            P(None, None, ("scen", "var"), None, ("sub", "site")),
            P(("scen", "site"), "sub", None),
            P(("scen", "site"), "sub", None),
            P(("scen", "site"), "sub", None),
            P("scen"),
        ),
        out_specs=P(None, None, None, "var", ("scen", "site", "sub")),
        check_vma=False,
    )
```

time: 214 us -> 66.1 us (0.31)
  waiting for transfers between devices: 108 us -> 36.1 us
  local copies, waits for them, and re-layouts: 29.8 us -> 1.26 us
  matrix products: 27.9 us -> 0 us
  loops' own time: 20.9 us -> 0 us
  starting transfers between devices: 0.08 us -> 14.2 us
  between operations: 13.8 us -> 0.82 us
  Pallas kernels: 0 us -> 12.1 us
  other arithmetic: 12.8 us -> 1.36 us
    all_gather x2 -> x0, waiting for transfers between devices: 88.6 us -> none  [the longest x1 67 us: shards(): spectra = lax.all_gather(rupture_spectra, 'site', axis=4, tiled=True)]
    ppermute x0 -> x12, waiting for transfers between devices: none -> 36.1 us  [the longest x2 13 us: line_steps(): outer = [move(inner[f], perm=OUTER) for f in range(FREQS)]]
    dynamic_slice x64 -> x0, local copies, waits for them, and re-layouts: 28.9 us -> none  [the longest x16 9.52 us: add_pair(): corner = (total_start, 0, 0, 0, site_table[slot] * block_sites)]
    dot_general x16 -> x0, matrix products: 27.9 us -> none  [add_pair(): jnp.einsum('fpcsmk,fqvmk->fpqcvs', tensor_tile, spectrum, preferred_eleme...]
    another operation x1 -> x0, loops' own time: 20.9 us -> none  [pair_terms(): return lax.fori_loop(0, slot_count, add_pair, totals)]
    reduce_scatter x1 -> x0, waiting for transfers between devices: 18.1 us -> none  [shards(): lax.psum_scatter(totals, 'sub', scatter_dimension=4, tiled=True)]
    ppermute x0 -> x12, starting transfers between devices: none -> 14.2 us  [the longest x2 3.12 us: exchange(): return lax.ppermute(send, 'sub', [(0, 1), (1, 0)])]
    pallas_call x0 -> x6, Pallas kernels: none -> 12.1 us  [the longest x1 4.81 us: prepare(): pl.pallas_call(functools.partial(prepare_kernel, line), out_shape=pltpu.V...]
  transfers between devices with their start and end apart: 3 -> 12, of which waited for: 3 -> 6; matrix products, arithmetic and copies ran while one was open for 0% -> 4% of each run, Pallas kernels for 0% -> 15%
where the time goes in v2:
time: 66.1 us; the launch traced here: 65.8 us
  waiting for transfers between devices  36.1 us (55%)
  starting transfers between devices  14.2 us (21%)
  Pallas kernels  12.1 us (18%)
  other arithmetic  1.36 us (2%)
  local copies, waits for them, and re-layouts  1.26 us (2%)
  between operations  0.82 us (1%)
    ppermute x2, waiting for transfers between devices, line_steps(): outer = [move(inner[f], perm=OUTER) for f in range(FREQS)]  13 us
    ppermute x2, waiting for transfers between devices, line_steps(): move(after(middle[f], outer[f], acc), perm=OUTER)  11.1 us
    ppermute x1, waiting for transfers between devices, line_steps(): pairs = move(own, perm=PAIRS)  8.41 us
    pallas_call x1, Pallas kernels, prepare(): pl.pallas_call(functools.partial(prepare_kernel, line), out_shape=pltpu.V...  4.81 us
    ppermute x2, waiting for transfers between devices, exchange(): return lax.ppermute(send, 'sub', [(0, 1), (1, 0)])  3.51 us
    ppermute x2, starting transfers between devices, exchange(): return lax.ppermute(send, 'sub', [(0, 1), (1, 0)])  3.12 us
    pallas_call x2, Pallas kernels, late(): pl.pallas_call(functools.partial(late_kernel, f), out_shape=(half, half)...  3.11 us
    ppermute x2, starting transfers between devices, line_steps(): outer = [move(inner[f], perm=OUTER) for f in range(FREQS)]  2.7 us
  transfers between devices with their start and end apart: 12, of which 6 were waited for; matrix products, arithmetic and copies ran while one was open for 4% of the time, Pallas kernels for 15%

profile of v2, /device:TPU:0, one launch (start us, length us, event | category | flops | bytes accessed | tf_op | source)
XLA Modules:
  0.0 65.8 jit_solution(9817317913812970289)
XLA Ops:
  0.0 0.5 collective-permute-start
  0.5 2.6 %collective-permute-start.1 = (bf16[2,2,6,128,128]{4,3,2,1,0:T(8,128)(2,1)}, bf16[2,2,6,128,128]{4,3,2,1,0:T(8,128)(2,1)S(1)}, u32[]{:S(2)}, u32[]{:S(2)}) collective-permute-start(bf16[2,2,6,128,128]{4,3,2,1,0:T(8,128)(2,1)} %bitcast.23), channel_id=1, source_target_pairs={{0,4},{4,0},{8,12},{12,8},{1,5},{5,1},{9,13},{13,9},{2,6},{6,2},{1... | collective-permute-start | bytes 2359304 | tf_op jit(solution)/shard_map/ppermute | solution.py:349
  3.0 1.2 %slice_bitcast_fusion = (bf16[2,6,128,128]{3,2,1,0:T(8,128)(2,1)S(1)}, bf16[2,6,128,128]{3,2,1,0:T(8,128)(2,1)S(1)}) fusion(bf16[2,2,6,128,128]{4,3,2,1,0:T(8,128)(2,1)} %bitcast.24), kind=kLoop, calls=%fused_computation | loop fusion | bytes 1572864 | tf_op jit(solution)/shard_map/squeeze | solution.py:350
  4.2 0.7 %collective-permute-start.2 = (bf16[2,6,128,128]{3,2,1,0:T(8,128)(2,1)S(1)}, bf16[2,6,128,128]{3,2,1,0:T(8,128)(2,1)S(1)}, u32[]{:S(2)}, u32[]{:S(2)}) collective-permute-start(bf16[2,6,128,128]{3,2,1,0:T(8,128)(2,1)S(1)} %get-tuple-element.28), channel_id=1, source_target_pairs={{4,8},{8,4},{5,9},{9,5},{6,10},{10,6},{7,11},{11,7},{20,24},{24,20... | collective-permute-start | bytes 1179656 | tf_op jit(solution)/shard_map/ppermute | solution.py:350
  4.9 0.7 %collective-permute-start.3 = (bf16[2,6,128,128]{3,2,1,0:T(8,128)(2,1)S(1)}, bf16[2,6,128,128]{3,2,1,0:T(8,128)(2,1)S(1)}, u32[]{:S(2)}, u32[]{:S(2)}) collective-permute-start(bf16[2,6,128,128]{3,2,1,0:T(8,128)(2,1)S(1)} %get-tuple-element.27), channel_id=1, source_target_pairs={{4,8},{8,4},{5,9},{9,5},{6,10},{10,6},{7,11},{11,7},{20,24},{24,20... | collective-permute-start | bytes 1179656 | tf_op jit(solution)/shard_map/ppermute | solution.py:350
  5.6 0.1 pad_add_fusion.1
  5.7 1.3 %pad_add_fusion.table = s32[4,16]{1,0:T(4,128)} fusion(s32[1,16]{1,0:T(1,128)S(1)} %pad_bitcast_fusion, s32[1,16]{1,0:T(1,128)} %bitcast.28, s32[1,16]{1,0:T(1,128)} %bitcast.29, s32[1,16]{1,0:T(1,128)} %bitcast.30), kind=kLoop, calls=%fused_computation.4 | loop fusion | flops 192 | bytes 512 | tf_op jit(solution)/shard_map/stack | solution.py:372
  7.0 0.0 copy-start
  7.0 0.0 collective-permute-done.2.refs_0_
  7.0 1.4 %collective-permute-start.5 = (bf16[2,6,128,128]{3,2,1,0:T(8,128)(2,1)S(1)}, bf16[2,6,128,128]{3,2,1,0:T(8,128)(2,1)S(1)}, u32[]{:S(2)}, u32[]{:S(2)}) collective-permute-start(bf16[2,6,128,128]{3,2,1,0:T(8,128)(2,1)S(1)} %collective-permute-done.2.refs_0_), channel_id=1, source_target_pairs={{4,0},{8,12},{5,1},{9,13},{6,2},{10,14},{7,3},{11,15},{20,16},{24,... | collective-permute-start | bytes 1179656 | tf_op jit(solution)/shard_map/ppermute | solution.py:351
  8.4 0.0 collective-permute-done.other
  8.4 4.8 %shard_map.64.dense = bf16[2,4,3,256,768]{4,3,2,1,0:T(8,128)(2,1)S(1)} custom-call(s32[4,16]{1,0:T(4,128)} %pad_add_fusion.table, bf16[16,2,3,6,32,128]{5,4,3,2,1,0:T(8,128)(2,1)} %bitcast.27, bf16[16,2,3,6,32,128]{5,4,3,2,1,0:T(8,128)(2,1)} %collective-permute-done.other), custom_call_target="tpu_custom_call" | custom-call | bytes 12000000 | tf_op jit(solution)/shard_map/pallas_call | solution.py:97
  13.2 8.4 %collective-permute-done.1.pairs = bf16[2,2,6,128,128]{4,3,2,1,0:T(8,128)(2,1)S(1)} collective-permute-done((bf16[2,2,6,128,128]{4,3,2,1,0:T(8,128)(2,1)}, bf16[2,2,6,128,128]{4,3,2,1,0:T(8,128)(2,1)S(1)}, u32[]{:S(2)}, u32[]{:S(2)}) %collective-permute-start.1) | collective-permute-done | bytes 786464 | tf_op jit(solution)/shard_map/ppermute | solution.py:349
  21.6 0.1 slice_bitcast_fusion.2
  21.7 0.0 collective-permute-done.3.refs_0_
  21.7 0.7 %collective-permute-start.4 = (bf16[2,6,128,128]{3,2,1,0:T(8,128)(2,1)S(1)}, bf16[2,6,128,128]{3,2,1,0:T(8,128)(2,1)S(1)}, u32[]{:S(2)}, u32[]{:S(2)}) collective-permute-start(bf16[2,6,128,128]{3,2,1,0:T(8,128)(2,1)S(1)} %get-tuple-element.16), channel_id=1, source_target_pairs={{4,8},{8,4},{5,9},{9,5},{6,10},{10,6},{7,11},{11,7},{20,24},{24,20... | collective-permute-start | bytes 1179656 | tf_op jit(solution)/shard_map/ppermute | solution.py:353
  22.4 1.3 %collective-permute-start.8 = (bf16[2,6,128,128]{3,2,1,0:T(8,128)(2,1)S(1)}, bf16[2,6,128,128]{3,2,1,0:T(8,128)(2,1)S(1)}, u32[]{:S(2)}, u32[]{:S(2)}) collective-permute-start(bf16[2,6,128,128]{3,2,1,0:T(8,128)(2,1)S(1)} %collective-permute-done.3.refs_0_), channel_id=1, source_target_pairs={{4,0},{8,12},{5,1},{9,13},{6,2},{10,14},{7,3},{11,15},{20,16},{24,... | collective-permute-start | bytes 1179656 | tf_op jit(solution)/shard_map/ppermute | solution.py:351
  23.7 0.0 copy-start.1
  23.7 0.7 %collective-permute-start.9 = (bf16[2,6,128,128]{3,2,1,0:T(8,128)(2,1)S(1)}, bf16[2,6,128,128]{3,2,1,0:T(8,128)(2,1)S(1)}, u32[]{:S(2)}, u32[]{:S(2)}) collective-permute-start(bf16[2,6,128,128]{3,2,1,0:T(8,128)(2,1)S(1)} %get-tuple-element.20), channel_id=1, source_target_pairs={{4,8},{8,4},{5,9},{9,5},{6,10},{10,6},{7,11},{11,7},{20,24},{24,20... | collective-permute-start | bytes 1179656 | tf_op jit(solution)/shard_map/ppermute | solution.py:353
  24.4 0.0 copy-done
  24.4 1.8 %shard_map.65.acc = f32[2,2,3,128,128]{4,3,2,1,0:T(8,128)S(1)} custom-call(bf16[2,4,3,256,768]{4,3,2,1,0:T(8,128)(2,1)S(1)} %shard_map.64.dense, bf16[2,2,6,128,128]{4,3,2,1,0:T(8,128)(2,1)S(1)} %bitcast.25, bf16[2,2,6,128,128]{4,3,2,1,0:T(8,128)(2,1)S(1)} %collective-permute-done.1.pairs), custom_call_target="tpu_custom_call" | custom-call | flops 1207959552 | bytes 4000000 | tf_op jit(solution)/shard_map/pallas_call | solution.py:162
  26.2 3.7 %collective-permute-done.5.refs_2_ = bf16[2,6,128,128]{3,2,1,0:T(8,128)(2,1)S(1)} collective-permute-done((bf16[2,6,128,128]{3,2,1,0:T(8,128)(2,1)S(1)}, bf16[2,6,128,128]{3,2,1,0:T(8,128)(2,1)S(1)}, u32[]{:S(2)}, u32[]{:S(2)}) %collective-permute-start.5) | collective-permute-done | bytes 393248 | tf_op jit(solution)/shard_map/ppermute | solution.py:351
  29.9 0.0 collective-permute-done.4.refs_1_
  29.9 1.3 %collective-permute-start.6 = (bf16[2,6,128,128]{3,2,1,0:T(8,128)(2,1)S(1)}, bf16[2,6,128,128]{3,2,1,0:T(8,128)(2,1)S(1)}, u32[]{:S(2)}, u32[]{:S(2)}) collective-permute-start(bf16[2,6,128,128]{3,2,1,0:T(8,128)(2,1)S(1)} %collective-permute-done.4.refs_1_), channel_id=1, source_target_pairs={{4,0},{8,12},{5,1},{9,13},{6,2},{10,14},{7,3},{11,15},{20,16},{24,... | collective-permute-start | bytes 1179656 | tf_op jit(solution)/shard_map/ppermute | solution.py:355
  31.2 9.4 %collective-permute-done.8.refs_1_ = bf16[2,6,128,128]{3,2,1,0:T(8,128)(2,1)S(1)} collective-permute-done((bf16[2,6,128,128]{3,2,1,0:T(8,128)(2,1)S(1)}, bf16[2,6,128,128]{3,2,1,0:T(8,128)(2,1)S(1)}, u32[]{:S(2)}, u32[]{:S(2)}) %collective-permute-start.8) | collective-permute-done | bytes 393248 | tf_op jit(solution)/shard_map/ppermute | solution.py:351
  40.5 0.0 collective-permute-done.9.middle
  40.5 1.3 %collective-permute-start.10 = (bf16[2,6,128,128]{3,2,1,0:T(8,128)(2,1)S(1)}, bf16[2,6,128,128]{3,2,1,0:T(8,128)(2,1)S(1)}, u32[]{:S(2)}, u32[]{:S(2)}) collective-permute-start(bf16[2,6,128,128]{3,2,1,0:T(8,128)(2,1)S(1)} %collective-permute-done.9.middle), channel_id=1, source_target_pairs={{4,0},{8,12},{5,1},{9,13},{6,2},{10,14},{7,3},{11,15},{20,16},{24,... | collective-permute-start | bytes 1179656 | tf_op jit(solution)/shard_map/ppermute | solution.py:355
  41.8 7.4 %collective-permute-done.6.refs_3_ = bf16[2,6,128,128]{3,2,1,0:T(8,128)(2,1)S(1)} collective-permute-done((bf16[2,6,128,128]{3,2,1,0:T(8,128)(2,1)S(1)}, bf16[2,6,128,128]{3,2,1,0:T(8,128)(2,1)S(1)}, u32[]{:S(2)}, u32[]{:S(2)}) %collective-permute-start.6) | collective-permute-done | bytes 393248 | tf_op jit(solution)/shard_map/ppermute | solution.py:355
  49.2 0.0 copy-done.1
  49.2 1.8 %shard_map.66 = (f32[2,3,64,128]{3,2,1,0:T(8,128)S(1)}, f32[2,3,64,128]{3,2,1,0:T(8,128)S(1)}) custom-call(s32[4,16]{1,0:T(4,128)S(1)} %copy-done.1, bf16[2,4,3,256,768]{4,3,2,1,0:T(8,128)(2,1)S(1)} %shard_map.64.dense, f32[2,2,3,128,128]{4,3,2,1,0:T(8,128)S(1)} %shard_map.65.acc, bf16[2,6,128,128]{3,2,1,0:T(8,128)(2,1)S(1)} %collective-permute-done.2.refs_0_, ...), custom_call_target="tpu_custom_call" | custom-call | flops 603979776 | bytes 1600000 | tf_op jit(solution)/shard_map/pallas_call | solution.py:227
  51.0 1.6 %collective-permute-start.7 = (f32[2,3,64,128]{3,2,1,0:T(8,128)S(1)}, f32[2,3,64,128]{3,2,1,0:T(8,128)S(1)}, u32[]{:S(2)}, u32[]{:S(2)}) collective-permute-start(f32[2,3,64,128]{3,2,1,0:T(8,128)S(1)} %get-tuple-element.19), channel_id=1, source_target_pairs={{0,2},{2,0},{1,3},{3,1},{4,6},{6,4},{5,7},{7,5},{8,10},{10,8},{9,1... | collective-permute-start | bytes 589832 | tf_op jit(solution)/shard_map/ppermute | solution.py:361
  52.6 1.3 %shard_map.67.acc = f32[2,3,128,128]{3,2,1,0:T(8,128)S(1)} custom-call(s32[4,16]{1,0:T(4,128)S(1)} %copy-done.1, bf16[2,4,3,256,768]{4,3,2,1,0:T(8,128)(2,1)S(1)} %shard_map.64.dense, f32[2,2,3,128,128]{4,3,2,1,0:T(8,128)S(1)} %shard_map.65.acc, bf16[2,6,128,128]{3,2,1,0:T(8,128)(2,1)S(1)} %collective-permute-done.3.refs_0_, ...), custom_call_target="tpu_custom_call" | custom-call | flops 301989888 | bytes 800000 | tf_op jit(solution)/shard_map/pallas_call | solution.py:227
  53.9 3.7 %collective-permute-done.10.far = bf16[2,6,128,128]{3,2,1,0:T(8,128)(2,1)S(1)} collective-permute-done((bf16[2,6,128,128]{3,2,1,0:T(8,128)(2,1)S(1)}, bf16[2,6,128,128]{3,2,1,0:T(8,128)(2,1)S(1)}, u32[]{:S(2)}, u32[]{:S(2)}) %collective-permute-start.10) | collective-permute-done | bytes 393248 | tf_op jit(solution)/shard_map/ppermute | solution.py:355
  57.6 0.0 collective-permute-done.7.refs_1_
  57.6 1.1 %shard_map.68 = (f32[2,3,64,128]{3,2,1,0:T(8,128)S(1)}, f32[2,3,64,128]{3,2,1,0:T(8,128)S(1)}) custom-call(s32[4,16]{1,0:T(4,128)S(1)} %copy-done.1, bf16[2,4,3,256,768]{4,3,2,1,0:T(8,128)(2,1)S(1)} %shard_map.64.dense, f32[2,3,128,128]{3,2,1,0:T(8,128)S(1)} %shard_map.67.acc, bf16[2,6,128,128]{3,2,1,0:T(8,128)(2,1)S(1)} %collective-permute-done.9.middle, ...), custom_call_target="tpu_custom_call" | custom-call | flops 301989888 | bytes 1000000 | tf_op jit(solution)/shard_map/pallas_call | solution.py:265
  58.7 1.6 %collective-permute-start.11 = (f32[2,3,64,128]{3,2,1,0:T(8,128)S(1)}, f32[2,3,64,128]{3,2,1,0:T(8,128)S(1)}, u32[]{:S(2)}, u32[]{:S(2)}) collective-permute-start(f32[2,3,64,128]{3,2,1,0:T(8,128)S(1)} %get-tuple-element.24), channel_id=1, source_target_pairs={{0,2},{2,0},{1,3},{3,1},{4,6},{6,4},{5,7},{7,5},{8,10},{10,8},{9,1... | collective-permute-start | bytes 589832 | tf_op jit(solution)/shard_map/ppermute | solution.py:361
  61.0 3.5 %collective-permute-done.11.refs_3_ = f32[2,3,64,128]{3,2,1,0:T(8,128)S(1)} collective-permute-done((f32[2,3,64,128]{3,2,1,0:T(8,128)S(1)}, f32[2,3,64,128]{3,2,1,0:T(8,128)S(1)}, u32[]{:S(2)}, u32[]{:S(2)}) %collective-permute-start.11) | collective-permute-done | bytes 196640 | tf_op jit(solution)/shard_map/ppermute | solution.py:361
  64.5 1.3 %shard_map.69 = f32[2,2,3,64,128]{4,3,2,1,0:T(8,128)} custom-call(f32[2]{0:T(128)S(1)} %add_divide_fusion.brune, f32[2,3,64,128]{3,2,1,0:T(8,128)S(1)} %get-tuple-element.18.refs_0_, f32[2,3,64,128]{3,2,1,0:T(8,128)S(1)} %collective-permute-done.7.refs_1_, f32[2,3,64,128]{3,2,1,0:T(8,128)S(1)} %get-tuple-element.23.refs_2_, ...), custom_call_target="tpu_custom_call" | custom-call | flops 400000 | bytes 600000 | tf_op jit(solution)/shard_map/pallas_call | solution.py:322
  (2 shorter events, 0.0 us)
Async XLA Ops:
  0.0 8.4 %collective-permute-start = (bf16[16,2,3,6,32,128]{5,4,3,2,1,0:T(8,128)(2,1)}, bf16[16,2,3,6,32,128]{5,4,3,2,1,0:T(8,128)(2,1)}, u32[]{:S(2)}, u32[]{:S(2)}) collective-permute-start(bf16[16,2,3,6,32,128]{5,4,3,2,1,0:T(8,128)(2,1)} %bitcast.26), channel_id=1, source_target_pairs={{0,1},{1,0},{2,3},{3,2},{4,5},{5,4},{6,7},{7,6},{8,9},{9,8},{10,11... | collective-permute-start | bytes 14155784 | tf_op jit(solution)/shard_map/ppermute | solution.py:375
  0.5 21.2 %collective-permute-start.1 = (bf16[2,2,6,128,128]{4,3,2,1,0:T(8,128)(2,1)}, bf16[2,2,6,128,128]{4,3,2,1,0:T(8,128)(2,1)S(1)}, u32[]{:S(2)}, u32[]{:S(2)}) collective-permute-start(bf16[2,2,6,128,128]{4,3,2,1,0:T(8,128)(2,1)} %bitcast.23), channel_id=1, source_target_pairs={{0,4},{4,0},{8,12},{12,8},{1,5},{5,1},{9,13},{13,9},{2,6},{6,2},{1... | collective-permute-start | bytes 2359304 | tf_op jit(solution)/shard_map/ppermute | solution.py:349
  4.2 2.8 %collective-permute-start.2 = (bf16[2,6,128,128]{3,2,1,0:T(8,128)(2,1)S(1)}, bf16[2,6,128,128]{3,2,1,0:T(8,128)(2,1)S(1)}, u32[]{:S(2)}, u32[]{:S(2)}) collective-permute-start(bf16[2,6,128,128]{3,2,1,0:T(8,128)(2,1)S(1)} %get-tuple-element.28), channel_id=1, source_target_pairs={{4,8},{8,4},{5,9},{9,5},{6,10},{10,6},{7,11},{11,7},{20,24},{24,20... | collective-permute-start | bytes 1179656 | tf_op jit(solution)/shard_map/ppermute | solution.py:350
  4.9 16.8 %collective-permute-start.3 = (bf16[2,6,128,128]{3,2,1,0:T(8,128)(2,1)S(1)}, bf16[2,6,128,128]{3,2,1,0:T(8,128)(2,1)S(1)}, u32[]{:S(2)}, u32[]{:S(2)}) collective-permute-start(bf16[2,6,128,128]{3,2,1,0:T(8,128)(2,1)S(1)} %get-tuple-element.27), channel_id=1, source_target_pairs={{4,8},{8,4},{5,9},{9,5},{6,10},{10,6},{7,11},{11,7},{20,24},{24,20... | collective-permute-start | bytes 1179656 | tf_op jit(solution)/shard_map/ppermute | solution.py:350
  7.0 17.4 %copy-start = (bf16[2,2,128,6,128]{4,2,3,1,0:T(8,128)(2,1)S(1)}, bf16[2,2,128,6,128]{4,2,3,1,0:T(8,128)(2,1)}, u32[]{:S(2)}) copy-start(bf16[2,2,128,6,128]{4,2,3,1,0:T(8,128)(2,1)} %param.7) | copy-start | bytes 2359300
  7.0 22.9 %collective-permute-start.5 = (bf16[2,6,128,128]{3,2,1,0:T(8,128)(2,1)S(1)}, bf16[2,6,128,128]{3,2,1,0:T(8,128)(2,1)S(1)}, u32[]{:S(2)}, u32[]{:S(2)}) collective-permute-start(bf16[2,6,128,128]{3,2,1,0:T(8,128)(2,1)S(1)} %collective-permute-done.2.refs_0_), channel_id=1, source_target_pairs={{4,0},{8,12},{5,1},{9,13},{6,2},{10,14},{7,3},{11,15},{20,16},{24,... | collective-permute-start | bytes 1179656 | tf_op jit(solution)/shard_map/ppermute | solution.py:351
  21.7 8.2 %collective-permute-start.4 = (bf16[2,6,128,128]{3,2,1,0:T(8,128)(2,1)S(1)}, bf16[2,6,128,128]{3,2,1,0:T(8,128)(2,1)S(1)}, u32[]{:S(2)}, u32[]{:S(2)}) collective-permute-start(bf16[2,6,128,128]{3,2,1,0:T(8,128)(2,1)S(1)} %get-tuple-element.16), channel_id=1, source_target_pairs={{4,8},{8,4},{5,9},{9,5},{6,10},{10,6},{7,11},{11,7},{20,24},{24,20... | collective-permute-start | bytes 1179656 | tf_op jit(solution)/shard_map/ppermute | solution.py:353
  22.4 18.1 %collective-permute-start.8 = (bf16[2,6,128,128]{3,2,1,0:T(8,128)(2,1)S(1)}, bf16[2,6,128,128]{3,2,1,0:T(8,128)(2,1)S(1)}, u32[]{:S(2)}, u32[]{:S(2)}) collective-permute-start(bf16[2,6,128,128]{3,2,1,0:T(8,128)(2,1)S(1)} %collective-permute-done.3.refs_0_), channel_id=1, source_target_pairs={{4,0},{8,12},{5,1},{9,13},{6,2},{10,14},{7,3},{11,15},{20,16},{24,... | collective-permute-start | bytes 1179656 | tf_op jit(solution)/shard_map/ppermute | solution.py:351
  23.7 25.5 %copy-start.1 = (s32[4,16]{1,0:T(4,128)S(1)}, s32[4,16]{1,0:T(4,128)}, u32[]{:S(2)}) copy-start(s32[4,16]{1,0:T(4,128)} %pad_add_fusion.table) | copy-start | bytes 772
  23.7 16.8 %collective-permute-start.9 = (bf16[2,6,128,128]{3,2,1,0:T(8,128)(2,1)S(1)}, bf16[2,6,128,128]{3,2,1,0:T(8,128)(2,1)S(1)}, u32[]{:S(2)}, u32[]{:S(2)}) collective-permute-start(bf16[2,6,128,128]{3,2,1,0:T(8,128)(2,1)S(1)} %get-tuple-element.20), channel_id=1, source_target_pairs={{4,8},{8,4},{5,9},{9,5},{6,10},{10,6},{7,11},{11,7},{20,24},{24,20... | collective-permute-start | bytes 1179656 | tf_op jit(solution)/shard_map/ppermute | solution.py:353
  29.9 19.3 %collective-permute-start.6 = (bf16[2,6,128,128]{3,2,1,0:T(8,128)(2,1)S(1)}, bf16[2,6,128,128]{3,2,1,0:T(8,128)(2,1)S(1)}, u32[]{:S(2)}, u32[]{:S(2)}) collective-permute-start(bf16[2,6,128,128]{3,2,1,0:T(8,128)(2,1)S(1)} %collective-permute-done.4.refs_1_), channel_id=1, source_target_pairs={{4,0},{8,12},{5,1},{9,13},{6,2},{10,14},{7,3},{11,15},{20,16},{24,... | collective-permute-start | bytes 1179656 | tf_op jit(solution)/shard_map/ppermute | solution.py:355
  40.5 17.1 %collective-permute-start.10 = (bf16[2,6,128,128]{3,2,1,0:T(8,128)(2,1)S(1)}, bf16[2,6,128,128]{3,2,1,0:T(8,128)(2,1)S(1)}, u32[]{:S(2)}, u32[]{:S(2)}) collective-permute-start(bf16[2,6,128,128]{3,2,1,0:T(8,128)(2,1)S(1)} %collective-permute-done.9.middle), channel_id=1, source_target_pairs={{4,0},{8,12},{5,1},{9,13},{6,2},{10,14},{7,3},{11,15},{20,16},{24,... | collective-permute-start | bytes 1179656 | tf_op jit(solution)/shard_map/ppermute | solution.py:355
  51.0 6.6 %collective-permute-start.7 = (f32[2,3,64,128]{3,2,1,0:T(8,128)S(1)}, f32[2,3,64,128]{3,2,1,0:T(8,128)S(1)}, u32[]{:S(2)}, u32[]{:S(2)}) collective-permute-start(f32[2,3,64,128]{3,2,1,0:T(8,128)S(1)} %get-tuple-element.19), channel_id=1, source_target_pairs={{0,2},{2,0},{1,3},{3,1},{4,6},{6,4},{5,7},{7,5},{8,10},{10,8},{9,1... | collective-permute-start | bytes 589832 | tf_op jit(solution)/shard_map/ppermute | solution.py:361
  58.7 5.7 %collective-permute-start.11 = (f32[2,3,64,128]{3,2,1,0:T(8,128)S(1)}, f32[2,3,64,128]{3,2,1,0:T(8,128)S(1)}, u32[]{:S(2)}, u32[]{:S(2)}) collective-permute-start(f32[2,3,64,128]{3,2,1,0:T(8,128)S(1)} %get-tuple-element.24), channel_id=1, source_target_pairs={{0,2},{2,0},{1,3},{3,1},{4,6},{6,4},{5,7},{7,5},{8,10},{10,8},{9,1... | collective-permute-start | bytes 589832 | tf_op jit(solution)/shard_map/ppermute | solution.py:361

commit v3 on v2

--- a/solution.py
+++ b/solution.py
@@ -242,8 +242,9 @@
     )(table, dense, acc, *sources)
 
 
-def last_kernel(table, dense, acc, middle, far, keep, send):
-    is_mid = jnp.logical_and(table[3, 0] > 0, table[3, 0] < 3)
+def last_kernel(dense, acc, middle, far, keep, send):
+    z = lax.axis_index("site")
+    is_mid = jnp.logical_and(z > 0, z < 3)
 
     def run(source):
         for c in range(dense.shape[2]):
@@ -259,13 +260,13 @@
         run(far)
 
 
-def last(table, dense, acc, middle, far):
+def last(dense, acc, middle, far):
     _, _, comps, rows, depth = dense.shape
     half = (2, comps, rows // 4, middle.shape[2])
     return pl.pallas_call(
         last_kernel,
         out_shape=(pltpu.VMEM(half, jnp.float32),) * 2,
-        in_specs=[SMEM_SPEC] + [VMEM_SPEC] * 4,
+        in_specs=[VMEM_SPEC] * 4,
         out_specs=(VMEM_SPEC,) * 2,
         compiler_params=pltpu.CompilerParams(vmem_limit_bytes=VMEM_LIMIT),
         cost_estimate=pl.CostEstimate(
@@ -273,7 +274,7 @@
             bytes_accessed=1_000_000,
             transcendentals=0,
         ),
-    )(table, dense, acc, middle, far)
+    )(dense, acc, middle, far)
 
 
 def whole_kernel(f, dense, parts, keep, send, spec, sem):
@@ -309,7 +310,7 @@
     for f in range(FREQS):
         keep, got = refs[2 * f : 2 * f + 2]
         for r in range(2):
-            value[f, r] = (keep[r] + got[r]) * brune[f]
+            value[f, r] = (keep[r] + got[r]) * brune[f, :1]
             copy = pltpu.make_async_copy(value.at[f, r], result.at[f, r], sem.at[f, r])
             copy.start()
             copies.append(copy)
@@ -322,7 +323,7 @@
     return pl.pallas_call(
         finish_kernel,
         out_shape=jax.ShapeDtypeStruct(shape, pieces[0].dtype),
-        in_specs=[SMEM_SPEC] + [VMEM_SPEC] * len(pieces),
+        in_specs=[VMEM_SPEC] * (1 + len(pieces)),
         out_specs=HBM_SPEC,
         scratch_shapes=[
             pltpu.VMEM(shape, pieces[0].dtype),
@@ -350,8 +351,8 @@
     inner = [move(own[f], perm=INNER) for f in range(FREQS)]
     outer = [move(inner[f], perm=OUTER) for f in range(FREQS)]
     ready = after(pairs, dense)
-    middle = [move(after(ready[f], *inner), perm=INNER) for f in range(FREQS)]
     acc = early(dense, own, pairs)
+    middle = [move(after(ready[0], inner[0]), perm=INNER), move(after(ready[1], *inner, acc), perm=INNER)]
     far = [move(after(middle[f], outer[f], acc), perm=OUTER) for f in range(FREQS)]
     first, second = zip(inner, middle, outer, far)
     return acc, first, second
@@ -381,7 +382,7 @@
         pieces = [keep, exchange(send)]
         more = late(1, table, dense, acc, (inner1, outer1))
         far1 = after(far1, pieces[1], more)
-        keep, send = last(table, dense, more, middle1, far1)
+        keep, send = last(dense, more, middle1, far1)
         pieces += [keep, exchange(send)]
     else:
         gathered = lax.all_gather(spectra, "site", axis=4, tiled=True)
@@ -395,7 +396,8 @@
                 both = jnp.concatenate([keep, send], axis=2)
                 keep = lax.psum_scatter(both, "sub", scatter_dimension=2, tiled=True)
                 pieces += [keep, jnp.zeros_like(keep)]
-    result = finish(brune, pieces)
+    rows = jnp.broadcast_to(brune[:, None, None], (FREQS, 8, pieces[0].shape[3]))
+    result = finish(rows, pieces)
     return result.transpose(0, 1, 2, 4, 3)
 
 

time: 66.1 us -> 63.6 us (0.962)
  Pallas kernels: 12.1 us -> 10.5 us
  starting transfers between devices: 14.2 us -> 13.2 us
    ppermute x2, starting transfers between devices: 3.12 us -> 2.13 us  [exchange(): return lax.ppermute(send, 'sub', [(0, 1), (1, 0)])]
  transfers between devices with their start and end apart: 12 -> 12, of which waited for: 6 -> 6; matrix products, arithmetic and copies ran while one was open for 4% -> 4% of each run, Pallas kernels for 15% -> 14%
where the time goes in v3:
time: 63.6 us
  waiting for transfers between devices  36.4 us (57%)
  starting transfers between devices  13.2 us (21%)
  Pallas kernels  10.5 us (17%)
  other arithmetic  1.36 us (2%)
  local copies, waits for them, and re-layouts  1.33 us (2%)
  between operations  0.82 us (1%)
    ppermute x2, waiting for transfers between devices, line_steps(): outer = [move(inner[f], perm=OUTER) for f in range(FREQS)]  12.6 us
    ppermute x2, waiting for transfers between devices, line_steps(): move(after(middle[f], outer[f], acc), perm=OUTER)  10.8 us
    ppermute x1, waiting for transfers between devices, line_steps(): pairs = move(own, perm=PAIRS)  8.96 us
    pallas_call x1, Pallas kernels, prepare(): pl.pallas_call(functools.partial(prepare_kernel, line), out_shape=pltpu.V...  4.26 us
    ppermute x2, waiting for transfers between devices, exchange(): return lax.ppermute(send, 'sub', [(0, 1), (1, 0)])  4.05 us
    pallas_call x2, Pallas kernels, late(): pl.pallas_call(functools.partial(late_kernel, f), out_shape=(half, half)...  3.12 us
    ppermute x2, starting transfers between devices, line_steps(): outer = [move(inner[f], perm=OUTER) for f in range(FREQS)]  2.7 us
    ppermute x1, starting transfers between devices, line_steps(): pairs = move(own, perm=PAIRS)  2.57 us
  transfers between devices with their start and end apart: 12, of which 6 were waited for; matrix products, arithmetic and copies ran while one was open for 4% of the time, Pallas kernels for 14%

profile of v3, /device:TPU:0, one launch (start us, length us, event | category | flops | bytes accessed | tf_op | source)
XLA Modules:
  0.0 63.6 jit_solution(4791150261544389292)
XLA Ops:
  0.0 0.5 collective-permute-start
  0.5 2.6 %collective-permute-start.1 = (bf16[2,2,6,128,128]{4,3,2,1,0:T(8,128)(2,1)}, bf16[2,2,6,128,128]{4,3,2,1,0:T(8,128)(2,1)S(1)}, u32[]{:S(2)}, u32[]{:S(2)}) collective-permute-start(bf16[2,2,6,128,128]{4,3,2,1,0:T(8,128)(2,1)} %bitcast.23), channel_id=1, source_target_pairs={{0,4},{4,0},{8,12},{12,8},{1,5},{5,1},{9,13},{13,9},{2,6},{6,2},{1... | collective-permute-start | bytes 2359304 | tf_op jit(solution)/shard_map/ppermute | solution.py:350
  3.0 1.2 %slice_bitcast_fusion = (bf16[2,6,128,128]{3,2,1,0:T(8,128)(2,1)S(1)}, bf16[2,6,128,128]{3,2,1,0:T(8,128)(2,1)S(1)}) fusion(bf16[2,2,6,128,128]{4,3,2,1,0:T(8,128)(2,1)} %bitcast.24), kind=kLoop, calls=%fused_computation | loop fusion | bytes 1572864 | tf_op jit(solution)/shard_map/squeeze | solution.py:351
  4.2 0.7 %collective-permute-start.2 = (bf16[2,6,128,128]{3,2,1,0:T(8,128)(2,1)S(1)}, bf16[2,6,128,128]{3,2,1,0:T(8,128)(2,1)S(1)}, u32[]{:S(2)}, u32[]{:S(2)}) collective-permute-start(bf16[2,6,128,128]{3,2,1,0:T(8,128)(2,1)S(1)} %get-tuple-element.28), channel_id=1, source_target_pairs={{4,8},{8,4},{5,9},{9,5},{6,10},{10,6},{7,11},{11,7},{20,24},{24,20... | collective-permute-start | bytes 1179656 | tf_op jit(solution)/shard_map/ppermute | solution.py:351
  4.9 0.7 %collective-permute-start.7 = (bf16[2,6,128,128]{3,2,1,0:T(8,128)(2,1)S(1)}, bf16[2,6,128,128]{3,2,1,0:T(8,128)(2,1)S(1)}, u32[]{:S(2)}, u32[]{:S(2)}) collective-permute-start(bf16[2,6,128,128]{3,2,1,0:T(8,128)(2,1)S(1)} %get-tuple-element.27), channel_id=1, source_target_pairs={{4,8},{8,4},{5,9},{9,5},{6,10},{10,6},{7,11},{11,7},{20,24},{24,20... | collective-permute-start | bytes 1179656 | tf_op jit(solution)/shard_map/ppermute | solution.py:351
  5.6 0.1 pad_add_fusion.1
  5.7 1.3 %pad_add_fusion.table = s32[4,16]{1,0:T(4,128)} fusion(s32[1,16]{1,0:T(1,128)S(1)} %pad_bitcast_fusion, s32[1,16]{1,0:T(1,128)} %bitcast.28, s32[1,16]{1,0:T(1,128)} %bitcast.29, s32[1,16]{1,0:T(1,128)} %bitcast.30), kind=kLoop, calls=%fused_computation.4 | loop fusion | flops 192 | bytes 512 | tf_op jit(solution)/shard_map/stack | solution.py:373
  7.0 0.0 copy-start
  7.0 0.0 collective-permute-done.2.refs_0_
  7.0 1.4 %collective-permute-start.4 = (bf16[2,6,128,128]{3,2,1,0:T(8,128)(2,1)S(1)}, bf16[2,6,128,128]{3,2,1,0:T(8,128)(2,1)S(1)}, u32[]{:S(2)}, u32[]{:S(2)}) collective-permute-start(bf16[2,6,128,128]{3,2,1,0:T(8,128)(2,1)S(1)} %collective-permute-done.2.refs_0_), channel_id=1, source_target_pairs={{4,0},{8,12},{5,1},{9,13},{6,2},{10,14},{7,3},{11,15},{20,16},{24,... | collective-permute-start | bytes 1179656 | tf_op jit(solution)/shard_map/ppermute | solution.py:352
  8.4 0.0 collective-permute-done.other
  8.4 4.3 %shard_map.64.dense = bf16[2,4,3,256,768]{4,3,2,1,0:T(8,128)(2,1)S(1)} custom-call(s32[4,16]{1,0:T(4,128)} %pad_add_fusion.table, bf16[16,2,3,6,32,128]{5,4,3,2,1,0:T(8,128)(2,1)} %bitcast.27, bf16[16,2,3,6,32,128]{5,4,3,2,1,0:T(8,128)(2,1)} %collective-permute-done.other), custom_call_target="tpu_custom_call" | custom-call | bytes 12000000 | tf_op jit(solution)/shard_map/pallas_call | solution.py:97
  12.7 9.0 %collective-permute-done.1.pairs = bf16[2,2,6,128,128]{4,3,2,1,0:T(8,128)(2,1)S(1)} collective-permute-done((bf16[2,2,6,128,128]{4,3,2,1,0:T(8,128)(2,1)}, bf16[2,2,6,128,128]{4,3,2,1,0:T(8,128)(2,1)S(1)}, u32[]{:S(2)}, u32[]{:S(2)}) %collective-permute-start.1) | collective-permute-done | bytes 786464 | tf_op jit(solution)/shard_map/ppermute | solution.py:350
  21.6 0.1 slice_bitcast_fusion.2
  21.7 0.0 copy-start.1
  21.7 0.7 %collective-permute-start.3 = (bf16[2,6,128,128]{3,2,1,0:T(8,128)(2,1)S(1)}, bf16[2,6,128,128]{3,2,1,0:T(8,128)(2,1)S(1)}, u32[]{:S(2)}, u32[]{:S(2)}) collective-permute-start(bf16[2,6,128,128]{3,2,1,0:T(8,128)(2,1)S(1)} %get-tuple-element.16), channel_id=1, source_target_pairs={{4,8},{8,4},{5,9},{9,5},{6,10},{10,6},{7,11},{11,7},{20,24},{24,20... | collective-permute-start | bytes 1179656 | tf_op jit(solution)/shard_map/ppermute | solution.py:355
  22.4 0.0 collective-permute-done.7.refs_0_
  22.4 1.3 %collective-permute-start.8 = (bf16[2,6,128,128]{3,2,1,0:T(8,128)(2,1)S(1)}, bf16[2,6,128,128]{3,2,1,0:T(8,128)(2,1)S(1)}, u32[]{:S(2)}, u32[]{:S(2)}) collective-permute-start(bf16[2,6,128,128]{3,2,1,0:T(8,128)(2,1)S(1)} %collective-permute-done.7.refs_0_), channel_id=1, source_target_pairs={{4,0},{8,12},{5,1},{9,13},{6,2},{10,14},{7,3},{11,15},{20,16},{24,... | collective-permute-start | bytes 1179656 | tf_op jit(solution)/shard_map/ppermute | solution.py:352
  23.7 0.0 copy-done
  23.7 1.8 %shard_map.65.acc = f32[2,2,3,128,128]{4,3,2,1,0:T(8,128)S(1)} custom-call(bf16[2,4,3,256,768]{4,3,2,1,0:T(8,128)(2,1)S(1)} %shard_map.64.dense, bf16[2,2,6,128,128]{4,3,2,1,0:T(8,128)(2,1)S(1)} %bitcast.25, bf16[2,2,6,128,128]{4,3,2,1,0:T(8,128)(2,1)S(1)} %collective-permute-done.1.pairs), custom_call_target="tpu_custom_call" | custom-call | flops 1207959552 | bytes 4000000 | tf_op jit(solution)/shard_map/pallas_call | solution.py:162
  25.5 0.7 %collective-permute-start.9 = (bf16[2,6,128,128]{3,2,1,0:T(8,128)(2,1)S(1)}, bf16[2,6,128,128]{3,2,1,0:T(8,128)(2,1)S(1)}, u32[]{:S(2)}, u32[]{:S(2)}) collective-permute-start(bf16[2,6,128,128]{3,2,1,0:T(8,128)(2,1)S(1)} %get-tuple-element.20), channel_id=1, source_target_pairs={{4,8},{8,4},{5,9},{9,5},{6,10},{10,6},{7,11},{11,7},{20,24},{24,20... | collective-permute-start | bytes 1179656 | tf_op jit(solution)/shard_map/ppermute | solution.py:355
  26.2 3.7 %collective-permute-done.4.refs_2_ = bf16[2,6,128,128]{3,2,1,0:T(8,128)(2,1)S(1)} collective-permute-done((bf16[2,6,128,128]{3,2,1,0:T(8,128)(2,1)S(1)}, bf16[2,6,128,128]{3,2,1,0:T(8,128)(2,1)S(1)}, u32[]{:S(2)}, u32[]{:S(2)}) %collective-permute-start.4) | collective-permute-done | bytes 393248 | tf_op jit(solution)/shard_map/ppermute | solution.py:352
  29.9 0.0 collective-permute-done.3.refs_1_
  29.9 1.3 %collective-permute-start.5 = (bf16[2,6,128,128]{3,2,1,0:T(8,128)(2,1)S(1)}, bf16[2,6,128,128]{3,2,1,0:T(8,128)(2,1)S(1)}, u32[]{:S(2)}, u32[]{:S(2)}) collective-permute-start(bf16[2,6,128,128]{3,2,1,0:T(8,128)(2,1)S(1)} %collective-permute-done.3.refs_1_), channel_id=1, source_target_pairs={{4,0},{8,12},{5,1},{9,13},{6,2},{10,14},{7,3},{11,15},{20,16},{24,... | collective-permute-start | bytes 1179656 | tf_op jit(solution)/shard_map/ppermute | solution.py:356
  31.2 8.9 %collective-permute-done.8.refs_1_ = bf16[2,6,128,128]{3,2,1,0:T(8,128)(2,1)S(1)} collective-permute-done((bf16[2,6,128,128]{3,2,1,0:T(8,128)(2,1)S(1)}, bf16[2,6,128,128]{3,2,1,0:T(8,128)(2,1)S(1)}, u32[]{:S(2)}, u32[]{:S(2)}) %collective-permute-start.8) | collective-permute-done | bytes 393248 | tf_op jit(solution)/shard_map/ppermute | solution.py:352
  40.1 0.0 collective-permute-done.9.middle
  40.1 1.3 %collective-permute-start.10 = (bf16[2,6,128,128]{3,2,1,0:T(8,128)(2,1)S(1)}, bf16[2,6,128,128]{3,2,1,0:T(8,128)(2,1)S(1)}, u32[]{:S(2)}, u32[]{:S(2)}) collective-permute-start(bf16[2,6,128,128]{3,2,1,0:T(8,128)(2,1)S(1)} %collective-permute-done.9.middle), channel_id=1, source_target_pairs={{4,0},{8,12},{5,1},{9,13},{6,2},{10,14},{7,3},{11,15},{20,16},{24,... | collective-permute-start | bytes 1179656 | tf_op jit(solution)/shard_map/ppermute | solution.py:356
  41.4 7.1 %collective-permute-done.5.refs_3_ = bf16[2,6,128,128]{3,2,1,0:T(8,128)(2,1)S(1)} collective-permute-done((bf16[2,6,128,128]{3,2,1,0:T(8,128)(2,1)S(1)}, bf16[2,6,128,128]{3,2,1,0:T(8,128)(2,1)S(1)}, u32[]{:S(2)}, u32[]{:S(2)}) %collective-permute-start.5) | collective-permute-done | bytes 393248 | tf_op jit(solution)/shard_map/ppermute | solution.py:356
  48.5 0.0 copy-done.1
  48.5 1.8 %shard_map.66 = (f32[2,3,64,128]{3,2,1,0:T(8,128)S(1)}, f32[2,3,64,128]{3,2,1,0:T(8,128)S(1)}) custom-call(s32[4,16]{1,0:T(4,128)S(1)} %copy-done.1, bf16[2,4,3,256,768]{4,3,2,1,0:T(8,128)(2,1)S(1)} %shard_map.64.dense, f32[2,2,3,128,128]{4,3,2,1,0:T(8,128)S(1)} %shard_map.65.acc, bf16[2,6,128,128]{3,2,1,0:T(8,128)(2,1)S(1)} %collective-permute-done.2.refs_0_, ...), custom_call_target="tpu_custom_call" | custom-call | flops 603979776 | bytes 1600000 | tf_op jit(solution)/shard_map/pallas_call | solution.py:227
  50.4 1.1 %collective-permute-start.6 = (f32[2,3,64,128]{3,2,1,0:T(8,128)S(1)}, f32[2,3,64,128]{3,2,1,0:T(8,128)S(1)}, u32[]{:S(2)}, u32[]{:S(2)}) collective-permute-start(f32[2,3,64,128]{3,2,1,0:T(8,128)S(1)} %get-tuple-element.19), channel_id=1, source_target_pairs={{0,2},{2,0},{1,3},{3,1},{4,6},{6,4},{5,7},{7,5},{8,10},{10,8},{9,1... | collective-permute-start | bytes 589832 | tf_op jit(solution)/shard_map/ppermute | solution.py:362
  51.5 1.3 %shard_map.67.acc = f32[2,3,128,128]{3,2,1,0:T(8,128)S(1)} custom-call(s32[4,16]{1,0:T(4,128)S(1)} %copy-done.1, bf16[2,4,3,256,768]{4,3,2,1,0:T(8,128)(2,1)S(1)} %shard_map.64.dense, f32[2,2,3,128,128]{4,3,2,1,0:T(8,128)S(1)} %shard_map.65.acc, bf16[2,6,128,128]{3,2,1,0:T(8,128)(2,1)S(1)} %collective-permute-done.7.refs_0_, ...), custom_call_target="tpu_custom_call" | custom-call | flops 301989888 | bytes 800000 | tf_op jit(solution)/shard_map/pallas_call | solution.py:227
  52.8 3.7 %collective-permute-done.10.far = bf16[2,6,128,128]{3,2,1,0:T(8,128)(2,1)S(1)} collective-permute-done((bf16[2,6,128,128]{3,2,1,0:T(8,128)(2,1)S(1)}, bf16[2,6,128,128]{3,2,1,0:T(8,128)(2,1)S(1)}, u32[]{:S(2)}, u32[]{:S(2)}) %collective-permute-start.10) | collective-permute-done | bytes 393248 | tf_op jit(solution)/shard_map/ppermute | solution.py:356
  56.5 0.0 collective-permute-done.6.refs_1_
  56.5 0.5 shard_map.68
  57.0 1.0 %collective-permute-start.11 = (f32[2,3,64,128]{3,2,1,0:T(8,128)S(1)}, f32[2,3,64,128]{3,2,1,0:T(8,128)S(1)}, u32[]{:S(2)}, u32[]{:S(2)}) collective-permute-start(f32[2,3,64,128]{3,2,1,0:T(8,128)S(1)} %get-tuple-element.24), channel_id=1, source_target_pairs={{0,2},{2,0},{1,3},{3,1},{4,6},{6,4},{5,7},{7,5},{8,10},{10,8},{9,1... | collective-permute-start | bytes 589832 | tf_op jit(solution)/shard_map/ppermute | solution.py:362
  58.7 4.0 %collective-permute-done.11.refs_3_ = f32[2,3,64,128]{3,2,1,0:T(8,128)S(1)} collective-permute-done((f32[2,3,64,128]{3,2,1,0:T(8,128)S(1)}, f32[2,3,64,128]{3,2,1,0:T(8,128)S(1)}, u32[]{:S(2)}, u32[]{:S(2)}) %collective-permute-start.11) | collective-permute-done | bytes 196640 | tf_op jit(solution)/shard_map/ppermute | solution.py:362
  62.7 0.1 broadcast_in_dim.2.brune
  62.8 0.8 %shard_map.69 = f32[2,2,3,64,128]{4,3,2,1,0:T(8,128)} custom-call(f32[2,8,128]{2,1,0:T(8,128)S(1)} %broadcast_in_dim.2.brune, f32[2,3,64,128]{3,2,1,0:T(8,128)S(1)} %get-tuple-element.18.refs_0_, f32[2,3,64,128]{3,2,1,0:T(8,128)S(1)} %collective-permute-done.6.refs_1_, f32[2,3,64,128]{3,2,1,0:T(8,128)S(1)} %get-tuple-element.23.refs_2_, ...), custom_call_target="tpu_custom_call" | custom-call | flops 400000 | bytes 600000 | tf_op jit(solution)/shard_map/pallas_call | solution.py:323
  (2 shorter events, 0.0 us)
Async XLA Ops:
  0.0 8.4 %collective-permute-start = (bf16[16,2,3,6,32,128]{5,4,3,2,1,0:T(8,128)(2,1)}, bf16[16,2,3,6,32,128]{5,4,3,2,1,0:T(8,128)(2,1)}, u32[]{:S(2)}, u32[]{:S(2)}) collective-permute-start(bf16[16,2,3,6,32,128]{5,4,3,2,1,0:T(8,128)(2,1)} %bitcast.26), channel_id=1, source_target_pairs={{0,1},{1,0},{2,3},{3,2},{4,5},{5,4},{6,7},{7,6},{8,9},{9,8},{10,11... | collective-permute-start | bytes 14155784 | tf_op jit(solution)/shard_map/ppermute | solution.py:376
  0.5 21.2 %collective-permute-start.1 = (bf16[2,2,6,128,128]{4,3,2,1,0:T(8,128)(2,1)}, bf16[2,2,6,128,128]{4,3,2,1,0:T(8,128)(2,1)S(1)}, u32[]{:S(2)}, u32[]{:S(2)}) collective-permute-start(bf16[2,2,6,128,128]{4,3,2,1,0:T(8,128)(2,1)} %bitcast.23), channel_id=1, source_target_pairs={{0,4},{4,0},{8,12},{12,8},{1,5},{5,1},{9,13},{13,9},{2,6},{6,2},{1... | collective-permute-start | bytes 2359304 | tf_op jit(solution)/shard_map/ppermute | solution.py:350
  4.2 2.8 %collective-permute-start.2 = (bf16[2,6,128,128]{3,2,1,0:T(8,128)(2,1)S(1)}, bf16[2,6,128,128]{3,2,1,0:T(8,128)(2,1)S(1)}, u32[]{:S(2)}, u32[]{:S(2)}) collective-permute-start(bf16[2,6,128,128]{3,2,1,0:T(8,128)(2,1)S(1)} %get-tuple-element.28), channel_id=1, source_target_pairs={{4,8},{8,4},{5,9},{9,5},{6,10},{10,6},{7,11},{11,7},{20,24},{24,20... | collective-permute-start | bytes 1179656 | tf_op jit(solution)/shard_map/ppermute | solution.py:351
  4.9 17.5 %collective-permute-start.7 = (bf16[2,6,128,128]{3,2,1,0:T(8,128)(2,1)S(1)}, bf16[2,6,128,128]{3,2,1,0:T(8,128)(2,1)S(1)}, u32[]{:S(2)}, u32[]{:S(2)}) collective-permute-start(bf16[2,6,128,128]{3,2,1,0:T(8,128)(2,1)S(1)} %get-tuple-element.27), channel_id=1, source_target_pairs={{4,8},{8,4},{5,9},{9,5},{6,10},{10,6},{7,11},{11,7},{20,24},{24,20... | collective-permute-start | bytes 1179656 | tf_op jit(solution)/shard_map/ppermute | solution.py:351
  7.0 16.8 %copy-start = (bf16[2,2,128,6,128]{4,2,3,1,0:T(8,128)(2,1)S(1)}, bf16[2,2,128,6,128]{4,2,3,1,0:T(8,128)(2,1)}, u32[]{:S(2)}) copy-start(bf16[2,2,128,6,128]{4,2,3,1,0:T(8,128)(2,1)} %param.7) | copy-start | bytes 2359300
  7.0 22.9 %collective-permute-start.4 = (bf16[2,6,128,128]{3,2,1,0:T(8,128)(2,1)S(1)}, bf16[2,6,128,128]{3,2,1,0:T(8,128)(2,1)S(1)}, u32[]{:S(2)}, u32[]{:S(2)}) collective-permute-start(bf16[2,6,128,128]{3,2,1,0:T(8,128)(2,1)S(1)} %collective-permute-done.2.refs_0_), channel_id=1, source_target_pairs={{4,0},{8,12},{5,1},{9,13},{6,2},{10,14},{7,3},{11,15},{20,16},{24,... | collective-permute-start | bytes 1179656 | tf_op jit(solution)/shard_map/ppermute | solution.py:352
  21.7 26.8 %copy-start.1 = (s32[4,16]{1,0:T(4,128)S(1)}, s32[4,16]{1,0:T(4,128)}, u32[]{:S(2)}) copy-start(s32[4,16]{1,0:T(4,128)} %pad_add_fusion.table) | copy-start | bytes 772
  21.7 8.2 %collective-permute-start.3 = (bf16[2,6,128,128]{3,2,1,0:T(8,128)(2,1)S(1)}, bf16[2,6,128,128]{3,2,1,0:T(8,128)(2,1)S(1)}, u32[]{:S(2)}, u32[]{:S(2)}) collective-permute-start(bf16[2,6,128,128]{3,2,1,0:T(8,128)(2,1)S(1)} %get-tuple-element.16), channel_id=1, source_target_pairs={{4,8},{8,4},{5,9},{9,5},{6,10},{10,6},{7,11},{11,7},{20,24},{24,20... | collective-permute-start | bytes 1179656 | tf_op jit(solution)/shard_map/ppermute | solution.py:355
  22.4 17.7 %collective-permute-start.8 = (bf16[2,6,128,128]{3,2,1,0:T(8,128)(2,1)S(1)}, bf16[2,6,128,128]{3,2,1,0:T(8,128)(2,1)S(1)}, u32[]{:S(2)}, u32[]{:S(2)}) collective-permute-start(bf16[2,6,128,128]{3,2,1,0:T(8,128)(2,1)S(1)} %collective-permute-done.7.refs_0_), channel_id=1, source_target_pairs={{4,0},{8,12},{5,1},{9,13},{6,2},{10,14},{7,3},{11,15},{20,16},{24,... | collective-permute-start | bytes 1179656 | tf_op jit(solution)/shard_map/ppermute | solution.py:352
  25.5 14.6 %collective-permute-start.9 = (bf16[2,6,128,128]{3,2,1,0:T(8,128)(2,1)S(1)}, bf16[2,6,128,128]{3,2,1,0:T(8,128)(2,1)S(1)}, u32[]{:S(2)}, u32[]{:S(2)}) collective-permute-start(bf16[2,6,128,128]{3,2,1,0:T(8,128)(2,1)S(1)} %get-tuple-element.20), channel_id=1, source_target_pairs={{4,8},{8,4},{5,9},{9,5},{6,10},{10,6},{7,11},{11,7},{20,24},{24,20... | collective-permute-start | bytes 1179656 | tf_op jit(solution)/shard_map/ppermute | solution.py:355
  29.9 18.7 %collective-permute-start.5 = (bf16[2,6,128,128]{3,2,1,0:T(8,128)(2,1)S(1)}, bf16[2,6,128,128]{3,2,1,0:T(8,128)(2,1)S(1)}, u32[]{:S(2)}, u32[]{:S(2)}) collective-permute-start(bf16[2,6,128,128]{3,2,1,0:T(8,128)(2,1)S(1)} %collective-permute-done.3.refs_1_), channel_id=1, source_target_pairs={{4,0},{8,12},{5,1},{9,13},{6,2},{10,14},{7,3},{11,15},{20,16},{24,... | collective-permute-start | bytes 1179656 | tf_op jit(solution)/shard_map/ppermute | solution.py:356
  40.1 16.4 %collective-permute-start.10 = (bf16[2,6,128,128]{3,2,1,0:T(8,128)(2,1)S(1)}, bf16[2,6,128,128]{3,2,1,0:T(8,128)(2,1)S(1)}, u32[]{:S(2)}, u32[]{:S(2)}) collective-permute-start(bf16[2,6,128,128]{3,2,1,0:T(8,128)(2,1)S(1)} %collective-permute-done.9.middle), channel_id=1, source_target_pairs={{4,0},{8,12},{5,1},{9,13},{6,2},{10,14},{7,3},{11,15},{20,16},{24,... | collective-permute-start | bytes 1179656 | tf_op jit(solution)/shard_map/ppermute | solution.py:356
  50.4 6.1 %collective-permute-start.6 = (f32[2,3,64,128]{3,2,1,0:T(8,128)S(1)}, f32[2,3,64,128]{3,2,1,0:T(8,128)S(1)}, u32[]{:S(2)}, u32[]{:S(2)}) collective-permute-start(f32[2,3,64,128]{3,2,1,0:T(8,128)S(1)} %get-tuple-element.19), channel_id=1, source_target_pairs={{0,2},{2,0},{1,3},{3,1},{4,6},{6,4},{5,7},{7,5},{8,10},{10,8},{9,1... | collective-permute-start | bytes 589832 | tf_op jit(solution)/shard_map/ppermute | solution.py:362
  57.0 5.7 %collective-permute-start.11 = (f32[2,3,64,128]{3,2,1,0:T(8,128)S(1)}, f32[2,3,64,128]{3,2,1,0:T(8,128)S(1)}, u32[]{:S(2)}, u32[]{:S(2)}) collective-permute-start(f32[2,3,64,128]{3,2,1,0:T(8,128)S(1)} %get-tuple-element.24), channel_id=1, source_target_pairs={{0,2},{2,0},{1,3},{3,1},{4,6},{6,4},{5,7},{7,5},{8,10},{10,8},{9,1... | collective-permute-start | bytes 589832 | tf_op jit(solution)/shard_map/ppermute | solution.py:362

commit v4 on v3

--- a/solution.py
+++ b/solution.py
@@ -182,6 +182,23 @@
     return pair if sums is None else [a + b for a, b in zip(sums, pair)]
 
 
+def swap_lanes(value):
+    return pltpu.roll(value, value.shape[1] // 2, axis=1)
+
+
+def low_lanes(value):
+    lane = lax.broadcasted_iota(jnp.int32, value.shape, 1)
+    return lane < value.shape[1] // 2
+
+
+def repack(first, second):
+    low = low_lanes(first)
+    return (
+        jnp.where(low, first, swap_lanes(second)),
+        jnp.where(low, swap_lanes(first), second),
+    )
+
+
 def split_halves(sums, c, keep, send):
     half = keep.shape[2]
     for r, value in enumerate(sums):
@@ -189,82 +206,61 @@
         send[r, c] = value[half:]
 
 
-def late_kernel(f, table, dense, acc, *refs):
-    places = 2 - f
-    sources = refs[: 2 * places]
-    *outs, spec, sem = refs[2 * places :]
-    is_mid = jnp.logical_and(table[3, 0] > 0, table[3, 0] < 3)
+def by_position(run, middle, end):
+    z = lax.axis_index("site")
+    is_mid = jnp.logical_and(z > 0, z < 3)
 
     @pl.when(is_mid)
     def _():
-        for n, source in enumerate(sources[:places]):
-            pltpu.make_async_copy(source, spec.at[n], sem.at[n]).start()
+        run(middle)
 
     @pl.when(jnp.logical_not(is_mid))
     def _():
-        for n, source in enumerate(sources[places:]):
-            pltpu.make_async_copy(source, spec.at[n], sem.at[n]).start()
-
-    for n in range(places):
-        pltpu.make_async_copy(sources[n], spec.at[n], sem.at[n]).wait()
-    for c in range(dense.shape[2]):
-        sums = [acc[f, r, c] for r in range(2)]
-        for n in range(places):
-            sums = place_sums(dense, f, 2 + n, c, spec[n], sums)
-        if f == 0:
-            split_halves(sums, c, *outs)
-        else:
-            for r, value in enumerate(sums):
-                outs[0][r, c] = value
-
-
-def late(f, table, dense, acc, sources):
+        run(end)
+
+
+def third_kernel(f, dense, acc, inner, outer, total):
+    def run(source):
+        for c in range(dense.shape[2]):
+            sums = [acc[f, r, c] for r in range(2)]
+            sums = place_sums(dense, f, 2, c, source[...], sums)
+            for n, value in enumerate(sums if f == 0 else repack(*sums)):
+                total[n, c] = value
+
+    by_position(run, inner, outer)
+
+
+def third(f, dense, acc, inner, outer):
     _, _, comps, rows, depth = dense.shape
-    shape = sources[0].shape
-    places = len(sources) // 2
-    half = pltpu.VMEM((2, comps, rows // 4, shape[2]), jnp.float32)
-    full = pltpu.VMEM((2, comps, rows // 2, shape[2]), jnp.float32)
-    return pl.pallas_call(
-        functools.partial(late_kernel, f),
-        out_shape=(half, half) if f == 0 else full,
-        in_specs=[SMEM_SPEC, VMEM_SPEC, VMEM_SPEC] + [HBM_SPEC] * len(sources),
-        out_specs=(VMEM_SPEC, VMEM_SPEC) if f == 0 else VMEM_SPEC,
-        scratch_shapes=[
-            pltpu.VMEM((places,) + shape, dense.dtype),
-            pltpu.SemaphoreType.DMA((places,)),
-        ],
-        compiler_params=pltpu.CompilerParams(vmem_limit_bytes=VMEM_LIMIT),
-        cost_estimate=pl.CostEstimate(
-            flops=2 * places * comps * rows * 2 * shape[2] * depth,
-            bytes_accessed=800_000 * places,
+    variants = inner.shape[2]
+    return pl.pallas_call(
+        functools.partial(third_kernel, f),
+        out_shape=pltpu.VMEM((2, comps, rows // 2, variants), jnp.float32),
+        in_specs=[VMEM_SPEC] * 4,
+        out_specs=VMEM_SPEC,
+        compiler_params=pltpu.CompilerParams(vmem_limit_bytes=VMEM_LIMIT),
+        cost_estimate=pl.CostEstimate(
+            flops=2 * comps * rows * 2 * variants * depth,
+            bytes_accessed=1_000_000,
             transcendentals=0,
         ),
-    )(table, dense, acc, *sources)
-
-
-def last_kernel(dense, acc, middle, far, keep, send):
-    z = lax.axis_index("site")
-    is_mid = jnp.logical_and(z > 0, z < 3)
-
+    )(dense, acc, inner, outer)
+
+
+def fourth_kernel(dense, acc, middle, far, keep, send):
     def run(source):
         for c in range(dense.shape[2]):
             sums = [acc[r, c] for r in range(2)]
-            split_halves(place_sums(dense, 1, 3, c, source[...], sums), c, keep, send)
-
-    @pl.when(is_mid)
-    def _():
-        run(middle)
-
-    @pl.when(jnp.logical_not(is_mid))
-    def _():
-        run(far)
-
-
-def last(dense, acc, middle, far):
+            split_halves(place_sums(dense, 0, 3, c, source[...], sums), c, keep, send)
+
+    by_position(run, middle, far)
+
+
+def fourth(dense, acc, middle, far):
     _, _, comps, rows, depth = dense.shape
     half = (2, comps, rows // 4, middle.shape[2])
     return pl.pallas_call(
-        last_kernel,
+        fourth_kernel,
         out_shape=(pltpu.VMEM(half, jnp.float32),) * 2,
         in_specs=[VMEM_SPEC] * 4,
         out_specs=(VMEM_SPEC,) * 2,
@@ -272,6 +268,52 @@
         cost_estimate=pl.CostEstimate(
             flops=2 * comps * rows * 2 * middle.shape[2] * depth,
             bytes_accessed=1_000_000,
+            transcendentals=0,
+        ),
+    )(dense, acc, middle, far)
+
+
+def last_kernel(h, dense, acc, middle, far, keep, send):
+    moments, width, columns = far.shape[1:]
+    half = keep.shape[1]
+
+    def run(source):
+        at = h * width if source is middle else 0
+        rhs = jnp.concatenate(
+            [
+                source[:, m, at : at + width].reshape(2 * width, columns)
+                for m in range(moments)
+            ],
+            axis=1,
+        )
+        for c in range(dense.shape[2]):
+            total = lax.dot_general(
+                dense[1, 3, c],
+                rhs,
+                (((1,), (1,)), ((), ())),
+                preferred_element_type=jnp.float32,
+            )
+            crossed = swap_lanes(total[2 * half :])
+            crossed = jnp.where(low_lanes(crossed), -crossed, crossed)
+            value = acc[h, c] + (total[: 2 * half] + crossed)
+            keep[c] = value[:half]
+            send[c] = value[half:]
+
+    by_position(run, middle, far)
+
+
+def last(h, dense, acc, middle, far):
+    _, _, comps, rows, depth = dense.shape
+    half = (comps, rows // 4, 2 * far.shape[2])
+    return pl.pallas_call(
+        functools.partial(last_kernel, h),
+        out_shape=(pltpu.VMEM(half, jnp.float32),) * 2,
+        in_specs=[VMEM_SPEC] * 4,
+        out_specs=(VMEM_SPEC,) * 2,
+        compiler_params=pltpu.CompilerParams(vmem_limit_bytes=VMEM_LIMIT),
+        cost_estimate=pl.CostEstimate(
+            flops=2 * comps * rows * half[2] * depth,
+            bytes_accessed=500_000,
             transcendentals=0,
         ),
     )(dense, acc, middle, far)
@@ -336,6 +378,71 @@
     )(brune, *pieces)
 
 
+def finish_first_kernel(brune, keep, got, keep_a, got_a, result, part, value, sem):
+    copies = []
+    for r in range(2):
+        value[r] = (keep[r] + got[r]) * brune[0, :1]
+        copies.append(
+            pltpu.make_async_copy(value.at[r], result.at[0, r], sem.at[r])
+        )
+        copies[r].start()
+    part[...] = (keep_a[...] + got_a[...]) * brune[1, :1]
+    for copy in copies:
+        copy.wait()
+
+
+def finish_first(brune, keep, got, keep_a, got_a):
+    return pl.pallas_call(
+        finish_first_kernel,
+        out_shape=(
+            jax.ShapeDtypeStruct((FREQS,) + keep.shape, keep.dtype),
+            pltpu.VMEM(keep_a.shape, keep.dtype),
+        ),
+        in_specs=[VMEM_SPEC] * 5,
+        out_specs=(HBM_SPEC, VMEM_SPEC),
+        scratch_shapes=[
+            pltpu.VMEM(keep.shape, keep.dtype),
+            pltpu.SemaphoreType.DMA((2,)),
+        ],
+        compiler_params=pltpu.CompilerParams(vmem_limit_bytes=VMEM_LIMIT),
+        cost_estimate=pl.CostEstimate(
+            flops=400_000, bytes_accessed=8_000_000, transcendentals=0
+        ),
+    )(brune, keep, got, keep_a, got_a)
+
+
+def finish_last_kernel(brune, part, keep_b, got_b, _, result, value, sem):
+    copies = []
+    for r in range(2):
+        for c in range(part.shape[0]):
+            second = (keep_b[c] + got_b[c]) * brune[1, :1]
+            value[r, c] = repack(part[c], second)[r]
+        copies.append(
+            pltpu.make_async_copy(value.at[r], result.at[1, r], sem.at[r])
+        )
+        copies[r].start()
+    for copy in copies:
+        copy.wait()
+
+
+def finish_last(brune, part, keep_b, got_b, result):
+    return pl.pallas_call(
+        finish_last_kernel,
+        out_shape=jax.ShapeDtypeStruct(result.shape, result.dtype),
+        in_specs=[VMEM_SPEC] * 4 + [HBM_SPEC],
+        out_specs=HBM_SPEC,
+        scratch_shapes=[
+            pltpu.VMEM(result.shape[1:], result.dtype),
+            pltpu.SemaphoreType.DMA((2,)),
+        ],
+        input_output_aliases={4: 0},
+        compiler_params=pltpu.CompilerParams(vmem_limit_bytes=VMEM_LIMIT),
+        cost_estimate=pl.CostEstimate(
+            flops=400_000, bytes_accessed=600_000, transcendentals=0
+        ),
+    )(brune, part, keep_b, got_b, result)
+
+
 def after(value, *others):
     return lax.optimization_barrier((value, *others))[0]
 
@@ -345,17 +452,25 @@
 OUTER = [(1, 0), (2, 3)]
 
 
-def line_steps(own, dense):
+def line_steps(own, dense, table):
     move = functools.partial(lax.ppermute, axis_name="site")
     pairs = move(own, perm=PAIRS)
-    inner = [move(own[f], perm=INNER) for f in range(FREQS)]
+    inner = [move(own[0], perm=INNER), move(after(own, table)[1], perm=INNER)]
     outer = [move(inner[f], perm=OUTER) for f in range(FREQS)]
     ready = after(pairs, dense)
     acc = early(dense, own, pairs)
-    middle = [move(after(ready[0], inner[0]), perm=INNER), move(after(ready[1], *inner, acc), perm=INNER)]
-    far = [move(after(middle[f], outer[f], acc), perm=OUTER) for f in range(FREQS)]
-    first, second = zip(inner, middle, outer, far)
-    return acc, first, second
+    middle = [
+        move(after(ready[0], inner[0]), perm=INNER),
+        move(after(ready[1], *inner, acc), perm=INNER),
+    ]
+    sums = [third(f, dense, acc, inner[f], outer[f]) for f in range(FREQS)]
+    far0 = move(after(middle[0], sums[0]), perm=OUTER)
+    width = own.shape[3] // 2
+    handed = after(middle[1], sums[1])
+    far1 = [
+        move(handed[:, :, h * width : (h + 1) * width], perm=OUTER) for h in range(2)
+    ]
+    return sums, middle, far0, far1
 
 
 def exchange(send):
@@ -373,17 +488,20 @@
     table = jnp.stack([pair_site[0, 0], pair_block[0, 0], pair_count[0, 0], ids])
     freq_index = (offset[0] + jnp.arange(FREQS, dtype=jnp.int32)).astype(jnp.float32)
     brune = 1.0 / (1.0 + (freq_index / CORNER) ** 2)
+    rows = jnp.broadcast_to(brune[:, None, None], (FREQS, 8, spectra.shape[3]))
     other = lax.ppermute(tensor, "var", [(0, 1), (1, 0)])
     dense = prepare(line, table, tensor, other)
     if line:
-        acc, first, second = line_steps(spectra, dense)
-        inner1, middle1, outer1, far1 = second
-        keep, send = late(0, table, dense, acc, first)
-        pieces = [keep, exchange(send)]
-        more = late(1, table, dense, acc, (inner1, outer1))
-        far1 = after(far1, pieces[1], more)
-        keep, send = last(dense, more, middle1, far1)
-        pieces += [keep, exchange(send)]
+        sums, middle, far0, far1 = line_steps(spectra, dense, table)
+        pieces = fourth(dense, sums[0], middle[0], far0)
+        pieces = (pieces[0], exchange(pieces[1]))
+        keep_a, send_a = last(0, dense, sums[1], middle[1], far1[0])
+        got_a = exchange(send_a)
+        final = after(far1[1], pieces[1], keep_a)
+        keep_b, send_b = last(1, dense, sums[1], middle[1], final)
+        got_b = exchange(send_b)
+        result, part = finish_first(rows, *pieces, keep_a, got_a)
+        result = finish_last(rows, part, keep_b, got_b, result)
     else:
         gathered = lax.all_gather(spectra, "site", axis=4, tiled=True)
         pieces = []
@@ -396,8 +514,7 @@
                 both = jnp.concatenate([keep, send], axis=2)
                 keep = lax.psum_scatter(both, "sub", scatter_dimension=2, tiled=True)
                 pieces += [keep, jnp.zeros_like(keep)]
-    rows = jnp.broadcast_to(brune[:, None, None], (FREQS, 8, pieces[0].shape[3]))
-    result = finish(rows, pieces)
+        result = finish(rows, pieces)
     return result.transpose(0, 1, 2, 4, 3)
 
 

time: 63.6 us -> 62.7 us (0.986)
  waiting for transfers between devices: 36.4 us -> 32 us
  starting transfers between devices: 13.2 us -> 14.7 us
  local copies, waits for them, and re-layouts: 1.33 us -> 2.24 us
    ppermute x2, waiting for transfers between devices: 12.6 us -> 10.6 us  [line_steps(): outer = [move(inner[f], perm=OUTER) for f in range(FREQS)]]
    ppermute x1, waiting for transfers between devices: 8.96 us -> 7.12 us  [line_steps(): pairs = move(own, perm=PAIRS)]
    ppermute x4 -> x5, starting transfers between devices: 3.93 us -> 5.38 us  [the longest x2 2.58 us: line_steps(): move(handed[:, :, h * width:(h + 1) * width], perm=OUTER)]
    pallas_call x1, Pallas kernels: 4.26 us -> 5.18 us  [prepare(): pl.pallas_call(functools.partial(prepare_kernel, line), out_shape=pltpu.V...]
    squeeze x1 -> x2, local copies, waits for them, and re-layouts: 1.18 us -> 2.08 us  [line_steps(): inner = [move(own[0], perm=INNER), move(after(own, table)[1], perm=INNER)]]
    ppermute x2 -> x3, waiting for transfers between devices: 4.05 us -> 3.21 us  [exchange(): return lax.ppermute(send, 'sub', [(0, 1), (1, 0)])]
    pallas_call x4 -> x7, Pallas kernels: 4.41 us -> 4.15 us  [the longest x2 1.08 us: third(): pl.pallas_call(functools.partial(third_kernel, f), out_shape=pltpu.VMEM((...]
    ppermute x4 -> x5, waiting for transfers between devices: 10.8 us -> 11.1 us  [the longest x1 5.93 us: line_steps(): far0 = move(after(middle[0], sums[0]), perm=OUTER)]
  transfers between devices with their start and end apart: 12 -> 14, of which waited for: 6 -> 8; matrix products, arithmetic and copies ran while one was open for 4% -> 6% of each run, Pallas kernels for 14% -> 17%
where the time goes in v4:
time: 62.7 us; the launch traced here: 62.2 us
  waiting for transfers between devices  32 us (51%)
  starting transfers between devices  14.7 us (23%)
  Pallas kernels  11.1 us (18%)
  local copies, waits for them, and re-layouts  2.24 us (4%)
  other arithmetic  1.36 us (2%)
  between operations  0.88 us (1%)
    ppermute x2, waiting for transfers between devices, line_steps(): outer = [move(inner[f], perm=OUTER) for f in range(FREQS)]  10.6 us
    ppermute x1, waiting for transfers between devices, line_steps(): pairs = move(own, perm=PAIRS)  7.12 us
    ppermute x1, waiting for transfers between devices, line_steps(): far0 = move(after(middle[0], sums[0]), perm=OUTER)  5.93 us
    pallas_call x1, Pallas kernels, prepare(): pl.pallas_call(functools.partial(prepare_kernel, line), out_shape=pltpu.V...  5.18 us
    ppermute x2, waiting for transfers between devices, line_steps(): move(handed[:, :, h * width:(h + 1) * width], perm=OUTER)  5.16 us
    ppermute x3, waiting for transfers between devices, exchange(): return lax.ppermute(send, 'sub', [(0, 1), (1, 0)])  3.21 us
    ppermute x2, starting transfers between devices, line_steps(): move(handed[:, :, h * width:(h + 1) * width], perm=OUTER)  2.58 us
    ppermute x2, starting transfers between devices, line_steps(): outer = [move(inner[f], perm=OUTER) for f in range(FREQS)]  2.58 us
  transfers between devices with their start and end apart: 14, of which 8 were waited for; matrix products, arithmetic and copies ran while one was open for 6% of the time, Pallas kernels for 17%

profile of v4, /device:TPU:0, one launch (start us, length us, event | category | flops | bytes accessed | tf_op | source)
XLA Modules:
  0.0 62.2 jit_solution(7922554123176845461)
XLA Ops:
  0.0 0.5 collective-permute-start
  0.5 2.6 %collective-permute-start.1 = (bf16[2,2,6,128,128]{4,3,2,1,0:T(8,128)(2,1)}, bf16[2,2,6,128,128]{4,3,2,1,0:T(8,128)(2,1)S(1)}, u32[]{:S(2)}, u32[]{:S(2)}) collective-permute-start(bf16[2,2,6,128,128]{4,3,2,1,0:T(8,128)(2,1)} %bitcast.23), channel_id=1, source_target_pairs={{0,4},{4,0},{8,12},{12,8},{1,5},{5,1},{9,13},{13,9},{2,6},{6,2},{1... | collective-permute-start | bytes 2359304 | tf_op jit(solution)/shard_map/ppermute | solution.py:457
  3.0 1.1 %slice_bitcast_fusion = bf16[2,6,128,128]{3,2,1,0:T(8,128)(2,1)S(1)} fusion(bf16[2,2,6,128,128]{4,3,2,1,0:T(8,128)(2,1)} %bitcast.24), kind=kLoop, calls=%fused_computation | loop fusion | bytes 786432 | tf_op jit(solution)/shard_map/squeeze | solution.py:458
  4.1 0.7 %collective-permute-start.2 = (bf16[2,6,128,128]{3,2,1,0:T(8,128)(2,1)S(1)}, bf16[2,6,128,128]{3,2,1,0:T(8,128)(2,1)S(1)}, u32[]{:S(2)}, u32[]{:S(2)}) collective-permute-start(bf16[2,6,128,128]{3,2,1,0:T(8,128)(2,1)S(1)} %slice_bitcast_fusion), channel_id=1, source_target_pairs={{4,8},{8,4},{5,9},{9,5},{6,10},{10,6},{7,11},{11,7},{20,24},{24,20... | collective-permute-start | bytes 1179656 | tf_op jit(solution)/shard_map/ppermute | solution.py:458
  4.8 0.1 pad_add_fusion.1
  4.9 1.3 %pad_add_fusion.table = s32[4,16]{1,0:T(4,128)} fusion(s32[1,16]{1,0:T(1,128)S(1)} %pad_bitcast_fusion, s32[1,16]{1,0:T(1,128)} %bitcast.29, s32[1,16]{1,0:T(1,128)} %bitcast.30, s32[1,16]{1,0:T(1,128)} %bitcast.31), kind=kLoop, calls=%fused_computation.4 | loop fusion | flops 192 | bytes 512 | tf_op jit(solution)/shard_map/stack | solution.py:488
  6.1 1.0 %slice_bitcast_fusion.2 = bf16[2,6,128,128]{3,2,1,0:T(8,128)(2,1)S(1)} fusion(bf16[2,2,6,128,128]{4,3,2,1,0:T(8,128)(2,1)} %bitcast.25), kind=kLoop, calls=%fused_computation.2 | loop fusion | bytes 786432 | tf_op jit(solution)/shard_map/squeeze | solution.py:458
  7.2 0.0 copy-start
  7.2 0.8 %collective-permute-start.7 = (bf16[2,6,128,128]{3,2,1,0:T(8,128)(2,1)S(1)}, bf16[2,6,128,128]{3,2,1,0:T(8,128)(2,1)S(1)}, u32[]{:S(2)}, u32[]{:S(2)}) collective-permute-start(bf16[2,6,128,128]{3,2,1,0:T(8,128)(2,1)S(1)} %slice_bitcast_fusion.2), channel_id=1, source_target_pairs={{4,8},{8,4},{5,9},{9,5},{6,10},{10,6},{7,11},{11,7},{20,24},{24,20... | collective-permute-start | bytes 1179656 | tf_op jit(solution)/shard_map/ppermute | solution.py:458
  8.0 0.0 collective-permute-done.2.inner
  8.0 1.3 %collective-permute-start.3 = (bf16[2,6,128,128]{3,2,1,0:T(8,128)(2,1)S(1)}, bf16[2,6,128,128]{3,2,1,0:T(8,128)(2,1)S(1)}, u32[]{:S(2)}, u32[]{:S(2)}) collective-permute-start(bf16[2,6,128,128]{3,2,1,0:T(8,128)(2,1)S(1)} %collective-permute-done.2.inner), channel_id=1, source_target_pairs={{4,0},{8,12},{5,1},{9,13},{6,2},{10,14},{7,3},{11,15},{20,16},{24,... | collective-permute-start | bytes 1179656 | tf_op jit(solution)/shard_map/ppermute | solution.py:459
  9.3 0.0 collective-permute-done.other
  9.3 5.2 %shard_map.64.dense = bf16[2,4,3,256,768]{4,3,2,1,0:T(8,128)(2,1)S(1)} custom-call(s32[4,16]{1,0:T(4,128)} %pad_add_fusion.table, bf16[16,2,3,6,32,128]{5,4,3,2,1,0:T(8,128)(2,1)} %bitcast.28, bf16[16,2,3,6,32,128]{5,4,3,2,1,0:T(8,128)(2,1)} %collective-permute-done.other), custom_call_target="tpu_custom_call" | custom-call | bytes 12000000 | tf_op jit(solution)/shard_map/pallas_call | solution.py:97
  14.5 7.1 %collective-permute-done.1.pairs = bf16[2,2,6,128,128]{4,3,2,1,0:T(8,128)(2,1)S(1)} collective-permute-done((bf16[2,2,6,128,128]{4,3,2,1,0:T(8,128)(2,1)}, bf16[2,2,6,128,128]{4,3,2,1,0:T(8,128)(2,1)S(1)}, u32[]{:S(2)}, u32[]{:S(2)}) %collective-permute-start.1) | collective-permute-done | bytes 786464 | tf_op jit(solution)/shard_map/ppermute | solution.py:457
  21.6 0.1 slice_bitcast_fusion.1
  21.7 0.7 %collective-permute-start.4 = (bf16[2,6,128,128]{3,2,1,0:T(8,128)(2,1)S(1)}, bf16[2,6,128,128]{3,2,1,0:T(8,128)(2,1)S(1)}, u32[]{:S(2)}, u32[]{:S(2)}) collective-permute-start(bf16[2,6,128,128]{3,2,1,0:T(8,128)(2,1)S(1)} %get-tuple-element.21), channel_id=1, source_target_pairs={{4,8},{8,4},{5,9},{9,5},{6,10},{10,6},{7,11},{11,7},{20,24},{24,20... | collective-permute-start | bytes 1179656 | tf_op jit(solution)/shard_map/ppermute | solution.py:463
  22.4 0.0 collective-permute-done.7.inner
  22.4 1.3 %collective-permute-start.8 = (bf16[2,6,128,128]{3,2,1,0:T(8,128)(2,1)S(1)}, bf16[2,6,128,128]{3,2,1,0:T(8,128)(2,1)S(1)}, u32[]{:S(2)}, u32[]{:S(2)}) collective-permute-start(bf16[2,6,128,128]{3,2,1,0:T(8,128)(2,1)S(1)} %collective-permute-done.7.inner), channel_id=1, source_target_pairs={{4,0},{8,12},{5,1},{9,13},{6,2},{10,14},{7,3},{11,15},{20,16},{24,... | collective-permute-start | bytes 1179656 | tf_op jit(solution)/shard_map/ppermute | solution.py:459
  23.7 0.0 copy-done
  23.7 1.7 %shard_map.65.acc = f32[2,2,3,128,128]{4,3,2,1,0:T(8,128)S(1)} custom-call(bf16[2,4,3,256,768]{4,3,2,1,0:T(8,128)(2,1)S(1)} %shard_map.64.dense, bf16[2,2,6,128,128]{4,3,2,1,0:T(8,128)(2,1)S(1)} %bitcast.26, bf16[2,2,6,128,128]{4,3,2,1,0:T(8,128)(2,1)S(1)} %collective-permute-done.1.pairs), custom_call_target="tpu_custom_call" | custom-call | flops 1207959552 | bytes 4000000 | tf_op jit(solution)/shard_map/pallas_call | solution.py:162
  25.5 0.7 %collective-permute-start.9 = (bf16[2,6,128,128]{3,2,1,0:T(8,128)(2,1)S(1)}, bf16[2,6,128,128]{3,2,1,0:T(8,128)(2,1)S(1)}, u32[]{:S(2)}, u32[]{:S(2)}) collective-permute-start(bf16[2,6,128,128]{3,2,1,0:T(8,128)(2,1)S(1)} %get-tuple-element.26), channel_id=1, source_target_pairs={{4,8},{8,4},{5,9},{9,5},{6,10},{10,6},{7,11},{11,7},{20,24},{24,20... | collective-permute-start | bytes 1179656 | tf_op jit(solution)/shard_map/ppermute | solution.py:464
  26.1 3.7 %collective-permute-done.3.outer = bf16[2,6,128,128]{3,2,1,0:T(8,128)(2,1)S(1)} collective-permute-done((bf16[2,6,128,128]{3,2,1,0:T(8,128)(2,1)S(1)}, bf16[2,6,128,128]{3,2,1,0:T(8,128)(2,1)S(1)}, u32[]{:S(2)}, u32[]{:S(2)}) %collective-permute-start.3) | collective-permute-done | bytes 393248 | tf_op jit(solution)/shard_map/ppermute | solution.py:459
  29.9 0.5 shard_map.66.acc
  30.4 0.0 collective-permute-done.4.middle
  30.4 1.3 %collective-permute-start.5 = (bf16[2,6,128,128]{3,2,1,0:T(8,128)(2,1)S(1)}, bf16[2,6,128,128]{3,2,1,0:T(8,128)(2,1)S(1)}, u32[]{:S(2)}, u32[]{:S(2)}) collective-permute-start(bf16[2,6,128,128]{3,2,1,0:T(8,128)(2,1)S(1)} %collective-permute-done.4.middle), channel_id=1, source_target_pairs={{4,0},{8,12},{5,1},{9,13},{6,2},{10,14},{7,3},{11,15},{20,16},{24,... | collective-permute-start | bytes 1179656 | tf_op jit(solution)/shard_map/ppermute | solution.py:467
  31.7 6.9 %collective-permute-done.8.outer = bf16[2,6,128,128]{3,2,1,0:T(8,128)(2,1)S(1)} collective-permute-done((bf16[2,6,128,128]{3,2,1,0:T(8,128)(2,1)S(1)}, bf16[2,6,128,128]{3,2,1,0:T(8,128)(2,1)S(1)}, u32[]{:S(2)}, u32[]{:S(2)}) %collective-permute-start.8) | collective-permute-done | bytes 393248 | tf_op jit(solution)/shard_map/ppermute | solution.py:459
  38.6 0.6 shard_map.68.acc
  39.1 0.0 collective-permute-done.9.middle
  39.2 1.3 %collective-permute-start.10 = (bf16[2,6,64,128]{3,2,1,0:T(8,128)(2,1)S(1)}, bf16[2,6,64,128]{3,2,1,0:T(8,128)(2,1)S(1)}, u32[]{:S(2)}, u32[]{:S(2)}) collective-permute-start(bf16[2,6,64,128]{3,2,1,0:T(8,128)(2,1)S(1)} %get-tuple-element.38), channel_id=1, source_target_pairs={{4,0},{8,12},{5,1},{9,13},{6,2},{10,14},{7,3},{11,15},{20,16},{24,... | collective-permute-start | bytes 589832 | tf_op jit(solution)/shard_map/ppermute | solution.py:471
  40.5 1.3 %collective-permute-start.12 = (bf16[2,6,64,128]{3,2,1,0:T(8,128)(2,1)S(1)}, bf16[2,6,64,128]{3,2,1,0:T(8,128)(2,1)S(1)}, u32[]{:S(2)}, u32[]{:S(2)}) collective-permute-start(bf16[2,6,64,128]{3,2,1,0:T(8,128)(2,1)S(1)} %get-tuple-element.37), channel_id=1, source_target_pairs={{4,0},{8,12},{5,1},{9,13},{6,2},{10,14},{7,3},{11,15},{20,16},{24,... | collective-permute-start | bytes 589832 | tf_op jit(solution)/shard_map/ppermute | solution.py:471
  41.8 5.9 %collective-permute-done.5.far = bf16[2,6,128,128]{3,2,1,0:T(8,128)(2,1)S(1)} collective-permute-done((bf16[2,6,128,128]{3,2,1,0:T(8,128)(2,1)S(1)}, bf16[2,6,128,128]{3,2,1,0:T(8,128)(2,1)S(1)}, u32[]{:S(2)}, u32[]{:S(2)}) %collective-permute-start.5) | collective-permute-done | bytes 393248 | tf_op jit(solution)/shard_map/ppermute | solution.py:467
  47.7 0.5 shard_map.67
  48.2 1.5 %collective-permute-start.6 = (f32[2,3,64,128]{3,2,1,0:T(8,128)S(1)}, f32[2,3,64,128]{3,2,1,0:T(8,128)S(1)}, u32[]{:S(2)}, u32[]{:S(2)}) collective-permute-start(f32[2,3,64,128]{3,2,1,0:T(8,128)S(1)} %get-tuple-element.24), channel_id=1, source_target_pairs={{0,2},{2,0},{1,3},{3,1},{4,6},{6,4},{5,7},{7,5},{8,10},{10,8},{9,1... | collective-permute-start | bytes 589832 | tf_op jit(solution)/shard_map/ppermute | solution.py:477
  50.3 3.7 %collective-permute-done.10.far = bf16[2,6,64,128]{3,2,1,0:T(8,128)(2,1)S(1)} collective-permute-done((bf16[2,6,64,128]{3,2,1,0:T(8,128)(2,1)S(1)}, bf16[2,6,64,128]{3,2,1,0:T(8,128)(2,1)S(1)}, u32[]{:S(2)}, u32[]{:S(2)}) %collective-permute-start.10) | collective-permute-done | bytes 196640 | tf_op jit(solution)/shard_map/ppermute | solution.py:471
  54.1 0.5 shard_map.69
  54.6 0.1 collective-permute-start.11
  54.8 1.4 %collective-permute-done.12.far = bf16[2,6,64,128]{3,2,1,0:T(8,128)(2,1)S(1)} collective-permute-done((bf16[2,6,64,128]{3,2,1,0:T(8,128)(2,1)S(1)}, bf16[2,6,64,128]{3,2,1,0:T(8,128)(2,1)S(1)}, u32[]{:S(2)}, u32[]{:S(2)}) %collective-permute-start.12) | collective-permute-done | bytes 196640 | tf_op jit(solution)/shard_map/ppermute | solution.py:471
  56.2 0.0 collective-permute-done.6.got
  56.2 0.5 shard_map.71
  56.7 0.7 %collective-permute-start.13 = (f32[3,64,128]{2,1,0:T(8,128)S(1)}, f32[3,64,128]{2,1,0:T(8,128)S(1)}, u32[]{:S(2)}, u32[]{:S(2)}) collective-permute-start(f32[3,64,128]{2,1,0:T(8,128)S(1)} %get-tuple-element.33), channel_id=1, source_target_pairs={{0,2},{2,0},{1,3},{3,1},{4,6},{6,4},{5,7},{7,5},{8,10},{10,8},{9,1... | collective-permute-start | bytes 294920 | tf_op jit(solution)/shard_map/ppermute | solution.py:477
  57.4 1.9 %collective-permute-done.11.got_a = f32[3,64,128]{2,1,0:T(8,128)S(1)} collective-permute-done((f32[3,64,128]{2,1,0:T(8,128)S(1)}, f32[3,64,128]{2,1,0:T(8,128)S(1)}, u32[]{:S(2)}, u32[]{:S(2)}) %collective-permute-start.11) | collective-permute-done | bytes 98336 | tf_op jit(solution)/shard_map/ppermute | solution.py:477
  59.3 0.1 broadcast_in_dim.2.brune
  59.4 0.7 %shard_map.70 = (f32[2,2,3,64,128]{4,3,2,1,0:T(8,128)}, f32[3,64,128]{2,1,0:T(8,128)S(1)}) custom-call(f32[2,8,128]{2,1,0:T(8,128)S(1)} %broadcast_in_dim.2.brune, f32[2,3,64,128]{3,2,1,0:T(8,128)S(1)} %get-tuple-element.23.keep, f32[2,3,64,128]{3,2,1,0:T(8,128)S(1)} %collective-permute-done.6.got, f32[3,64,128]{2,1,0:T(8,128)S(1)} %get-tuple-element.28.keep_a, ...), custom_call_target="tpu_custom_call" | custom-call | flops 400000 | bytes 8000000 | tf_op jit(solution)/shard_map/pallas_call | solution.py:395
  60.1 1.3 %collective-permute-done.13.got_b = f32[3,64,128]{2,1,0:T(8,128)S(1)} collective-permute-done((f32[3,64,128]{2,1,0:T(8,128)S(1)}, f32[3,64,128]{2,1,0:T(8,128)S(1)}, u32[]{:S(2)}, u32[]{:S(2)}) %collective-permute-start.13) | collective-permute-done | bytes 98336 | tf_op jit(solution)/shard_map/ppermute | solution.py:477
  61.4 0.8 %shard_map.72 = f32[2,2,3,64,128]{4,3,2,1,0:T(8,128)} custom-call(f32[2,8,128]{2,1,0:T(8,128)S(1)} %broadcast_in_dim.2.brune, f32[3,64,128]{2,1,0:T(8,128)S(1)} %get-tuple-element.30.part, f32[3,64,128]{2,1,0:T(8,128)S(1)} %get-tuple-element.32.keep_b, f32[3,64,128]{2,1,0:T(8,128)S(1)} %collective-permute-done.13.got_b, ...), custom_call_target="tpu_custom_call", output_to_operand_aliasing={{}: (4, {})} | custom-call | flops 400000 | bytes 600000 | tf_op jit(solution)/shard_map/pallas_call | solution.py:429
  (3 shorter events, 0.0 us)
Async XLA Ops:
  0.0 9.3 %collective-permute-start = (bf16[16,2,3,6,32,128]{5,4,3,2,1,0:T(8,128)(2,1)}, bf16[16,2,3,6,32,128]{5,4,3,2,1,0:T(8,128)(2,1)}, u32[]{:S(2)}, u32[]{:S(2)}) collective-permute-start(bf16[16,2,3,6,32,128]{5,4,3,2,1,0:T(8,128)(2,1)} %bitcast.27), channel_id=1, source_target_pairs={{0,1},{1,0},{2,3},{3,2},{4,5},{5,4},{6,7},{7,6},{8,9},{9,8},{10,11... | collective-permute-start | bytes 14155784 | tf_op jit(solution)/shard_map/ppermute | solution.py:492
  0.5 21.2 %collective-permute-start.1 = (bf16[2,2,6,128,128]{4,3,2,1,0:T(8,128)(2,1)}, bf16[2,2,6,128,128]{4,3,2,1,0:T(8,128)(2,1)S(1)}, u32[]{:S(2)}, u32[]{:S(2)}) collective-permute-start(bf16[2,2,6,128,128]{4,3,2,1,0:T(8,128)(2,1)} %bitcast.23), channel_id=1, source_target_pairs={{0,4},{4,0},{8,12},{12,8},{1,5},{5,1},{9,13},{13,9},{2,6},{6,2},{1... | collective-permute-start | bytes 2359304 | tf_op jit(solution)/shard_map/ppermute | solution.py:457
  4.1 3.9 %collective-permute-start.2 = (bf16[2,6,128,128]{3,2,1,0:T(8,128)(2,1)S(1)}, bf16[2,6,128,128]{3,2,1,0:T(8,128)(2,1)S(1)}, u32[]{:S(2)}, u32[]{:S(2)}) collective-permute-start(bf16[2,6,128,128]{3,2,1,0:T(8,128)(2,1)S(1)} %slice_bitcast_fusion), channel_id=1, source_target_pairs={{4,8},{8,4},{5,9},{9,5},{6,10},{10,6},{7,11},{11,7},{20,24},{24,20... | collective-permute-start | bytes 1179656 | tf_op jit(solution)/shard_map/ppermute | solution.py:458
  7.2 16.5 %copy-start = (bf16[2,2,128,6,128]{4,2,3,1,0:T(8,128)(2,1)S(1)}, bf16[2,2,128,6,128]{4,2,3,1,0:T(8,128)(2,1)}, u32[]{:S(2)}) copy-start(bf16[2,2,128,6,128]{4,2,3,1,0:T(8,128)(2,1)} %param.7) | copy-start | bytes 2359300
  7.2 15.2 %collective-permute-start.7 = (bf16[2,6,128,128]{3,2,1,0:T(8,128)(2,1)S(1)}, bf16[2,6,128,128]{3,2,1,0:T(8,128)(2,1)S(1)}, u32[]{:S(2)}, u32[]{:S(2)}) collective-permute-start(bf16[2,6,128,128]{3,2,1,0:T(8,128)(2,1)S(1)} %slice_bitcast_fusion.2), channel_id=1, source_target_pairs={{4,8},{8,4},{5,9},{9,5},{6,10},{10,6},{7,11},{11,7},{20,24},{24,20... | collective-permute-start | bytes 1179656 | tf_op jit(solution)/shard_map/ppermute | solution.py:458
  8.0 21.9 %collective-permute-start.3 = (bf16[2,6,128,128]{3,2,1,0:T(8,128)(2,1)S(1)}, bf16[2,6,128,128]{3,2,1,0:T(8,128)(2,1)S(1)}, u32[]{:S(2)}, u32[]{:S(2)}) collective-permute-start(bf16[2,6,128,128]{3,2,1,0:T(8,128)(2,1)S(1)} %collective-permute-done.2.inner), channel_id=1, source_target_pairs={{4,0},{8,12},{5,1},{9,13},{6,2},{10,14},{7,3},{11,15},{20,16},{24,... | collective-permute-start | bytes 1179656 | tf_op jit(solution)/shard_map/ppermute | solution.py:459
  21.7 8.7 %collective-permute-start.4 = (bf16[2,6,128,128]{3,2,1,0:T(8,128)(2,1)S(1)}, bf16[2,6,128,128]{3,2,1,0:T(8,128)(2,1)S(1)}, u32[]{:S(2)}, u32[]{:S(2)}) collective-permute-start(bf16[2,6,128,128]{3,2,1,0:T(8,128)(2,1)S(1)} %get-tuple-element.21), channel_id=1, source_target_pairs={{4,8},{8,4},{5,9},{9,5},{6,10},{10,6},{7,11},{11,7},{20,24},{24,20... | collective-permute-start | bytes 1179656 | tf_op jit(solution)/shard_map/ppermute | solution.py:463
  22.4 16.2 %collective-permute-start.8 = (bf16[2,6,128,128]{3,2,1,0:T(8,128)(2,1)S(1)}, bf16[2,6,128,128]{3,2,1,0:T(8,128)(2,1)S(1)}, u32[]{:S(2)}, u32[]{:S(2)}) collective-permute-start(bf16[2,6,128,128]{3,2,1,0:T(8,128)(2,1)S(1)} %collective-permute-done.7.inner), channel_id=1, source_target_pairs={{4,0},{8,12},{5,1},{9,13},{6,2},{10,14},{7,3},{11,15},{20,16},{24,... | collective-permute-start | bytes 1179656 | tf_op jit(solution)/shard_map/ppermute | solution.py:459
  25.5 13.7 %collective-permute-start.9 = (bf16[2,6,128,128]{3,2,1,0:T(8,128)(2,1)S(1)}, bf16[2,6,128,128]{3,2,1,0:T(8,128)(2,1)S(1)}, u32[]{:S(2)}, u32[]{:S(2)}) collective-permute-start(bf16[2,6,128,128]{3,2,1,0:T(8,128)(2,1)S(1)} %get-tuple-element.26), channel_id=1, source_target_pairs={{4,8},{8,4},{5,9},{9,5},{6,10},{10,6},{7,11},{11,7},{20,24},{24,20... | collective-permute-start | bytes 1179656 | tf_op jit(solution)/shard_map/ppermute | solution.py:464
  30.4 17.3 %collective-permute-start.5 = (bf16[2,6,128,128]{3,2,1,0:T(8,128)(2,1)S(1)}, bf16[2,6,128,128]{3,2,1,0:T(8,128)(2,1)S(1)}, u32[]{:S(2)}, u32[]{:S(2)}) collective-permute-start(bf16[2,6,128,128]{3,2,1,0:T(8,128)(2,1)S(1)} %collective-permute-done.4.middle), channel_id=1, source_target_pairs={{4,0},{8,12},{5,1},{9,13},{6,2},{10,14},{7,3},{11,15},{20,16},{24,... | collective-permute-start | bytes 1179656 | tf_op jit(solution)/shard_map/ppermute | solution.py:467
  39.2 14.9 %collective-permute-start.10 = (bf16[2,6,64,128]{3,2,1,0:T(8,128)(2,1)S(1)}, bf16[2,6,64,128]{3,2,1,0:T(8,128)(2,1)S(1)}, u32[]{:S(2)}, u32[]{:S(2)}) collective-permute-start(bf16[2,6,64,128]{3,2,1,0:T(8,128)(2,1)S(1)} %get-tuple-element.38), channel_id=1, source_target_pairs={{4,0},{8,12},{5,1},{9,13},{6,2},{10,14},{7,3},{11,15},{20,16},{24,... | collective-permute-start | bytes 589832 | tf_op jit(solution)/shard_map/ppermute | solution.py:471
  40.5 15.7 %collective-permute-start.12 = (bf16[2,6,64,128]{3,2,1,0:T(8,128)(2,1)S(1)}, bf16[2,6,64,128]{3,2,1,0:T(8,128)(2,1)S(1)}, u32[]{:S(2)}, u32[]{:S(2)}) collective-permute-start(bf16[2,6,64,128]{3,2,1,0:T(8,128)(2,1)S(1)} %get-tuple-element.37), channel_id=1, source_target_pairs={{4,0},{8,12},{5,1},{9,13},{6,2},{10,14},{7,3},{11,15},{20,16},{24,... | collective-permute-start | bytes 589832 | tf_op jit(solution)/shard_map/ppermute | solution.py:471
  48.2 8.0 %collective-permute-start.6 = (f32[2,3,64,128]{3,2,1,0:T(8,128)S(1)}, f32[2,3,64,128]{3,2,1,0:T(8,128)S(1)}, u32[]{:S(2)}, u32[]{:S(2)}) collective-permute-start(f32[2,3,64,128]{3,2,1,0:T(8,128)S(1)} %get-tuple-element.24), channel_id=1, source_target_pairs={{0,2},{2,0},{1,3},{3,1},{4,6},{6,4},{5,7},{7,5},{8,10},{10,8},{9,1... | collective-permute-start | bytes 589832 | tf_op jit(solution)/shard_map/ppermute | solution.py:477
  54.6 4.7 %collective-permute-start.11 = (f32[3,64,128]{2,1,0:T(8,128)S(1)}, f32[3,64,128]{2,1,0:T(8,128)S(1)}, u32[]{:S(2)}, u32[]{:S(2)}) collective-permute-start(f32[3,64,128]{2,1,0:T(8,128)S(1)} %get-tuple-element.29), channel_id=1, source_target_pairs={{0,2},{2,0},{1,3},{3,1},{4,6},{6,4},{5,7},{7,5},{8,10},{10,8},{9,1... | collective-permute-start | bytes 294920 | tf_op jit(solution)/shard_map/ppermute | solution.py:477
  56.7 4.7 %collective-permute-start.13 = (f32[3,64,128]{2,1,0:T(8,128)S(1)}, f32[3,64,128]{2,1,0:T(8,128)S(1)}, u32[]{:S(2)}, u32[]{:S(2)}) collective-permute-start(f32[3,64,128]{2,1,0:T(8,128)S(1)} %get-tuple-element.33), channel_id=1, source_target_pairs={{0,2},{2,0},{1,3},{3,1},{4,6},{6,4},{5,7},{7,5},{8,10},{10,8},{9,1... | collective-permute-start | bytes 294920 | tf_op jit(solution)/shard_map/ppermute | solution.py:477

commit v5 on v4

--- a/solution.py
+++ b/solution.py
@@ -273,9 +273,10 @@
     )(dense, acc, middle, far)
 
 
-def last_kernel(h, dense, acc, middle, far, keep, send):
+def last_kernel(h, sent, dense, acc, middle, far, out):
     moments, width, columns = far.shape[1:]
-    half = keep.shape[1]
+    half = out.shape[1]
+    low = half if sent else 0
 
     def run(source):
         at = h * width if source is middle else 0
@@ -287,32 +288,34 @@
             axis=1,
         )
         for c in range(dense.shape[2]):
+            lhs = jnp.concatenate(
+                [
+                    dense[1, 3, c, low + 2 * half * r : low + 2 * half * r + half]
+                    for r in range(2)
+                ],
+                axis=0,
+            )
             total = lax.dot_general(
-                dense[1, 3, c],
-                rhs,
-                (((1,), (1,)), ((), ())),
-                preferred_element_type=jnp.float32,
+                lhs, rhs, (((1,), (1,)), ((), ())), preferred_element_type=jnp.float32
             )
-            crossed = swap_lanes(total[2 * half :])
+            crossed = swap_lanes(total[half:])
             crossed = jnp.where(low_lanes(crossed), -crossed, crossed)
-            value = acc[h, c] + (total[: 2 * half] + crossed)
-            keep[c] = value[:half]
-            send[c] = value[half:]
+            out[c] = acc[h, c, low : low + half] + (total[:half] + crossed)
 
     by_position(run, middle, far)
 
 
-def last(h, dense, acc, middle, far):
+def last(h, sent, dense, acc, middle, far):
     _, _, comps, rows, depth = dense.shape
     half = (comps, rows // 4, 2 * far.shape[2])
     return pl.pallas_call(
-        functools.partial(last_kernel, h),
-        out_shape=(pltpu.VMEM(half, jnp.float32),) * 2,
+        functools.partial(last_kernel, h, sent),
+        out_shape=pltpu.VMEM(half, jnp.float32),
         in_specs=[VMEM_SPEC] * 4,
-        out_specs=(VMEM_SPEC,) * 2,
-        compiler_params=pltpu.CompilerParams(vmem_limit_bytes=VMEM_LIMIT),
-        cost_estimate=pl.CostEstimate(
-            flops=2 * comps * rows * half[2] * depth,
+        out_specs=VMEM_SPEC,
+        compiler_params=pltpu.CompilerParams(vmem_limit_bytes=VMEM_LIMIT),
+        cost_estimate=pl.CostEstimate(
+            flops=comps * rows * half[2] * depth,
             bytes_accessed=500_000,
             transcendentals=0,
         ),
@@ -413,14 +416,15 @@
 
 def finish_last_kernel(brune, part, keep_b, got_b, _, result, value, sem):
     copies = []
-    for r in range(2):
-        for c in range(part.shape[0]):
-            second = (keep_b[c] + got_b[c]) * brune[1, :1]
-            value[r, c] = repack(part[c], second)[r]
-        copies.append(
-            pltpu.make_async_copy(value.at[r], result.at[1, r], sem.at[r])
-        )
-        copies[r].start()
+    for c in range(part.shape[0]):
+        second = (keep_b[c] + got_b[c]) * brune[1, :1]
+        for r, total in enumerate(repack(part[c], second)):
+            value[r, c] = total
+            copy = pltpu.make_async_copy(
+                value.at[r, c], result.at[1, r, c], sem.at[r, c]
+            )
+            copy.start()
+            copies.append(copy)
     for copy in copies:
         copy.wait()
 
@@ -433,7 +437,7 @@
         out_specs=HBM_SPEC,
         scratch_shapes=[
             pltpu.VMEM(result.shape[1:], result.dtype),
-            pltpu.SemaphoreType.DMA((2,)),
+            pltpu.SemaphoreType.DMA((2, 3)),
         ],
         input_output_aliases={4: 0},
         compiler_params=pltpu.CompilerParams(vmem_limit_bytes=VMEM_LIMIT),
@@ -460,7 +464,7 @@
     ready = after(pairs, dense)
     acc = early(dense, own, pairs)
     middle = [
-        move(after(ready[0], inner[0]), perm=INNER),
+        move(ready[0], perm=INNER),
         move(after(ready[1], *inner, acc), perm=INNER),
     ]
     sums = [third(f, dense, acc, inner[f], outer[f]) for f in range(FREQS)]
@@ -495,11 +499,14 @@
         sums, middle, far0, far1 = line_steps(spectra, dense, table)
         pieces = fourth(dense, sums[0], middle[0], far0)
         pieces = (pieces[0], exchange(pieces[1]))
-        keep_a, send_a = last(0, dense, sums[1], middle[1], far1[0])
+        shards_of = functools.partial(last, dense=dense, acc=sums[1], middle=middle[1])
+        send_a = shards_of(0, True, far=far1[0])
         got_a = exchange(send_a)
-        final = after(far1[1], pieces[1], keep_a)
-        keep_b, send_b = last(1, dense, sums[1], middle[1], final)
+        keep_a = shards_of(0, False, far=after(far1[0], send_a))
+        final = after(far1[1], pieces[1], send_a)
+        send_b = shards_of(1, True, far=final)
         got_b = exchange(send_b)
+        keep_b = shards_of(1, False, far=after(final, send_b))
         result, part = finish_first(rows, *pieces, keep_a, got_a)
         result = finish_last(rows, part, keep_b, got_b, result)
     else:

time: 62.7 us -> 62.2 us (level)
  waiting for transfers between devices: 32 us -> 27.5 us
  starting transfers between devices: 14.7 us -> 18.9 us
    ppermute x3, starting transfers between devices: 2.29 us -> 6.5 us  [exchange(): return lax.ppermute(send, 'sub', [(0, 1), (1, 0)])]
    ppermute x2, waiting for transfers between devices: 5.16 us -> 2.08 us  [line_steps(): move(handed[:, :, h * width:(h + 1) * width], perm=OUTER)]
    ppermute x3, waiting for transfers between devices: 3.21 us -> 1.15 us  [exchange(): return lax.ppermute(send, 'sub', [(0, 1), (1, 0)])]
    ppermute x1, waiting for transfers between devices: 5.93 us -> 5 us  [line_steps(): far0 = move(after(middle[0], sums[0]), perm=OUTER)]
    ppermute x1, waiting for transfers between devices: 7.12 us -> 8.04 us  [line_steps(): pairs = move(own, perm=PAIRS)]
    pallas_call x1, Pallas kernels: 5.18 us -> 4.26 us  [prepare(): pl.pallas_call(functools.partial(prepare_kernel, line), out_shape=pltpu.V...]
    pallas_call x2 -> x4, Pallas kernels: 1.08 us -> 1.56 us  [last(): pl.pallas_call(functools.partial(last_kernel, h, sent), out_shape=pltpu.V...]
  transfers between devices with their start and end apart: 14 -> 14, of which waited for: 8 -> 7; matrix products, arithmetic and copies ran while one was open for 6% -> 6% of each run, Pallas kernels for 17% -> 16%
where the time goes in v5:
time: 62.2 us; the launch traced here: 61.5 us
  waiting for transfers between devices  27.5 us (44%)
  starting transfers between devices  18.9 us (30%)
  Pallas kernels  10.7 us (17%)
  local copies, waits for them, and re-layouts  2.24 us (4%)
  other arithmetic  1.36 us (2%)
  between operations  0.88 us (1%)
    ppermute x2, waiting for transfers between devices, line_steps(): outer = [move(inner[f], perm=OUTER) for f in range(FREQS)]  11.2 us
    ppermute x1, waiting for transfers between devices, line_steps(): pairs = move(own, perm=PAIRS)  8.04 us
    ppermute x3, starting transfers between devices, exchange(): return lax.ppermute(send, 'sub', [(0, 1), (1, 0)])  6.5 us
    ppermute x1, waiting for transfers between devices, line_steps(): far0 = move(after(middle[0], sums[0]), perm=OUTER)  5 us
    pallas_call x1, Pallas kernels, prepare(): pl.pallas_call(functools.partial(prepare_kernel, line), out_shape=pltpu.V...  4.26 us
    ppermute x2, starting transfers between devices, line_steps(): move(handed[:, :, h * width:(h + 1) * width], perm=OUTER)  2.58 us
    ppermute x2, starting transfers between devices, line_steps(): outer = [move(inner[f], perm=OUTER) for f in range(FREQS)]  2.58 us
    ppermute x1, starting transfers between devices, line_steps(): pairs = move(own, perm=PAIRS)  2.57 us
  transfers between devices with their start and end apart: 14, of which 7 were waited for; matrix products, arithmetic and copies ran while one was open for 6% of the time, Pallas kernels for 16%

profile of v5, /device:TPU:0, one launch (start us, length us, event | category | flops | bytes accessed | tf_op | source)
XLA Modules:
  0.0 61.5 jit_solution(16964612806486605762)
XLA Ops:
  0.0 0.5 collective-permute-start
  0.5 2.6 %collective-permute-start.1 = (bf16[2,2,6,128,128]{4,3,2,1,0:T(8,128)(2,1)}, bf16[2,2,6,128,128]{4,3,2,1,0:T(8,128)(2,1)S(1)}, u32[]{:S(2)}, u32[]{:S(2)}) collective-permute-start(bf16[2,2,6,128,128]{4,3,2,1,0:T(8,128)(2,1)} %bitcast.23), channel_id=1, source_target_pairs={{0,4},{4,0},{8,12},{12,8},{1,5},{5,1},{9,13},{13,9},{2,6},{6,2},{1... | collective-permute-start | bytes 2359304 | tf_op jit(solution)/shard_map/ppermute | solution.py:461
  3.0 1.1 %slice_bitcast_fusion = bf16[2,6,128,128]{3,2,1,0:T(8,128)(2,1)S(1)} fusion(bf16[2,2,6,128,128]{4,3,2,1,0:T(8,128)(2,1)} %bitcast.24), kind=kLoop, calls=%fused_computation | loop fusion | bytes 786432 | tf_op jit(solution)/shard_map/squeeze | solution.py:462
  4.1 0.7 %collective-permute-start.2 = (bf16[2,6,128,128]{3,2,1,0:T(8,128)(2,1)S(1)}, bf16[2,6,128,128]{3,2,1,0:T(8,128)(2,1)S(1)}, u32[]{:S(2)}, u32[]{:S(2)}) collective-permute-start(bf16[2,6,128,128]{3,2,1,0:T(8,128)(2,1)S(1)} %slice_bitcast_fusion), channel_id=1, source_target_pairs={{4,8},{8,4},{5,9},{9,5},{6,10},{10,6},{7,11},{11,7},{20,24},{24,20... | collective-permute-start | bytes 1179656 | tf_op jit(solution)/shard_map/ppermute | solution.py:462
  4.8 0.1 pad_add_fusion.1
  4.9 1.3 %pad_add_fusion.table = s32[4,16]{1,0:T(4,128)} fusion(s32[1,16]{1,0:T(1,128)S(1)} %pad_bitcast_fusion, s32[1,16]{1,0:T(1,128)} %bitcast.29, s32[1,16]{1,0:T(1,128)} %bitcast.30, s32[1,16]{1,0:T(1,128)} %bitcast.31), kind=kLoop, calls=%fused_computation.4 | loop fusion | flops 192 | bytes 512 | tf_op jit(solution)/shard_map/stack | solution.py:492
  6.1 1.0 %slice_bitcast_fusion.2 = bf16[2,6,128,128]{3,2,1,0:T(8,128)(2,1)S(1)} fusion(bf16[2,2,6,128,128]{4,3,2,1,0:T(8,128)(2,1)} %bitcast.25), kind=kLoop, calls=%fused_computation.2 | loop fusion | bytes 786432 | tf_op jit(solution)/shard_map/squeeze | solution.py:462
  7.2 0.0 copy-start
  7.2 0.8 %collective-permute-start.7 = (bf16[2,6,128,128]{3,2,1,0:T(8,128)(2,1)S(1)}, bf16[2,6,128,128]{3,2,1,0:T(8,128)(2,1)S(1)}, u32[]{:S(2)}, u32[]{:S(2)}) collective-permute-start(bf16[2,6,128,128]{3,2,1,0:T(8,128)(2,1)S(1)} %slice_bitcast_fusion.2), channel_id=1, source_target_pairs={{4,8},{8,4},{5,9},{9,5},{6,10},{10,6},{7,11},{11,7},{20,24},{24,20... | collective-permute-start | bytes 1179656 | tf_op jit(solution)/shard_map/ppermute | solution.py:462
  8.0 0.0 collective-permute-done.2.inner
  8.0 1.3 %collective-permute-start.3 = (bf16[2,6,128,128]{3,2,1,0:T(8,128)(2,1)S(1)}, bf16[2,6,128,128]{3,2,1,0:T(8,128)(2,1)S(1)}, u32[]{:S(2)}, u32[]{:S(2)}) collective-permute-start(bf16[2,6,128,128]{3,2,1,0:T(8,128)(2,1)S(1)} %collective-permute-done.2.inner), channel_id=1, source_target_pairs={{4,0},{8,12},{5,1},{9,13},{6,2},{10,14},{7,3},{11,15},{20,16},{24,... | collective-permute-start | bytes 1179656 | tf_op jit(solution)/shard_map/ppermute | solution.py:463
  9.3 0.0 collective-permute-done.other
  9.3 4.3 %shard_map.64.dense = bf16[2,4,3,256,768]{4,3,2,1,0:T(8,128)(2,1)S(1)} custom-call(s32[4,16]{1,0:T(4,128)} %pad_add_fusion.table, bf16[16,2,3,6,32,128]{5,4,3,2,1,0:T(8,128)(2,1)} %bitcast.28, bf16[16,2,3,6,32,128]{5,4,3,2,1,0:T(8,128)(2,1)} %collective-permute-done.other), custom_call_target="tpu_custom_call" | custom-call | bytes 12000000 | tf_op jit(solution)/shard_map/pallas_call | solution.py:97
  13.6 8.0 %collective-permute-done.1.pairs = bf16[2,2,6,128,128]{4,3,2,1,0:T(8,128)(2,1)S(1)} collective-permute-done((bf16[2,2,6,128,128]{4,3,2,1,0:T(8,128)(2,1)}, bf16[2,2,6,128,128]{4,3,2,1,0:T(8,128)(2,1)S(1)}, u32[]{:S(2)}, u32[]{:S(2)}) %collective-permute-start.1) | collective-permute-done | bytes 786464 | tf_op jit(solution)/shard_map/ppermute | solution.py:461
  21.6 0.1 slice_bitcast_fusion.1
  21.7 0.7 %collective-permute-start.4 = (bf16[2,6,128,128]{3,2,1,0:T(8,128)(2,1)S(1)}, bf16[2,6,128,128]{3,2,1,0:T(8,128)(2,1)S(1)}, u32[]{:S(2)}, u32[]{:S(2)}) collective-permute-start(bf16[2,6,128,128]{3,2,1,0:T(8,128)(2,1)S(1)} %get-tuple-element.30), channel_id=1, source_target_pairs={{4,8},{8,4},{5,9},{9,5},{6,10},{10,6},{7,11},{11,7},{20,24},{24,20... | collective-permute-start | bytes 1179656 | tf_op jit(solution)/shard_map/ppermute | solution.py:467
  22.4 0.0 collective-permute-done.7.inner
  22.4 1.3 %collective-permute-start.8 = (bf16[2,6,128,128]{3,2,1,0:T(8,128)(2,1)S(1)}, bf16[2,6,128,128]{3,2,1,0:T(8,128)(2,1)S(1)}, u32[]{:S(2)}, u32[]{:S(2)}) collective-permute-start(bf16[2,6,128,128]{3,2,1,0:T(8,128)(2,1)S(1)} %collective-permute-done.7.inner), channel_id=1, source_target_pairs={{4,0},{8,12},{5,1},{9,13},{6,2},{10,14},{7,3},{11,15},{20,16},{24,... | collective-permute-start | bytes 1179656 | tf_op jit(solution)/shard_map/ppermute | solution.py:463
  23.7 0.0 copy-done
  23.7 1.7 %shard_map.65.acc = f32[2,2,3,128,128]{4,3,2,1,0:T(8,128)S(1)} custom-call(bf16[2,4,3,256,768]{4,3,2,1,0:T(8,128)(2,1)S(1)} %shard_map.64.dense, bf16[2,2,6,128,128]{4,3,2,1,0:T(8,128)(2,1)S(1)} %bitcast.26, bf16[2,2,6,128,128]{4,3,2,1,0:T(8,128)(2,1)S(1)} %collective-permute-done.1.pairs), custom_call_target="tpu_custom_call" | custom-call | flops 1207959552 | bytes 4000000 | tf_op jit(solution)/shard_map/pallas_call | solution.py:162
  25.5 0.7 %collective-permute-start.9 = (bf16[2,6,128,128]{3,2,1,0:T(8,128)(2,1)S(1)}, bf16[2,6,128,128]{3,2,1,0:T(8,128)(2,1)S(1)}, u32[]{:S(2)}, u32[]{:S(2)}) collective-permute-start(bf16[2,6,128,128]{3,2,1,0:T(8,128)(2,1)S(1)} %get-tuple-element.22), channel_id=1, source_target_pairs={{4,8},{8,4},{5,9},{9,5},{6,10},{10,6},{7,11},{11,7},{20,24},{24,20... | collective-permute-start | bytes 1179656 | tf_op jit(solution)/shard_map/ppermute | solution.py:468
  26.1 3.7 %collective-permute-done.3.outer = bf16[2,6,128,128]{3,2,1,0:T(8,128)(2,1)S(1)} collective-permute-done((bf16[2,6,128,128]{3,2,1,0:T(8,128)(2,1)S(1)}, bf16[2,6,128,128]{3,2,1,0:T(8,128)(2,1)S(1)}, u32[]{:S(2)}, u32[]{:S(2)}) %collective-permute-start.3) | collective-permute-done | bytes 393248 | tf_op jit(solution)/shard_map/ppermute | solution.py:463
  29.9 0.5 shard_map.66.acc
  30.4 0.0 collective-permute-done.4.middle
  30.4 1.3 %collective-permute-start.5 = (bf16[2,6,128,128]{3,2,1,0:T(8,128)(2,1)S(1)}, bf16[2,6,128,128]{3,2,1,0:T(8,128)(2,1)S(1)}, u32[]{:S(2)}, u32[]{:S(2)}) collective-permute-start(bf16[2,6,128,128]{3,2,1,0:T(8,128)(2,1)S(1)} %collective-permute-done.4.middle), channel_id=1, source_target_pairs={{4,0},{8,12},{5,1},{9,13},{6,2},{10,14},{7,3},{11,15},{20,16},{24,... | collective-permute-start | bytes 1179656 | tf_op jit(solution)/shard_map/ppermute | solution.py:471
  31.7 7.5 %collective-permute-done.8.outer = bf16[2,6,128,128]{3,2,1,0:T(8,128)(2,1)S(1)} collective-permute-done((bf16[2,6,128,128]{3,2,1,0:T(8,128)(2,1)S(1)}, bf16[2,6,128,128]{3,2,1,0:T(8,128)(2,1)S(1)}, u32[]{:S(2)}, u32[]{:S(2)}) %collective-permute-start.8) | collective-permute-done | bytes 393248 | tf_op jit(solution)/shard_map/ppermute | solution.py:463
  39.2 0.6 shard_map.68.acc
  39.7 0.0 collective-permute-done.9.middle
  39.8 1.3 %collective-permute-start.10 = (bf16[2,6,64,128]{3,2,1,0:T(8,128)(2,1)S(1)}, bf16[2,6,64,128]{3,2,1,0:T(8,128)(2,1)S(1)}, u32[]{:S(2)}, u32[]{:S(2)}) collective-permute-start(bf16[2,6,64,128]{3,2,1,0:T(8,128)(2,1)S(1)} %get-tuple-element.32), channel_id=1, source_target_pairs={{4,0},{8,12},{5,1},{9,13},{6,2},{10,14},{7,3},{11,15},{20,16},{24,... | collective-permute-start | bytes 589832 | tf_op jit(solution)/shard_map/ppermute | solution.py:475
  41.1 1.3 %collective-permute-start.12 = (bf16[2,6,64,128]{3,2,1,0:T(8,128)(2,1)S(1)}, bf16[2,6,64,128]{3,2,1,0:T(8,128)(2,1)S(1)}, u32[]{:S(2)}, u32[]{:S(2)}) collective-permute-start(bf16[2,6,64,128]{3,2,1,0:T(8,128)(2,1)S(1)} %get-tuple-element.31), channel_id=1, source_target_pairs={{4,0},{8,12},{5,1},{9,13},{6,2},{10,14},{7,3},{11,15},{20,16},{24,... | collective-permute-start | bytes 589832 | tf_op jit(solution)/shard_map/ppermute | solution.py:475
  42.4 5.0 %collective-permute-done.5.far = bf16[2,6,128,128]{3,2,1,0:T(8,128)(2,1)S(1)} collective-permute-done((bf16[2,6,128,128]{3,2,1,0:T(8,128)(2,1)S(1)}, bf16[2,6,128,128]{3,2,1,0:T(8,128)(2,1)S(1)}, u32[]{:S(2)}, u32[]{:S(2)}) %collective-permute-start.5) | collective-permute-done | bytes 393248 | tf_op jit(solution)/shard_map/ppermute | solution.py:471
  47.4 0.5 shard_map.67
  47.9 2.3 %collective-permute-start.6 = (f32[2,3,64,128]{3,2,1,0:T(8,128)S(1)}, f32[2,3,64,128]{3,2,1,0:T(8,128)S(1)}, u32[]{:S(2)}, u32[]{:S(2)}) collective-permute-start(f32[2,3,64,128]{3,2,1,0:T(8,128)S(1)} %get-tuple-element.20), channel_id=1, source_target_pairs={{0,2},{2,0},{1,3},{3,1},{4,6},{6,4},{5,7},{7,5},{8,10},{10,8},{9,1... | collective-permute-start | bytes 589832 | tf_op jit(solution)/shard_map/ppermute | solution.py:481
  50.8 2.1 %collective-permute-done.10.far = bf16[2,6,64,128]{3,2,1,0:T(8,128)(2,1)S(1)} collective-permute-done((bf16[2,6,64,128]{3,2,1,0:T(8,128)(2,1)S(1)}, bf16[2,6,64,128]{3,2,1,0:T(8,128)(2,1)S(1)}, u32[]{:S(2)}, u32[]{:S(2)}) %collective-permute-start.10) | collective-permute-done | bytes 196640 | tf_op jit(solution)/shard_map/ppermute | solution.py:475
  52.9 0.4 shard_map.69
  53.3 2.3 %collective-permute-start.11 = (f32[3,64,128]{2,1,0:T(8,128)S(1)}, f32[3,64,128]{2,1,0:T(8,128)S(1)}, u32[]{:S(2)}, u32[]{:S(2)}) collective-permute-start(f32[3,64,128]{2,1,0:T(8,128)S(1)} %shard_map.69), channel_id=1, source_target_pairs={{0,2},{2,0},{1,3},{3,1},{4,6},{6,4},{5,7},{7,5},{8,10},{10,8},{9,1... | collective-permute-start | bytes 294920 | tf_op jit(solution)/shard_map/ppermute | solution.py:481
  55.6 0.0 collective-permute-done.12.far
  55.6 0.0 collective-permute-done.6.got
  55.6 0.4 shard_map.72
  56.0 1.9 %collective-permute-start.13 = (f32[3,64,128]{2,1,0:T(8,128)S(1)}, f32[3,64,128]{2,1,0:T(8,128)S(1)}, u32[]{:S(2)}, u32[]{:S(2)}) collective-permute-start(f32[3,64,128]{2,1,0:T(8,128)S(1)} %shard_map.72), channel_id=1, source_target_pairs={{0,2},{2,0},{1,3},{3,1},{4,6},{6,4},{5,7},{7,5},{8,10},{10,8},{9,1... | collective-permute-start | bytes 294920 | tf_op jit(solution)/shard_map/ppermute | solution.py:481
  57.9 0.4 shard_map.70.keep_a
  58.3 0.8 %collective-permute-done.11.got_a = f32[3,64,128]{2,1,0:T(8,128)S(1)} collective-permute-done((f32[3,64,128]{2,1,0:T(8,128)S(1)}, f32[3,64,128]{2,1,0:T(8,128)S(1)}, u32[]{:S(2)}, u32[]{:S(2)}) %collective-permute-start.11) | collective-permute-done | bytes 98336 | tf_op jit(solution)/shard_map/ppermute | solution.py:481
  59.1 0.1 broadcast_in_dim.2.brune
  59.2 0.7 %shard_map.71 = (f32[2,2,3,64,128]{4,3,2,1,0:T(8,128)}, f32[3,64,128]{2,1,0:T(8,128)S(1)}) custom-call(f32[2,8,128]{2,1,0:T(8,128)S(1)} %broadcast_in_dim.2.brune, f32[2,3,64,128]{3,2,1,0:T(8,128)S(1)} %get-tuple-element.19.keep, f32[2,3,64,128]{3,2,1,0:T(8,128)S(1)} %collective-permute-done.6.got, f32[3,64,128]{2,1,0:T(8,128)S(1)} %shard_map.70.keep_a, ...), custom_call_target="tpu_custom_call" | custom-call | flops 400000 | bytes 8000000 | tf_op jit(solution)/shard_map/pallas_call | solution.py:398
  59.9 0.4 shard_map.73.keep_b
  60.3 0.4 collective-permute-done.13.got_b
  60.7 0.8 %shard_map.74 = f32[2,2,3,64,128]{4,3,2,1,0:T(8,128)} custom-call(f32[2,8,128]{2,1,0:T(8,128)S(1)} %broadcast_in_dim.2.brune, f32[3,64,128]{2,1,0:T(8,128)S(1)} %get-tuple-element.25.part, f32[3,64,128]{2,1,0:T(8,128)S(1)} %shard_map.73.keep_b, f32[3,64,128]{2,1,0:T(8,128)S(1)} %collective-permute-done.13.got_b, ...), custom_call_target="tpu_custom_call", output_to_operand_aliasing={{}: (4, {})} | custom-call | flops 400000 | bytes 600000 | tf_op jit(solution)/shard_map/pallas_call | solution.py:433
  (3 shorter events, 0.0 us)
Async XLA Ops:
  0.0 9.3 %collective-permute-start = (bf16[16,2,3,6,32,128]{5,4,3,2,1,0:T(8,128)(2,1)}, bf16[16,2,3,6,32,128]{5,4,3,2,1,0:T(8,128)(2,1)}, u32[]{:S(2)}, u32[]{:S(2)}) collective-permute-start(bf16[16,2,3,6,32,128]{5,4,3,2,1,0:T(8,128)(2,1)} %bitcast.27), channel_id=1, source_target_pairs={{0,1},{1,0},{2,3},{3,2},{4,5},{5,4},{6,7},{7,6},{8,9},{9,8},{10,11... | collective-permute-start | bytes 14155784 | tf_op jit(solution)/shard_map/ppermute | solution.py:496
  0.5 21.2 %collective-permute-start.1 = (bf16[2,2,6,128,128]{4,3,2,1,0:T(8,128)(2,1)}, bf16[2,2,6,128,128]{4,3,2,1,0:T(8,128)(2,1)S(1)}, u32[]{:S(2)}, u32[]{:S(2)}) collective-permute-start(bf16[2,2,6,128,128]{4,3,2,1,0:T(8,128)(2,1)} %bitcast.23), channel_id=1, source_target_pairs={{0,4},{4,0},{8,12},{12,8},{1,5},{5,1},{9,13},{13,9},{2,6},{6,2},{1... | collective-permute-start | bytes 2359304 | tf_op jit(solution)/shard_map/ppermute | solution.py:461
  4.1 3.9 %collective-permute-start.2 = (bf16[2,6,128,128]{3,2,1,0:T(8,128)(2,1)S(1)}, bf16[2,6,128,128]{3,2,1,0:T(8,128)(2,1)S(1)}, u32[]{:S(2)}, u32[]{:S(2)}) collective-permute-start(bf16[2,6,128,128]{3,2,1,0:T(8,128)(2,1)S(1)} %slice_bitcast_fusion), channel_id=1, source_target_pairs={{4,8},{8,4},{5,9},{9,5},{6,10},{10,6},{7,11},{11,7},{20,24},{24,20... | collective-permute-start | bytes 1179656 | tf_op jit(solution)/shard_map/ppermute | solution.py:462
  7.2 16.5 %copy-start = (bf16[2,2,128,6,128]{4,2,3,1,0:T(8,128)(2,1)S(1)}, bf16[2,2,128,6,128]{4,2,3,1,0:T(8,128)(2,1)}, u32[]{:S(2)}) copy-start(bf16[2,2,128,6,128]{4,2,3,1,0:T(8,128)(2,1)} %param.7) | copy-start | bytes 2359300
  7.2 15.2 %collective-permute-start.7 = (bf16[2,6,128,128]{3,2,1,0:T(8,128)(2,1)S(1)}, bf16[2,6,128,128]{3,2,1,0:T(8,128)(2,1)S(1)}, u32[]{:S(2)}, u32[]{:S(2)}) collective-permute-start(bf16[2,6,128,128]{3,2,1,0:T(8,128)(2,1)S(1)} %slice_bitcast_fusion.2), channel_id=1, source_target_pairs={{4,8},{8,4},{5,9},{9,5},{6,10},{10,6},{7,11},{11,7},{20,24},{24,20... | collective-permute-start | bytes 1179656 | tf_op jit(solution)/shard_map/ppermute | solution.py:462
  8.0 21.9 %collective-permute-start.3 = (bf16[2,6,128,128]{3,2,1,0:T(8,128)(2,1)S(1)}, bf16[2,6,128,128]{3,2,1,0:T(8,128)(2,1)S(1)}, u32[]{:S(2)}, u32[]{:S(2)}) collective-permute-start(bf16[2,6,128,128]{3,2,1,0:T(8,128)(2,1)S(1)} %collective-permute-done.2.inner), channel_id=1, source_target_pairs={{4,0},{8,12},{5,1},{9,13},{6,2},{10,14},{7,3},{11,15},{20,16},{24,... | collective-permute-start | bytes 1179656 | tf_op jit(solution)/shard_map/ppermute | solution.py:463
  21.7 8.7 %collective-permute-start.4 = (bf16[2,6,128,128]{3,2,1,0:T(8,128)(2,1)S(1)}, bf16[2,6,128,128]{3,2,1,0:T(8,128)(2,1)S(1)}, u32[]{:S(2)}, u32[]{:S(2)}) collective-permute-start(bf16[2,6,128,128]{3,2,1,0:T(8,128)(2,1)S(1)} %get-tuple-element.30), channel_id=1, source_target_pairs={{4,8},{8,4},{5,9},{9,5},{6,10},{10,6},{7,11},{11,7},{20,24},{24,20... | collective-permute-start | bytes 1179656 | tf_op jit(solution)/shard_map/ppermute | solution.py:467
  22.4 16.8 %collective-permute-start.8 = (bf16[2,6,128,128]{3,2,1,0:T(8,128)(2,1)S(1)}, bf16[2,6,128,128]{3,2,1,0:T(8,128)(2,1)S(1)}, u32[]{:S(2)}, u32[]{:S(2)}) collective-permute-start(bf16[2,6,128,128]{3,2,1,0:T(8,128)(2,1)S(1)} %collective-permute-done.7.inner), channel_id=1, source_target_pairs={{4,0},{8,12},{5,1},{9,13},{6,2},{10,14},{7,3},{11,15},{20,16},{24,... | collective-permute-start | bytes 1179656 | tf_op jit(solution)/shard_map/ppermute | solution.py:463
  25.5 14.3 %collective-permute-start.9 = (bf16[2,6,128,128]{3,2,1,0:T(8,128)(2,1)S(1)}, bf16[2,6,128,128]{3,2,1,0:T(8,128)(2,1)S(1)}, u32[]{:S(2)}, u32[]{:S(2)}) collective-permute-start(bf16[2,6,128,128]{3,2,1,0:T(8,128)(2,1)S(1)} %get-tuple-element.22), channel_id=1, source_target_pairs={{4,8},{8,4},{5,9},{9,5},{6,10},{10,6},{7,11},{11,7},{20,24},{24,20... | collective-permute-start | bytes 1179656 | tf_op jit(solution)/shard_map/ppermute | solution.py:468
  30.4 17.0 %collective-permute-start.5 = (bf16[2,6,128,128]{3,2,1,0:T(8,128)(2,1)S(1)}, bf16[2,6,128,128]{3,2,1,0:T(8,128)(2,1)S(1)}, u32[]{:S(2)}, u32[]{:S(2)}) collective-permute-start(bf16[2,6,128,128]{3,2,1,0:T(8,128)(2,1)S(1)} %collective-permute-done.4.middle), channel_id=1, source_target_pairs={{4,0},{8,12},{5,1},{9,13},{6,2},{10,14},{7,3},{11,15},{20,16},{24,... | collective-permute-start | bytes 1179656 | tf_op jit(solution)/shard_map/ppermute | solution.py:471
  39.8 13.1 %collective-permute-start.10 = (bf16[2,6,64,128]{3,2,1,0:T(8,128)(2,1)S(1)}, bf16[2,6,64,128]{3,2,1,0:T(8,128)(2,1)S(1)}, u32[]{:S(2)}, u32[]{:S(2)}) collective-permute-start(bf16[2,6,64,128]{3,2,1,0:T(8,128)(2,1)S(1)} %get-tuple-element.32), channel_id=1, source_target_pairs={{4,0},{8,12},{5,1},{9,13},{6,2},{10,14},{7,3},{11,15},{20,16},{24,... | collective-permute-start | bytes 589832 | tf_op jit(solution)/shard_map/ppermute | solution.py:475
  41.1 14.5 %collective-permute-start.12 = (bf16[2,6,64,128]{3,2,1,0:T(8,128)(2,1)S(1)}, bf16[2,6,64,128]{3,2,1,0:T(8,128)(2,1)S(1)}, u32[]{:S(2)}, u32[]{:S(2)}) collective-permute-start(bf16[2,6,64,128]{3,2,1,0:T(8,128)(2,1)S(1)} %get-tuple-element.31), channel_id=1, source_target_pairs={{4,0},{8,12},{5,1},{9,13},{6,2},{10,14},{7,3},{11,15},{20,16},{24,... | collective-permute-start | bytes 589832 | tf_op jit(solution)/shard_map/ppermute | solution.py:475
  47.9 7.7 %collective-permute-start.6 = (f32[2,3,64,128]{3,2,1,0:T(8,128)S(1)}, f32[2,3,64,128]{3,2,1,0:T(8,128)S(1)}, u32[]{:S(2)}, u32[]{:S(2)}) collective-permute-start(f32[2,3,64,128]{3,2,1,0:T(8,128)S(1)} %get-tuple-element.20), channel_id=1, source_target_pairs={{0,2},{2,0},{1,3},{3,1},{4,6},{6,4},{5,7},{7,5},{8,10},{10,8},{9,1... | collective-permute-start | bytes 589832 | tf_op jit(solution)/shard_map/ppermute | solution.py:481
  53.3 5.8 %collective-permute-start.11 = (f32[3,64,128]{2,1,0:T(8,128)S(1)}, f32[3,64,128]{2,1,0:T(8,128)S(1)}, u32[]{:S(2)}, u32[]{:S(2)}) collective-permute-start(f32[3,64,128]{2,1,0:T(8,128)S(1)} %shard_map.69), channel_id=1, source_target_pairs={{0,2},{2,0},{1,3},{3,1},{4,6},{6,4},{5,7},{7,5},{8,10},{10,8},{9,1... | collective-permute-start | bytes 294920 | tf_op jit(solution)/shard_map/ppermute | solution.py:481
  56.0 4.7 %collective-permute-start.13 = (f32[3,64,128]{2,1,0:T(8,128)S(1)}, f32[3,64,128]{2,1,0:T(8,128)S(1)}, u32[]{:S(2)}, u32[]{:S(2)}) collective-permute-start(f32[3,64,128]{2,1,0:T(8,128)S(1)} %shard_map.72), channel_id=1, source_target_pairs={{0,2},{2,0},{1,3},{3,1},{4,6},{6,4},{5,7},{7,5},{8,10},{10,8},{9,1... | collective-permute-start | bytes 294920 | tf_op jit(solution)/shard_map/ppermute | solution.py:481

commit v6 on v5

--- a/solution.py
+++ b/solution.py
@@ -389,7 +389,9 @@
             pltpu.make_async_copy(value.at[r], result.at[0, r], sem.at[r])
         )
         copies[r].start()
-    part[...] = (keep_a[...] + got_a[...]) * brune[1, :1]
+    for c in range(keep_a.shape[0]):
+        part[0, c] = (keep_a[c] + got_a[c]) * brune[1, :1]
+        part[1, c] = swap_lanes(part[0, c])
     for copy in copies:
         copy.wait()
 
@@ -399,7 +401,7 @@
         finish_first_kernel,
         out_shape=(
             jax.ShapeDtypeStruct((FREQS,) + keep.shape, keep.dtype),
-            pltpu.VMEM(keep_a.shape, keep.dtype),
+            pltpu.VMEM((2,) + keep_a.shape, keep.dtype),
         ),
         in_specs=[VMEM_SPEC] * 5,
         out_specs=(HBM_SPEC, VMEM_SPEC),
@@ -416,9 +418,11 @@
 
 def finish_last_kernel(brune, part, keep_b, got_b, _, result, value, sem):
     copies = []
-    for c in range(part.shape[0]):
+    low = low_lanes(keep_b[0])
+    for c in range(keep_b.shape[0]):
         second = (keep_b[c] + got_b[c]) * brune[1, :1]
-        for r, total in enumerate(repack(part[c], second)):
+        real = jnp.where(low, part[0, c], swap_lanes(second))
+        for r, total in enumerate((real, jnp.where(low, part[1, c], second))):
             value[r, c] = total
             copy = pltpu.make_async_copy(
                 value.at[r, c], result.at[1, r, c], sem.at[r, c]

time: 62.2 us -> 62.4 us (level)
  waiting for transfers between devices: 27.5 us -> 31.5 us
  starting transfers between devices: 18.9 us -> 15.4 us
    ppermute x3, starting transfers between devices: 6.5 us -> 3 us  [exchange(): return lax.ppermute(send, 'sub', [(0, 1), (1, 0)])]
    ppermute x2, waiting for transfers between devices: 2.08 us -> 4.37 us  [line_steps(): move(handed[:, :, h * width:(h + 1) * width], perm=OUTER)]
    ppermute x3, waiting for transfers between devices: 1.15 us -> 2.01 us  [exchange(): return lax.ppermute(send, 'sub', [(0, 1), (1, 0)])]
    ppermute x2, waiting for transfers between devices: 11.2 us -> 11.9 us  [line_steps(): outer = [move(inner[f], perm=OUTER) for f in range(FREQS)]]
  transfers between devices with their start and end apart: 14 -> 14, of which waited for: 7 -> 8; matrix products, arithmetic and copies ran while one was open for 6% -> 6% of each run, Pallas kernels for 16% -> 16%
where the time goes in v6:
time: 62.4 us; the launch traced here: 61.8 us
  waiting for transfers between devices  31.5 us (50%)
  starting transfers between devices  15.4 us (25%)
  Pallas kernels  10.5 us (17%)
  local copies, waits for them, and re-layouts  2.24 us (4%)
  other arithmetic  1.36 us (2%)
  between operations  0.89 us (1%)
    ppermute x2, waiting for transfers between devices, line_steps(): outer = [move(inner[f], perm=OUTER) for f in range(FREQS)]  11.9 us
    ppermute x1, waiting for transfers between devices, line_steps(): pairs = move(own, perm=PAIRS)  8.22 us
    ppermute x1, waiting for transfers between devices, line_steps(): far0 = move(after(middle[0], sums[0]), perm=OUTER)  5 us
    ppermute x2, waiting for transfers between devices, line_steps(): move(handed[:, :, h * width:(h + 1) * width], perm=OUTER)  4.37 us
    pallas_call x1, Pallas kernels, prepare(): pl.pallas_call(functools.partial(prepare_kernel, line), out_shape=pltpu.V...  4.07 us
    ppermute x3, starting transfers between devices, exchange(): return lax.ppermute(send, 'sub', [(0, 1), (1, 0)])  3 us
    ppermute x2, starting transfers between devices, line_steps(): move(handed[:, :, h * width:(h + 1) * width], perm=OUTER)  2.58 us
    ppermute x2, starting transfers between devices, line_steps(): outer = [move(inner[f], perm=OUTER) for f in range(FREQS)]  2.58 us
  transfers between devices with their start and end apart: 14, of which 8 were waited for; matrix products, arithmetic and copies ran while one was open for 6% of the time, Pallas kernels for 16%

profile of v6, /device:TPU:0, one launch (start us, length us, event | category | flops | bytes accessed | tf_op | source)
XLA Modules:
  0.0 61.8 jit_solution(13232431432224510778)
XLA Ops:
  0.0 0.5 collective-permute-start
  0.5 2.6 %collective-permute-start.1 = (bf16[2,2,6,128,128]{4,3,2,1,0:T(8,128)(2,1)}, bf16[2,2,6,128,128]{4,3,2,1,0:T(8,128)(2,1)S(1)}, u32[]{:S(2)}, u32[]{:S(2)}) collective-permute-start(bf16[2,2,6,128,128]{4,3,2,1,0:T(8,128)(2,1)} %bitcast.23), channel_id=1, source_target_pairs={{0,4},{4,0},{8,12},{12,8},{1,5},{5,1},{9,13},{13,9},{2,6},{6,2},{1... | collective-permute-start | bytes 2359304 | tf_op jit(solution)/shard_map/ppermute | solution.py:465
  3.0 1.1 %slice_bitcast_fusion = bf16[2,6,128,128]{3,2,1,0:T(8,128)(2,1)S(1)} fusion(bf16[2,2,6,128,128]{4,3,2,1,0:T(8,128)(2,1)} %bitcast.24), kind=kLoop, calls=%fused_computation | loop fusion | bytes 786432 | tf_op jit(solution)/shard_map/squeeze | solution.py:466
  4.1 0.7 %collective-permute-start.2 = (bf16[2,6,128,128]{3,2,1,0:T(8,128)(2,1)S(1)}, bf16[2,6,128,128]{3,2,1,0:T(8,128)(2,1)S(1)}, u32[]{:S(2)}, u32[]{:S(2)}) collective-permute-start(bf16[2,6,128,128]{3,2,1,0:T(8,128)(2,1)S(1)} %slice_bitcast_fusion), channel_id=1, source_target_pairs={{4,8},{8,4},{5,9},{9,5},{6,10},{10,6},{7,11},{11,7},{20,24},{24,20... | collective-permute-start | bytes 1179656 | tf_op jit(solution)/shard_map/ppermute | solution.py:466
  4.8 0.1 pad_add_fusion.1
  4.9 1.3 %pad_add_fusion.table = s32[4,16]{1,0:T(4,128)} fusion(s32[1,16]{1,0:T(1,128)S(1)} %pad_bitcast_fusion, s32[1,16]{1,0:T(1,128)} %bitcast.29, s32[1,16]{1,0:T(1,128)} %bitcast.30, s32[1,16]{1,0:T(1,128)} %bitcast.31), kind=kLoop, calls=%fused_computation.4 | loop fusion | flops 192 | bytes 512 | tf_op jit(solution)/shard_map/stack | solution.py:496
  6.1 1.0 %slice_bitcast_fusion.2 = bf16[2,6,128,128]{3,2,1,0:T(8,128)(2,1)S(1)} fusion(bf16[2,2,6,128,128]{4,3,2,1,0:T(8,128)(2,1)} %bitcast.25), kind=kLoop, calls=%fused_computation.2 | loop fusion | bytes 786432 | tf_op jit(solution)/shard_map/squeeze | solution.py:466
  7.2 0.0 copy-start
  7.2 0.8 %collective-permute-start.7 = (bf16[2,6,128,128]{3,2,1,0:T(8,128)(2,1)S(1)}, bf16[2,6,128,128]{3,2,1,0:T(8,128)(2,1)S(1)}, u32[]{:S(2)}, u32[]{:S(2)}) collective-permute-start(bf16[2,6,128,128]{3,2,1,0:T(8,128)(2,1)S(1)} %slice_bitcast_fusion.2), channel_id=1, source_target_pairs={{4,8},{8,4},{5,9},{9,5},{6,10},{10,6},{7,11},{11,7},{20,24},{24,20... | collective-permute-start | bytes 1179656 | tf_op jit(solution)/shard_map/ppermute | solution.py:466
  8.0 0.0 collective-permute-done.2.inner
  8.0 1.3 %collective-permute-start.3 = (bf16[2,6,128,128]{3,2,1,0:T(8,128)(2,1)S(1)}, bf16[2,6,128,128]{3,2,1,0:T(8,128)(2,1)S(1)}, u32[]{:S(2)}, u32[]{:S(2)}) collective-permute-start(bf16[2,6,128,128]{3,2,1,0:T(8,128)(2,1)S(1)} %collective-permute-done.2.inner), channel_id=1, source_target_pairs={{4,0},{8,12},{5,1},{9,13},{6,2},{10,14},{7,3},{11,15},{20,16},{24,... | collective-permute-start | bytes 1179656 | tf_op jit(solution)/shard_map/ppermute | solution.py:467
  9.3 0.0 collective-permute-done.other
  9.3 4.1 %shard_map.64.dense = bf16[2,4,3,256,768]{4,3,2,1,0:T(8,128)(2,1)S(1)} custom-call(s32[4,16]{1,0:T(4,128)} %pad_add_fusion.table, bf16[16,2,3,6,32,128]{5,4,3,2,1,0:T(8,128)(2,1)} %bitcast.28, bf16[16,2,3,6,32,128]{5,4,3,2,1,0:T(8,128)(2,1)} %collective-permute-done.other), custom_call_target="tpu_custom_call" | custom-call | bytes 12000000 | tf_op jit(solution)/shard_map/pallas_call | solution.py:97
  13.4 8.2 %collective-permute-done.1.pairs = bf16[2,2,6,128,128]{4,3,2,1,0:T(8,128)(2,1)S(1)} collective-permute-done((bf16[2,2,6,128,128]{4,3,2,1,0:T(8,128)(2,1)}, bf16[2,2,6,128,128]{4,3,2,1,0:T(8,128)(2,1)S(1)}, u32[]{:S(2)}, u32[]{:S(2)}) %collective-permute-start.1) | collective-permute-done | bytes 786464 | tf_op jit(solution)/shard_map/ppermute | solution.py:465
  21.6 0.1 slice_bitcast_fusion.1
  21.7 0.7 %collective-permute-start.4 = (bf16[2,6,128,128]{3,2,1,0:T(8,128)(2,1)S(1)}, bf16[2,6,128,128]{3,2,1,0:T(8,128)(2,1)S(1)}, u32[]{:S(2)}, u32[]{:S(2)}) collective-permute-start(bf16[2,6,128,128]{3,2,1,0:T(8,128)(2,1)S(1)} %get-tuple-element.30), channel_id=1, source_target_pairs={{4,8},{8,4},{5,9},{9,5},{6,10},{10,6},{7,11},{11,7},{20,24},{24,20... | collective-permute-start | bytes 1179656 | tf_op jit(solution)/shard_map/ppermute | solution.py:471
  22.4 0.0 collective-permute-done.7.inner
  22.4 1.3 %collective-permute-start.8 = (bf16[2,6,128,128]{3,2,1,0:T(8,128)(2,1)S(1)}, bf16[2,6,128,128]{3,2,1,0:T(8,128)(2,1)S(1)}, u32[]{:S(2)}, u32[]{:S(2)}) collective-permute-start(bf16[2,6,128,128]{3,2,1,0:T(8,128)(2,1)S(1)} %collective-permute-done.7.inner), channel_id=1, source_target_pairs={{4,0},{8,12},{5,1},{9,13},{6,2},{10,14},{7,3},{11,15},{20,16},{24,... | collective-permute-start | bytes 1179656 | tf_op jit(solution)/shard_map/ppermute | solution.py:467
  23.7 0.0 copy-done
  23.7 1.7 %shard_map.65.acc = f32[2,2,3,128,128]{4,3,2,1,0:T(8,128)S(1)} custom-call(bf16[2,4,3,256,768]{4,3,2,1,0:T(8,128)(2,1)S(1)} %shard_map.64.dense, bf16[2,2,6,128,128]{4,3,2,1,0:T(8,128)(2,1)S(1)} %bitcast.26, bf16[2,2,6,128,128]{4,3,2,1,0:T(8,128)(2,1)S(1)} %collective-permute-done.1.pairs), custom_call_target="tpu_custom_call" | custom-call | flops 1207959552 | bytes 4000000 | tf_op jit(solution)/shard_map/pallas_call | solution.py:162
  25.5 0.7 %collective-permute-start.9 = (bf16[2,6,128,128]{3,2,1,0:T(8,128)(2,1)S(1)}, bf16[2,6,128,128]{3,2,1,0:T(8,128)(2,1)S(1)}, u32[]{:S(2)}, u32[]{:S(2)}) collective-permute-start(bf16[2,6,128,128]{3,2,1,0:T(8,128)(2,1)S(1)} %get-tuple-element.22), channel_id=1, source_target_pairs={{4,8},{8,4},{5,9},{9,5},{6,10},{10,6},{7,11},{11,7},{20,24},{24,20... | collective-permute-start | bytes 1179656 | tf_op jit(solution)/shard_map/ppermute | solution.py:472
  26.1 3.7 %collective-permute-done.3.outer = bf16[2,6,128,128]{3,2,1,0:T(8,128)(2,1)S(1)} collective-permute-done((bf16[2,6,128,128]{3,2,1,0:T(8,128)(2,1)S(1)}, bf16[2,6,128,128]{3,2,1,0:T(8,128)(2,1)S(1)}, u32[]{:S(2)}, u32[]{:S(2)}) %collective-permute-start.3) | collective-permute-done | bytes 393248 | tf_op jit(solution)/shard_map/ppermute | solution.py:467
  29.9 0.5 shard_map.66.acc
  30.4 0.0 collective-permute-done.4.middle
  30.4 1.3 %collective-permute-start.5 = (bf16[2,6,128,128]{3,2,1,0:T(8,128)(2,1)S(1)}, bf16[2,6,128,128]{3,2,1,0:T(8,128)(2,1)S(1)}, u32[]{:S(2)}, u32[]{:S(2)}) collective-permute-start(bf16[2,6,128,128]{3,2,1,0:T(8,128)(2,1)S(1)} %collective-permute-done.4.middle), channel_id=1, source_target_pairs={{4,0},{8,12},{5,1},{9,13},{6,2},{10,14},{7,3},{11,15},{20,16},{24,... | collective-permute-start | bytes 1179656 | tf_op jit(solution)/shard_map/ppermute | solution.py:475
  31.7 8.2 %collective-permute-done.8.outer = bf16[2,6,128,128]{3,2,1,0:T(8,128)(2,1)S(1)} collective-permute-done((bf16[2,6,128,128]{3,2,1,0:T(8,128)(2,1)S(1)}, bf16[2,6,128,128]{3,2,1,0:T(8,128)(2,1)S(1)}, u32[]{:S(2)}, u32[]{:S(2)}) %collective-permute-start.8) | collective-permute-done | bytes 393248 | tf_op jit(solution)/shard_map/ppermute | solution.py:467
  39.9 0.6 shard_map.68.acc
  40.5 0.0 collective-permute-done.9.middle
  40.5 1.3 %collective-permute-start.10 = (bf16[2,6,64,128]{3,2,1,0:T(8,128)(2,1)S(1)}, bf16[2,6,64,128]{3,2,1,0:T(8,128)(2,1)S(1)}, u32[]{:S(2)}, u32[]{:S(2)}) collective-permute-start(bf16[2,6,64,128]{3,2,1,0:T(8,128)(2,1)S(1)} %get-tuple-element.32), channel_id=1, source_target_pairs={{4,0},{8,12},{5,1},{9,13},{6,2},{10,14},{7,3},{11,15},{20,16},{24,... | collective-permute-start | bytes 589832 | tf_op jit(solution)/shard_map/ppermute | solution.py:479
  41.8 1.3 %collective-permute-start.12 = (bf16[2,6,64,128]{3,2,1,0:T(8,128)(2,1)S(1)}, bf16[2,6,64,128]{3,2,1,0:T(8,128)(2,1)S(1)}, u32[]{:S(2)}, u32[]{:S(2)}) collective-permute-start(bf16[2,6,64,128]{3,2,1,0:T(8,128)(2,1)S(1)} %get-tuple-element.31), channel_id=1, source_target_pairs={{4,0},{8,12},{5,1},{9,13},{6,2},{10,14},{7,3},{11,15},{20,16},{24,... | collective-permute-start | bytes 589832 | tf_op jit(solution)/shard_map/ppermute | solution.py:479
  43.1 5.0 %collective-permute-done.5.far = bf16[2,6,128,128]{3,2,1,0:T(8,128)(2,1)S(1)} collective-permute-done((bf16[2,6,128,128]{3,2,1,0:T(8,128)(2,1)S(1)}, bf16[2,6,128,128]{3,2,1,0:T(8,128)(2,1)S(1)}, u32[]{:S(2)}, u32[]{:S(2)}) %collective-permute-start.5) | collective-permute-done | bytes 393248 | tf_op jit(solution)/shard_map/ppermute | solution.py:475
  48.1 0.5 shard_map.67
  48.6 1.6 %collective-permute-start.6 = (f32[2,3,64,128]{3,2,1,0:T(8,128)S(1)}, f32[2,3,64,128]{3,2,1,0:T(8,128)S(1)}, u32[]{:S(2)}, u32[]{:S(2)}) collective-permute-start(f32[2,3,64,128]{3,2,1,0:T(8,128)S(1)} %get-tuple-element.20), channel_id=1, source_target_pairs={{0,2},{2,0},{1,3},{3,1},{4,6},{6,4},{5,7},{7,5},{8,10},{10,8},{9,1... | collective-permute-start | bytes 589832 | tf_op jit(solution)/shard_map/ppermute | solution.py:485
  50.9 2.7 %collective-permute-done.10.far = bf16[2,6,64,128]{3,2,1,0:T(8,128)(2,1)S(1)} collective-permute-done((bf16[2,6,64,128]{3,2,1,0:T(8,128)(2,1)S(1)}, bf16[2,6,64,128]{3,2,1,0:T(8,128)(2,1)S(1)}, u32[]{:S(2)}, u32[]{:S(2)}) %collective-permute-start.10) | collective-permute-done | bytes 196640 | tf_op jit(solution)/shard_map/ppermute | solution.py:479
  53.6 0.4 shard_map.69
  54.0 0.3 collective-permute-start.11
  54.3 1.6 %collective-permute-done.12.far = bf16[2,6,64,128]{3,2,1,0:T(8,128)(2,1)S(1)} collective-permute-done((bf16[2,6,64,128]{3,2,1,0:T(8,128)(2,1)S(1)}, bf16[2,6,64,128]{3,2,1,0:T(8,128)(2,1)S(1)}, u32[]{:S(2)}, u32[]{:S(2)}) %collective-permute-start.12) | collective-permute-done | bytes 196640 | tf_op jit(solution)/shard_map/ppermute | solution.py:479
  56.0 0.0 collective-permute-done.6.got
  56.0 0.4 shard_map.72
  56.4 1.1 %collective-permute-start.13 = (f32[3,64,128]{2,1,0:T(8,128)S(1)}, f32[3,64,128]{2,1,0:T(8,128)S(1)}, u32[]{:S(2)}, u32[]{:S(2)}) collective-permute-start(f32[3,64,128]{2,1,0:T(8,128)S(1)} %shard_map.72), channel_id=1, source_target_pairs={{0,2},{2,0},{1,3},{3,1},{4,6},{6,4},{5,7},{7,5},{8,10},{10,8},{9,1... | collective-permute-start | bytes 294920 | tf_op jit(solution)/shard_map/ppermute | solution.py:485
  57.4 0.4 shard_map.70.keep_a
  57.8 1.5 %collective-permute-done.11.got_a = f32[3,64,128]{2,1,0:T(8,128)S(1)} collective-permute-done((f32[3,64,128]{2,1,0:T(8,128)S(1)}, f32[3,64,128]{2,1,0:T(8,128)S(1)}, u32[]{:S(2)}, u32[]{:S(2)}) %collective-permute-start.11) | collective-permute-done | bytes 98336 | tf_op jit(solution)/shard_map/ppermute | solution.py:485
  59.3 0.1 broadcast_in_dim.2.brune
  59.4 0.7 %shard_map.71 = (f32[2,2,3,64,128]{4,3,2,1,0:T(8,128)}, f32[2,3,64,128]{3,2,1,0:T(8,128)S(1)}) custom-call(f32[2,8,128]{2,1,0:T(8,128)S(1)} %broadcast_in_dim.2.brune, f32[2,3,64,128]{3,2,1,0:T(8,128)S(1)} %get-tuple-element.19.keep, f32[2,3,64,128]{3,2,1,0:T(8,128)S(1)} %collective-permute-done.6.got, f32[3,64,128]{2,1,0:T(8,128)S(1)} %shard_map.70.keep_a, ...), custom_call_target="tpu_custom_call" | custom-call | flops 400000 | bytes 8000000 | tf_op jit(solution)/shard_map/pallas_call | solution.py:400
  60.1 0.4 shard_map.73.keep_b
  60.6 0.5 collective-permute-done.13.got_b
  61.0 0.8 %shard_map.74 = f32[2,2,3,64,128]{4,3,2,1,0:T(8,128)} custom-call(f32[2,8,128]{2,1,0:T(8,128)S(1)} %broadcast_in_dim.2.brune, f32[2,3,64,128]{3,2,1,0:T(8,128)S(1)} %get-tuple-element.25.part, f32[3,64,128]{2,1,0:T(8,128)S(1)} %shard_map.73.keep_b, f32[3,64,128]{2,1,0:T(8,128)S(1)} %collective-permute-done.13.got_b, ...), custom_call_target="tpu_custom_call", output_to_operand_aliasing={{}: (4, {})} | custom-call | flops 400000 | bytes 600000 | tf_op jit(solution)/shard_map/pallas_call | solution.py:437
  (3 shorter events, 0.0 us)
Async XLA Ops:
  0.0 9.3 %collective-permute-start = (bf16[16,2,3,6,32,128]{5,4,3,2,1,0:T(8,128)(2,1)}, bf16[16,2,3,6,32,128]{5,4,3,2,1,0:T(8,128)(2,1)}, u32[]{:S(2)}, u32[]{:S(2)}) collective-permute-start(bf16[16,2,3,6,32,128]{5,4,3,2,1,0:T(8,128)(2,1)} %bitcast.27), channel_id=1, source_target_pairs={{0,1},{1,0},{2,3},{3,2},{4,5},{5,4},{6,7},{7,6},{8,9},{9,8},{10,11... | collective-permute-start | bytes 14155784 | tf_op jit(solution)/shard_map/ppermute | solution.py:500
  0.5 21.2 %collective-permute-start.1 = (bf16[2,2,6,128,128]{4,3,2,1,0:T(8,128)(2,1)}, bf16[2,2,6,128,128]{4,3,2,1,0:T(8,128)(2,1)S(1)}, u32[]{:S(2)}, u32[]{:S(2)}) collective-permute-start(bf16[2,2,6,128,128]{4,3,2,1,0:T(8,128)(2,1)} %bitcast.23), channel_id=1, source_target_pairs={{0,4},{4,0},{8,12},{12,8},{1,5},{5,1},{9,13},{13,9},{2,6},{6,2},{1... | collective-permute-start | bytes 2359304 | tf_op jit(solution)/shard_map/ppermute | solution.py:465
  4.1 3.9 %collective-permute-start.2 = (bf16[2,6,128,128]{3,2,1,0:T(8,128)(2,1)S(1)}, bf16[2,6,128,128]{3,2,1,0:T(8,128)(2,1)S(1)}, u32[]{:S(2)}, u32[]{:S(2)}) collective-permute-start(bf16[2,6,128,128]{3,2,1,0:T(8,128)(2,1)S(1)} %slice_bitcast_fusion), channel_id=1, source_target_pairs={{4,8},{8,4},{5,9},{9,5},{6,10},{10,6},{7,11},{11,7},{20,24},{24,20... | collective-permute-start | bytes 1179656 | tf_op jit(solution)/shard_map/ppermute | solution.py:466
  7.2 16.5 %copy-start = (bf16[2,2,128,6,128]{4,2,3,1,0:T(8,128)(2,1)S(1)}, bf16[2,2,128,6,128]{4,2,3,1,0:T(8,128)(2,1)}, u32[]{:S(2)}) copy-start(bf16[2,2,128,6,128]{4,2,3,1,0:T(8,128)(2,1)} %param.7) | copy-start | bytes 2359300
  7.2 15.2 %collective-permute-start.7 = (bf16[2,6,128,128]{3,2,1,0:T(8,128)(2,1)S(1)}, bf16[2,6,128,128]{3,2,1,0:T(8,128)(2,1)S(1)}, u32[]{:S(2)}, u32[]{:S(2)}) collective-permute-start(bf16[2,6,128,128]{3,2,1,0:T(8,128)(2,1)S(1)} %slice_bitcast_fusion.2), channel_id=1, source_target_pairs={{4,8},{8,4},{5,9},{9,5},{6,10},{10,6},{7,11},{11,7},{20,24},{24,20... | collective-permute-start | bytes 1179656 | tf_op jit(solution)/shard_map/ppermute | solution.py:466
  8.0 21.9 %collective-permute-start.3 = (bf16[2,6,128,128]{3,2,1,0:T(8,128)(2,1)S(1)}, bf16[2,6,128,128]{3,2,1,0:T(8,128)(2,1)S(1)}, u32[]{:S(2)}, u32[]{:S(2)}) collective-permute-start(bf16[2,6,128,128]{3,2,1,0:T(8,128)(2,1)S(1)} %collective-permute-done.2.inner), channel_id=1, source_target_pairs={{4,0},{8,12},{5,1},{9,13},{6,2},{10,14},{7,3},{11,15},{20,16},{24,... | collective-permute-start | bytes 1179656 | tf_op jit(solution)/shard_map/ppermute | solution.py:467
  21.7 8.7 %collective-permute-start.4 = (bf16[2,6,128,128]{3,2,1,0:T(8,128)(2,1)S(1)}, bf16[2,6,128,128]{3,2,1,0:T(8,128)(2,1)S(1)}, u32[]{:S(2)}, u32[]{:S(2)}) collective-permute-start(bf16[2,6,128,128]{3,2,1,0:T(8,128)(2,1)S(1)} %get-tuple-element.30), channel_id=1, source_target_pairs={{4,8},{8,4},{5,9},{9,5},{6,10},{10,6},{7,11},{11,7},{20,24},{24,20... | collective-permute-start | bytes 1179656 | tf_op jit(solution)/shard_map/ppermute | solution.py:471
  22.4 17.5 %collective-permute-start.8 = (bf16[2,6,128,128]{3,2,1,0:T(8,128)(2,1)S(1)}, bf16[2,6,128,128]{3,2,1,0:T(8,128)(2,1)S(1)}, u32[]{:S(2)}, u32[]{:S(2)}) collective-permute-start(bf16[2,6,128,128]{3,2,1,0:T(8,128)(2,1)S(1)} %collective-permute-done.7.inner), channel_id=1, source_target_pairs={{4,0},{8,12},{5,1},{9,13},{6,2},{10,14},{7,3},{11,15},{20,16},{24,... | collective-permute-start | bytes 1179656 | tf_op jit(solution)/shard_map/ppermute | solution.py:467
  25.5 15.0 %collective-permute-start.9 = (bf16[2,6,128,128]{3,2,1,0:T(8,128)(2,1)S(1)}, bf16[2,6,128,128]{3,2,1,0:T(8,128)(2,1)S(1)}, u32[]{:S(2)}, u32[]{:S(2)}) collective-permute-start(bf16[2,6,128,128]{3,2,1,0:T(8,128)(2,1)S(1)} %get-tuple-element.22), channel_id=1, source_target_pairs={{4,8},{8,4},{5,9},{9,5},{6,10},{10,6},{7,11},{11,7},{20,24},{24,20... | collective-permute-start | bytes 1179656 | tf_op jit(solution)/shard_map/ppermute | solution.py:472
  30.4 17.7 %collective-permute-start.5 = (bf16[2,6,128,128]{3,2,1,0:T(8,128)(2,1)S(1)}, bf16[2,6,128,128]{3,2,1,0:T(8,128)(2,1)S(1)}, u32[]{:S(2)}, u32[]{:S(2)}) collective-permute-start(bf16[2,6,128,128]{3,2,1,0:T(8,128)(2,1)S(1)} %collective-permute-done.4.middle), channel_id=1, source_target_pairs={{4,0},{8,12},{5,1},{9,13},{6,2},{10,14},{7,3},{11,15},{20,16},{24,... | collective-permute-start | bytes 1179656 | tf_op jit(solution)/shard_map/ppermute | solution.py:475
  40.5 13.1 %collective-permute-start.10 = (bf16[2,6,64,128]{3,2,1,0:T(8,128)(2,1)S(1)}, bf16[2,6,64,128]{3,2,1,0:T(8,128)(2,1)S(1)}, u32[]{:S(2)}, u32[]{:S(2)}) collective-permute-start(bf16[2,6,64,128]{3,2,1,0:T(8,128)(2,1)S(1)} %get-tuple-element.32), channel_id=1, source_target_pairs={{4,0},{8,12},{5,1},{9,13},{6,2},{10,14},{7,3},{11,15},{20,16},{24,... | collective-permute-start | bytes 589832 | tf_op jit(solution)/shard_map/ppermute | solution.py:479
  41.8 14.2 %collective-permute-start.12 = (bf16[2,6,64,128]{3,2,1,0:T(8,128)(2,1)S(1)}, bf16[2,6,64,128]{3,2,1,0:T(8,128)(2,1)S(1)}, u32[]{:S(2)}, u32[]{:S(2)}) collective-permute-start(bf16[2,6,64,128]{3,2,1,0:T(8,128)(2,1)S(1)} %get-tuple-element.31), channel_id=1, source_target_pairs={{4,0},{8,12},{5,1},{9,13},{6,2},{10,14},{7,3},{11,15},{20,16},{24,... | collective-permute-start | bytes 589832 | tf_op jit(solution)/shard_map/ppermute | solution.py:479
  48.6 7.3 %collective-permute-start.6 = (f32[2,3,64,128]{3,2,1,0:T(8,128)S(1)}, f32[2,3,64,128]{3,2,1,0:T(8,128)S(1)}, u32[]{:S(2)}, u32[]{:S(2)}) collective-permute-start(f32[2,3,64,128]{3,2,1,0:T(8,128)S(1)} %get-tuple-element.20), channel_id=1, source_target_pairs={{0,2},{2,0},{1,3},{3,1},{4,6},{6,4},{5,7},{7,5},{8,10},{10,8},{9,1... | collective-permute-start | bytes 589832 | tf_op jit(solution)/shard_map/ppermute | solution.py:485
  54.0 5.3 %collective-permute-start.11 = (f32[3,64,128]{2,1,0:T(8,128)S(1)}, f32[3,64,128]{2,1,0:T(8,128)S(1)}, u32[]{:S(2)}, u32[]{:S(2)}) collective-permute-start(f32[3,64,128]{2,1,0:T(8,128)S(1)} %shard_map.69), channel_id=1, source_target_pairs={{0,2},{2,0},{1,3},{3,1},{4,6},{6,4},{5,7},{7,5},{8,10},{10,8},{9,1... | collective-permute-start | bytes 294920 | tf_op jit(solution)/shard_map/ppermute | solution.py:485
  56.4 4.7 %collective-permute-start.13 = (f32[3,64,128]{2,1,0:T(8,128)S(1)}, f32[3,64,128]{2,1,0:T(8,128)S(1)}, u32[]{:S(2)}, u32[]{:S(2)}) collective-permute-start(f32[3,64,128]{2,1,0:T(8,128)S(1)} %shard_map.72), channel_id=1, source_target_pairs={{0,2},{2,0},{1,3},{3,1},{4,6},{6,4},{5,7},{7,5},{8,10},{10,8},{9,1... | collective-permute-start | bytes 294920 | tf_op jit(solution)/shard_map/ppermute | solution.py:485
